TPU v7x, 32 devices: a whole 2x2x4 slice. The times are simulated.
32 devices in a mesh: section: 2 (over x), dp: 8 (over z, y), tensor: 2 (over core).
Axes of the slice: x: 2, y: 2, z: 4, core: 2. Of those that a mesh axis runs over, the one named last changes fastest.
Arguments:
- tokens: bfloat16 [2, 4096, 384], P(None, 'dp'), may hold values from -6 to 6
- image_counts: int32 [2], replicated, may hold values from 15 to 20, as said below
- cotangent: bfloat16 [2, 4096, 384], P(None, 'dp'), may hold values from -6 to 6
- norm_gains: bfloat16 [2, 2, 384], P('section', None, 'dp'), may hold values from 0.5 to 1.5
- row_biases: bfloat16 [2, 4, 384], P('section', None, 'dp'), may hold values from -3 to 3
- qkv_weight: bfloat16 [2, 384, 3, 384], P('section', 'dp', None, 'tensor'), may hold values from -0.3125 to 0.3125
- qv_bias: bfloat16 [2, 2, 384], P('section', None, 'tensor'), may hold values from -3 to 3
- out_weight: bfloat16 [2, 384, 384], P('section', 'tensor', 'dp'), may hold values from -1.25 to 1.25
- up_weight: bfloat16 [2, 384, 1536], P('section', 'dp', 'tensor'), may hold values from -0.3125 to 0.3125
- up_bias: bfloat16 [2, 1536], P('section', 'tensor'), may hold values from -3 to 3
- down_weight: bfloat16 [2, 1536, 384], P('section', 'tensor', 'dp'), may hold values from -0.21875 to 0.21875
Outputs:
- layer_outputs: bfloat16 [2, 2, 4096, 384], P('section', None, 'dp')
- input_grads: float32 [2, 2, 4096, 384], P('section', None, 'dp')
- grad_norm_gains: float32 [2, 2, 384], P('section', None, 'dp')
- grad_row_biases: float32 [2, 4, 384], P('section', None, 'dp')
- grad_qkv: float32 [2, 384, 3, 384], P('section', 'dp', None, 'tensor')
- grad_qv_bias: float32 [2, 2, 384], P('section', None, 'tensor')
- grad_out: float32 [2, 384, 384], P('section', 'tensor', 'dp')
- grad_up: float32 [2, 384, 1536], P('section', 'dp', 'tensor')
- grad_up_bias: float32 [2, 1536], P('section', 'tensor')
- grad_down: float32 [2, 1536, 384], P('section', 'tensor', 'dp')
Inputs may be any that keep to these rules, and one draw needn't show every extreme that they name: `image_counts`: number of images in each micro-batch; image i fills rows i * 197 to (i + 1) * 197 - 1 of its micro-batch, later rows are padding; some micro-batch holds 20 images.
All inputs are finite; a program needn't handle non-finite values.
Results may differ from a plain program's by a relative error of at most 0.019.
Values may be sent and summed in bfloat16 or wider, within the bound.
No kernel may reach another device: no remote copies, remote signals or barrier semaphores. Data moves between devices by JAX's collectives and lax.ppermute only.
A program may use at most 128 MiB of HBM per device.

v0:
```python
import functools
import math

import jax
import jax.numpy as jnp
from jax import lax
from jax.experimental import pallas as pl
from jax.experimental.pallas import tpu as pltpu
from jax.sharding import PartitionSpec as P

IMG_LEN = 197
IMG_PAD = 208
HD = 64
EPSILON = 1e-06
NEGATIVE = -1e30
F32 = jnp.float32
BF16 = jnp.bfloat16
BLOCK = 128
HALF = 1280
COST = 10 ** 10
SCALE = 1.0 / math.sqrt(HD)


def mm(a, b, dims):
    return lax.dot_general(a, b, (dims, ((), ())), preferred_element_type=F32)


def nn(a, b):
    return mm(a, b, ((1,), (0,)))


def nt(a, b):
    return mm(a, b, ((1,), (1,)))


def tn(a, b):
    return mm(a, b, ((0,), (0,)))


def normed(x):
    centred = x - jnp.mean(x, -1, keepdims=True)
    inverse = lax.rsqrt(jnp.mean(centred * centred, -1, keepdims=True) + EPSILON)
    return centred * inverse, inverse


def norm_back(grad, xhat, inverse, gain):
    t = grad * gain
    return inverse * (
        t - jnp.mean(t, -1, keepdims=True) - xhat * jnp.mean(t * xhat, -1, keepdims=True)
    )


def gelu_parts(u):
    cdf = 0.5 * (1.0 + lax.erf(u * math.sqrt(0.5)))
    pdf = jnp.exp(-0.5 * u * u) * (1.0 / math.sqrt(2.0 * math.pi))
    return u * cdf, cdf + u * pdf


QK = 384
V = 256
OUT = 128
MISC = 384
MLP = 512
ATT = QK + V


def low_lanes():
    return lax.broadcasted_iota(jnp.int32, (1, BLOCK), 1) < HD


def turn(a):
    return jnp.concatenate([a[:, HD:], a[:, :HD]], 1)


def valid_rows(sc, n):
    row = lax.broadcasted_iota(jnp.int32, (IMG_PAD, 1), 0)
    return jnp.where((row < IMG_LEN) & (n < sc[0]), 1.0, 0.0)


def image_rows(n):
    return pl.ds(pl.multiple_of(n * IMG_PAD, 16), IMG_PAD)


def forward_image(n, sc, x_ref, w, vec, brow, out_ref, kept, ready):
    r = image_rows(n)
    x = x_ref[r, :].astype(F32)
    xhat, inv = normed(x)
    attn_in = (xhat * vec[0:1, :] + vec[2:3, :]).astype(BF16)
    kept["xh1"][r, :] = xhat
    kept["inv1"][r, :] = jnp.broadcast_to(inv, (IMG_PAD, BLOCK))
    kept["ain"][r, :] = attn_in
    residual = x + vec[3:4, :]
    low = low_lanes()
    lane = lax.broadcasted_iota(jnp.int32, (1, ATT), 1)
    factor = jnp.where(lane < 192, SCALE, jnp.where(lane < 576, 1.0, 0.0))
    real = lax.broadcasted_iota(jnp.int32, (1, IMG_PAD), 1) < IMG_LEN
    for t in range(2):
        bias = jnp.concatenate([brow[t, i:i + 1, :] for i in range(5)], 1)
        p = jnp.concatenate([nn(attn_in, w[t, 0, :, :QK]), nn(attn_in, w[t, 1, :, :V])], 1)
        p = ((p + bias) * factor).astype(BF16)
        kept["qkv"][t, r, :] = p
        q, qk, k, v, vx = [p[:, i * BLOCK:(i + 1) * BLOCK] for i in range(5)]
        kq, xv = turn(qk), turn(vx)
        outs = []
        for i, (qq, kk, vv) in enumerate(
                [(jnp.where(low, q, 0), k, v), (jnp.where(low, 0, q), k, v), (jnp.where(low, qk, 0), kq, xv)]):
            s = jnp.where(real, nt(qq, kk), NEGATIVE)
            e = jnp.exp(s - jnp.max(s, -1, keepdims=True))
            pr = (e * (1.0 / jnp.sum(e, -1, keepdims=True))).astype(BF16)
            kept["pr"][n * 6 + t * 3 + i] = pr
            outs.append(nn(pr, vv))
        mixed = jnp.concatenate([outs[2], jnp.where(low, outs[0], outs[1])], 1).astype(BF16)
        kept["mx"][t, r, :] = mixed
        residual = residual + nt(mixed, w[t, 1, :, OUT:MISC])
    xhat, inv = normed(residual)
    mlp_in = (xhat * vec[1:2, :] + vec[4:5, :]).astype(BF16)
    kept["xh2"][r, :] = xhat
    kept["inv2"][r, :] = jnp.broadcast_to(inv, (IMG_PAD, BLOCK))
    kept["min"][r, :] = mlp_in
    out = residual + vec[5:6, :]
    ready(1)
    ff = kept["hd"].shape[1] // 2
    for t in range(2):
        bias = jnp.concatenate([brow[t, 5 + i:6 + i, :] for i in range(ff // BLOCK)], 1)
        hidden, slope = gelu_parts(nn(mlp_in, w[t, 0, :, MLP:]) + bias)
        hidden = hidden.astype(BF16)
        kept["hd"][r, t * ff:(t + 1) * ff] = hidden
        kept["sl"][r, t * ff:(t + 1) * ff] = slope.astype(BF16)
        out = out + nt(hidden, w[t, 1, :, MLP:])
    out_ref[r, :] = (out * valid_rows(sc, n)).astype(BF16)


def rsum(a):
    return jnp.sum(a, 0, keepdims=True)


def backward_mlp(n, sc, u_ref, w, vec, kept, grad, sums, bsum):
    r = image_rows(n)

    masked = u_ref[r, :].astype(F32) * valid_rows(sc, n)
    sums[5:6, :] += rsum(masked)
    dg = masked.astype(BF16)
    grad["dg"][r, :] = dg
    mg = jnp.zeros(masked.shape, F32)
    ff = kept["hd"].shape[1] // 2
    for t in range(2):
        c = slice(t * ff, (t + 1) * ff)
        up = (nn(dg, w[t, 1, :, MLP:]) * kept["sl"][r, c].astype(F32)).astype(BF16)
        grad["up"][r, c] = up
        total = rsum(up.astype(F32))
        for i in range(ff // BLOCK):
            bsum[t, 5 + i:6 + i, :] += total[:, i * BLOCK:(i + 1) * BLOCK]
        mg = mg + nt(up, w[t, 0, :, MLP:])
    xhat = kept["xh2"][r, :]
    sums[4:5, :] += rsum(mg)
    sums[1:2, :] += rsum(mg * xhat)
    res = masked + norm_back(mg, xhat, kept["inv2"][r, :1], vec[1:2, :])
    sums[3:4, :] += rsum(res)
    grad["res"][r, :] = res


def backward_attention(n, w, vec, in_ref, kept, grad, sums, bsum):
    r = image_rows(n)
    res = grad["res"][r, :]
    ag = res.astype(BF16)
    grad["ag"][r, :] = ag
    low = low_lanes()
    ig = jnp.zeros(res.shape, F32)
    for t in range(2):
        xg = nn(ag, w[t, 1, :, OUT:MISC]).astype(BF16)
        gx = jnp.where(low, 0, xg[:, :BLOCK])
        g = xg[:, BLOCK:]
        p = kept["qkv"][t, r, :]
        q, qk, k, v, vx = [p[:, i * BLOCK:(i + 1) * BLOCK] for i in range(5)]
        kq, xv = turn(qk), turn(vx)
        dq, dk, dv = [], [], []
        for i, (qq, kk, vv, gm, gg) in enumerate(
                [(q, k, v, jnp.where(low, g, 0), g), (q, k, v, jnp.where(low, 0, g), g), (qk, kq, xv, gx, turn(gx))]):
            pb = kept["pr"][n * 6 + t * 3 + i]
            pf = pb.astype(F32)
            dp = nt(gm, vv)
            ds = (pf * (dp - jnp.sum(pf * dp, -1, keepdims=True))).astype(BF16)
            dv.append(tn(pb, gg))
            dq.append(nn(ds, kk) * SCALE)
            dk.append(tn(ds, kq if i == 2 else qq))
        blocks = [
            jnp.where(low, dq[0], dq[1]), jnp.where(low, dq[2], dk[2]), jnp.where(low, dk[0], dk[1]),
            jnp.where(low, dv[0], dv[1]), dv[2],
        ]
        d = jnp.concatenate(blocks, 1).astype(BF16)
        grad["dqkv"][t, r, :] = d
        total = rsum(d.astype(F32))
        for i in range(5):
            bsum[t, i:i + 1, :] += total[:, i * BLOCK:(i + 1) * BLOCK]
        ig = ig + nt(d[:, :QK], w[t, 0, :, :QK]) + nt(d[:, QK:], w[t, 1, :, :V])
    xhat = kept["xh1"][r, :]
    sums[2:3, :] += rsum(ig)
    sums[0:1, :] += rsum(ig * xhat)
    in_ref[r, :] = res + norm_back(ig, xhat, kept["inv1"][r, :1], vec[0:1, :])


def weight_grads(t, piece, kept, grad, g):
    ag, dg = grad["ag"][...], grad["dg"][...]
    ain, mlp_in = kept["ain"][...], kept["min"][...]
    width = ag.shape[1]
    high = jnp.where(low_lanes(), 0.0, 1.0)
    d = grad["dqkv"][t]
    g[0, :, :QK] = tn(ain, d[:, :QK]).astype(BF16)
    val = tn(ain, d[:, QK:])
    out = tn(ag, kept["mx"][t])
    g[1, :, :OUT] = val[:, :BLOCK].astype(BF16)
    g[1, :, OUT:V] = (val[:, BLOCK:] + out[:, :BLOCK] * high).astype(BF16)
    g[1, :, V:MISC] = out[:, BLOCK:].astype(BF16)
    sums = jnp.concatenate([grad["sums"][...], jnp.zeros((BLOCK - 8, width), F32)], 0)
    g[0, :, MISC:MLP] = sums.T.astype(BF16)
    ff = kept["hd"].shape[1] // 2
    c = pl.ds(pl.multiple_of(t * ff, BLOCK), ff)
    g[0, :, MLP:] = tn(mlp_in, grad["up"][:, c]).astype(BF16)
    g[1, :, MLP:] = tn(dg, kept["hd"][:, c]).astype(BF16)
    if piece % 16 == 0:
        rows = jnp.concatenate([grad["bsum"][t], jnp.zeros((piece - 16, BLOCK), F32)], 0).astype(BF16)
        for i in range(width // piece):
            g[1, i * piece:(i + 1) * piece, MISC:MLP] = rows


def kept_shapes(total, width, ff):
    images = total // IMG_PAD
    return dict(
        xh1=((total, width), F32), inv1=((total, BLOCK), F32), ain=((total, width), BF16), qkv=((2, total, ATT), BF16),
        pr=((images * 6, IMG_PAD, IMG_PAD), BF16), mx=((2, total, 2 * BLOCK), BF16), xh2=((total, width), F32),
        inv2=((total, BLOCK), F32), min=((total, width), BF16), sl=((total, ff), BF16), hd=((total, ff), BF16))


def grad_shapes(total, width, ff):
    return dict(dg=((total, width), BF16), up=((total, ff), BF16), res=((total, width), F32), sums=((8, width), F32),
                bsum=((2, 16, BLOCK), F32), ag=((total, width), BF16), dqkv=((2, total, ATT), BF16))


def layer_call(phases, sources, load, store, out_shapes, scalars, given, total, width, ff, piece):
    ks = kept_shapes(total, width, ff)
    gs = grad_shapes(total, width, ff)
    weights = ["ain", "mx", "min", "hd"] + [n for n in gs if n != "res"]
    need = {"forward": ["x"], "back": ["u"] + list(ks), "theirs": weights, "mine": weights}
    gives = {"forward": {"out": ((total, width), BF16), **ks}, "back": {"keep": ((total, width), BF16), "give": ((total, width), BF16), "in": ((total, width), F32), **gs},
             "theirs": {}, "mine": {}}
    made = {}
    for p in phases:
        made.update(gives[p])
    inputs = list(dict.fromkeys(n for p in phases for n in need[p] if n not in made))
    if phases[-1] == "forward":
        shown = list(made)
    else:
        shown = [n for n in made if n in weights or n in ("keep", "give")]
        if "forward" in phases:
            shown.append("in")
    inner = [n for n in made if n not in shown]
    side = {"theirs": 0, "mine": 1}.get(phases[-1])
    products = phases[0] != "mine"
    vmem = pl.BlockSpec(memory_space=pltpu.VMEM)
    anywhere = pl.BlockSpec(memory_space=pl.ANY)
    ends = [] if side is None else out_shapes[side]
    scratch = [pltpu.SemaphoreType.DMA((2,))] + [pltpu.VMEM(*made[n]) for n in inner]
    if products:
        scratch += [pltpu.VMEM((2, 2, width, HALF), BF16), pltpu.VMEM((8, width), F32), pltpu.VMEM((2, 16, BLOCK), F32)]
    if ends:
        scratch.append(pltpu.VMEM((2, width, HALF), BF16))

    def body(*refs):
        refs = list(refs)

        def take(n):
            got = refs[:n]
            del refs[:n]
            return got

        sc = take(1)[0]
        at = dict(zip(inputs, take(len(inputs))))
        src = take(len(sources))
        at.update(zip(shown, take(len(shown))))
        dst = take(len(ends))
        sem = take(1)[0]
        at.update(zip(inner, take(len(inner))))
        if products:
            w, vec, brow = take(3)
            pending = [load(sc, src, w, sem, c) for c in range(2)]
            for part in pending if "forward" in phases else pending[::-1]:
                for c in part:
                    c.start()

            def ready(c):
                for copy in pending[c]:
                    copy.wait()
                if c == 0 and pending[c]:
                    vec[...] = w[0, 0, :, MISC:MLP].astype(F32).T[:8, :]
                    for t in range(2):
                        brow[t] = w[t, 1, :16, MISC:MLP].astype(F32)
                pending[c] = []

            ready(0 if "forward" in phases else 1)
        if "forward" in phases:
            if "back" in phases:
                ready(1)

                def step(n, carry):
                    forward_image(n, sc, at["x"], w, vec, brow, at["out"], at, ready)
                    return carry
                lax.fori_loop(0, total // IMG_PAD, step, 0)
            else:
                for n in range(total // IMG_PAD):
                    forward_image(n, sc, at["x"], w, vec, brow, at["out"], at, ready)
        if "back" in phases:
            sums, bsum = at["sums"], at["bsum"]
            sums[...] = jnp.zeros_like(sums)
            bsum[...] = jnp.zeros_like(bsum)
            ready(0)

            def back(n, carry):
                backward_mlp(n, sc, at["u"], w, vec, at, at, sums, bsum)
                backward_attention(n, w, vec, at["in"], at, at, sums, bsum)
                return carry
            lax.fori_loop(0, total // IMG_PAD, back, 0)
            rows = [at[n] for n in (("x", "out") if "forward" in phases else ("in", "u"))]
            for here in range(2):
                @pl.when(sc[2] == here)
                def _():
                    at["keep"][...] = rows[here][...].astype(BF16)
                    at["give"][...] = rows[1 - here][...].astype(BF16)
        if ends:
            g = take(1)[0]
            t = jnp.where(sc[1] == 0, 1 - side, side)
            weight_grads(t, piece, at, at, g)
            copies = store(sc, side, g, dst, sem.at[0])
            for c in copies:
                c.start()
            for c in copies:
                c.wait()

    outs = [made[n] for n in shown] + ends
    args = [scalars, *[given[n] for n in inputs], *(sources if products else [])]
    if not products:
        sources = []
    got = pl.pallas_call(
        body,
        out_shape=[jax.ShapeDtypeStruct(*o) for o in outs],
        in_specs=[pl.BlockSpec(memory_space=pltpu.SMEM)] + [vmem] * len(inputs) + [anywhere] * len(sources),
        out_specs=[vmem] * (len(outs) - len(ends)) + [anywhere] * len(ends),
        scratch_shapes=scratch,
        compiler_params=pltpu.CompilerParams(vmem_limit_bytes=34 * 2 ** 20),
        cost_estimate=pl.CostEstimate(flops=COST * len(phases), transcendentals=0, bytes_accessed=2 ** 23),
    )(*args)
    got = list(got)
    res = dict(zip(shown, got))
    res["g"] = got[len(shown):]
    return res


def parts(a, b, ff):
    small = a[:, MISC:MLP].T
    rows = b[:16, MISC:MLP]

    def heads(c, pair, single):
        return jnp.concatenate([c[:, pair:pair + BLOCK], c[:, single:single + HD]], 1)

    def lanes(first, last):
        return jnp.concatenate([rows[i:i + 1, :] for i in range(first, last)], 1)

    size = 3 * HD
    qkv = jnp.stack([heads(a, 0, BLOCK), heads(a, 2 * BLOCK, BLOCK + HD), heads(b, 0, BLOCK)])
    biases = jnp.concatenate([lanes(0, 2)[:, :size], lanes(3, 5)[:, :size]], 0)
    out = heads(b, 2 * BLOCK, BLOCK + HD)
    return small[:2], small[2:6], qkv, biases, out, a[:, MLP:], lanes(5, 5 + ff // BLOCK), b[:, MLP:]


def finish(scalars, mine, other, ff):
    piece = mine.shape[0]

    def body(sc, mine_ref, other_ref, *outs):
        first = sc[2] == 0
        a, b = mine_ref[...], other_ref[...].astype(F32)
        for ref, got in zip(outs, parts(jnp.where(first, a, b), jnp.where(first, b, a), ff)):
            ref[...] = got

    vmem = pl.BlockSpec(memory_space=pltpu.VMEM)
    shapes = [(2, piece), (4, piece), (3, piece, 3 * HD), (2, 3 * HD), (piece, 3 * HD), (piece, ff), (1, ff), (piece, ff)]
    return pl.pallas_call(
        body,
        out_shape=[jax.ShapeDtypeStruct(s, F32) for s in shapes],
        in_specs=[pl.BlockSpec(memory_space=pltpu.SMEM), vmem, vmem],
        out_specs=[vmem] * len(shapes),
    )(scalars, mine, other)


def shards(tokens, image_counts, cotangent, norm_gains, row_biases, qkv_weight, qv_bias, out_weight,
           up_weight, up_bias, down_weight):
    sec = lax.axis_index("section")
    dp = lax.axis_index("dp")
    ten = lax.axis_index("tensor")
    n_dp = lax.axis_size("dp")
    m = n_dp // 2
    zi, yi = dp // 2, dp % 2
    local_rows, width = tokens.shape[1:]
    images = local_rows * n_dp // IMG_LEN
    piece = width // n_dp
    ff = 2 * up_weight.shape[2]
    direct = piece % 16 == 0 and m == 4

    def pt(a):
        return lax.ppermute(a, "tensor", [(0, 1), (1, 0)])

    def px(a):
        return lax.ppermute(a, "section", [(0, 1), (1, 0)])

    def py(a):
        return lax.ppermute(a, "dp", [(i, i ^ 1) for i in range(n_dp)])

    def pd(a):
        return lax.ppermute(a, ("section", "dp"), [(i, (i + n_dp) % (2 * n_dp) ^ 1) for i in range(2 * n_dp)])

    def after(a, *b):
        return lax.optimization_barrier((a, *b))

    def plus(*a):
        return sum(b.astype(F32) for b in a)

    def chip_sums(g, got):
        keep0, give0, keep1, give1 = [plus(a, got[i // 2, i % 2]) for i, a in enumerate(g)]
        return [keep0, give0.astype(BF16), keep1, give1.astype(BF16)]

    def cross_first(s):
        return [s[0], px(s[1]), s[2], py(s[3])]

    def cross_second(s):
        a, b = plus(s[0], s[1]), plus(s[2], s[3])
        return [a[0], py(a[1].astype(BF16)), b[0], px(b[1].astype(BF16))]

    def crossed(s):
        return jnp.stack([plus(s[0], s[1]), plus(s[2], s[3])])

    def pz_to(a, kk):
        return lax.ppermute(a, "dp", [(i, i ^ (2 * kk)) for i in range(n_dp)])

    def along(quad):
        low = quad.astype(BF16)
        return plus(quad[:, 0], *[pz_to(low[:, kk], kk) for kk in range(1, m)])

    def along_steps(quad):
        got = pz_to(quad[:, 1::2].astype(BF16), 1)
        quad = plus(quad[:, 0::2], got)
        return plus(quad[:, 0], pz_to(quad[:, 1].astype(BF16), 2))

    def pn(a):
        return lax.ppermute(a, ("dp", "tensor"), [(2 * i + 1, 2 * i + 3) for i in range(n_dp - 1)])

    def tails(keep, got):
        tail = select[:, local_rows:]
        return pn(jnp.stack([tn(tail, keep), tn(tail, got)]).astype(BF16))

    def placed(keep, got, tail):
        def place(a, b):
            a = tn(select[:, :local_rows], a).astype(BF16)
            return jnp.concatenate([a[:IMG_PAD] + b, a[IMG_PAD:]], 0)

        return jnp.stack([place(keep, tail[0]), place(got, tail[1])])

    def ordered(a, b):
        a = a + b
        return jnp.where(sec == 0, a, a[::-1])[None]

    batch_tokens = lax.dynamic_index_in_dim(tokens, sec, 0, keepdims=False)
    batch_cot = lax.dynamic_index_in_dim(cotangent, sec, 0, keepdims=False)
    count = lax.dynamic_index_in_dim(image_counts, sec, 0, keepdims=False)
    first = jnp.minimum((dp * local_rows + IMG_LEN - 1) // IMG_LEN, images)
    last = jnp.minimum(((dp + 1) * local_rows + IMG_LEN - 1) // IMG_LEN, images)
    held = last - first
    slots = -(-(-(-local_rows // IMG_LEN)) // 2)
    lower = held // 2
    own_first = jnp.where(ten == 0, first, first + lower)
    own_count = jnp.where(ten == 0, lower, held - lower)
    total = slots * IMG_PAD
    row = lax.broadcasted_iota(jnp.int32, (total, 1), 0)
    slot, inside = row // IMG_PAD, row % IMG_PAD
    exists = (inside < IMG_LEN) & (slot < own_count)
    target = (own_first + slot) * IMG_LEN + inside - dp * local_rows
    canvas_rows = local_rows + IMG_PAD
    select = ((lax.broadcasted_iota(jnp.int32, (total, canvas_rows), 1) == target) & exists).astype(BF16)
    scalars = jnp.stack([jnp.minimum(own_count, jnp.maximum(count - own_first, 0)), ten, sec, zi, yi]).astype(jnp.int32)

    both = jnp.stack([batch_tokens, batch_cot])
    halo = lax.ppermute(both[:, :IMG_PAD], ("dp", "tensor"), [(2 * i + 3, 2 * i + 1) for i in range(n_dp - 1)])
    q, k, v = [[qkv_weight[0, :, i, h * HD:(h + 1) * HD] for h in range(3)] for i in range(3)]
    o = out_weight[0].T
    o = [o[:, h * HD:(h + 1) * HD] for h in range(3)]
    misc = jnp.concatenate([norm_gains[0], row_biases[0]], 0).T
    misc = jnp.pad(misc, ((0, 0), (0, BLOCK - misc.shape[1])))
    gap = jnp.zeros((HD,), BF16)
    rows = jnp.concatenate([qv_bias[0, 0], gap, gap, gap, qv_bias[0, 1], gap, up_bias[0]]).reshape(-1, BLOCK)
    rows = jnp.pad(rows, ((0, piece - rows.shape[0]), (0, 0)))
    up, down = up_weight[0], down_weight[0].T
    part0 = jnp.concatenate([q[0], q[1], q[2], k[2], k[0], k[1], misc, up], 1)
    part1 = jnp.concatenate([v[0], v[1], v[2], o[2], o[0], o[1], rows, down], 1)

    if direct:
        keep = jnp.where(sec == 0, part0, part1)
        give = jnp.where(sec == 0, part1, part0)
        got, halo = after(px(give), halo)
        start = [jnp.where(sec == 0, keep, got), jnp.where(sec == 0, got, keep)]

        def load(l, sc, src, w, sem, c):
            copies = []
            cols = slice(0, MLP) if c == 0 else slice(MLP, HALF)
            for side in range(2):
                t = jnp.where(sc[1] == 0, side, 1 - side)
                own = src[side * 8:side * 8 + 8]
                for kk in range(m):
                    z = lax.bitwise_xor(sc[3], kk)
                    near = pl.ds(pl.multiple_of((2 * z + sc[4]) * piece, 16), piece)
                    far = pl.ds(pl.multiple_of((2 * z + 1 - sc[4]) * piece, 16), piece)
                    for i, (h, r) in enumerate(((sc[2], near), (1 - sc[2], near), (sc[2], far), (1 - sc[2], far))):
                        a = own[i].at[l, :, cols] if kk == 0 else own[4 + i].at[kk - 1, :, cols]
                        copies.append(pltpu.make_async_copy(a, w.at[t, h, r, cols], sem.at[c]))
            return copies

        part = HALF // 2

        def store(sc, side, g, dst, sem):
            copies = []
            for c in range(2):
                for i in range(2):
                    for j in range(2):
                        hr, yr = (i, j) if c == 0 else (j, i)
                        h = lax.bitwise_xor(sc[2], hr)
                        y = lax.bitwise_xor(sc[4], yr)
                        out = dst[0].at[c, i, j] if side == 0 else dst[2 * c + i].at[j]
                        for kk in range(m):
                            z = lax.bitwise_xor(sc[3], kk)
                            r = pl.ds(pl.multiple_of((2 * z + y) * piece, 16), piece)
                            a = g.at[h, r, c * part:(c + 1) * part]
                            copies.append(pltpu.make_async_copy(a, out.at[kk], sem))
            return copies

        out_shapes = [[((2, 2, 2, m, piece, part), BF16)], [((2, m, piece, part), BF16)] * 4]
        own = jnp.stack(start)
        firsts = [own, px(own), py(own), pd(own)]
        columns = [jnp.stack([pz_to(start[0], kk) for kk in range(1, m)])]
        start[1] = after(start[1], columns[0])[0]
        near = pz_to(start[1], 1)
        columns[0], near, *firsts = after(columns[0], near, *firsts)
        rest = [columns[0], px(columns[0]), py(columns[0]), pd(columns[0])]
        columns.append(jnp.concatenate([near[None], pz_to(jnp.stack([start[1], near]), 2)]))
        columns[1], *rest = after(columns[1], *rest)
        twins = [pt(a) for a in firsts]
        sources = [firsts + rest + twins + [pt(a) for a in rest]]
        sources.append(columns[1:] + [px(columns[1]), py(columns[1]), pd(columns[1])])
    else:
        def load(l, sc, src, w, sem, c):
            return [pltpu.make_async_copy(src[0], w, sem.at[c])] if c == 0 else []

        def store(sc, side, g, dst, sem):
            return [pltpu.make_async_copy(g, dst[0], sem)]

        out_shapes = [[((2, width, HALF), BF16)]] * 2
        a = lax.all_gather(jnp.stack([part0, part1]), "dp", axis=1, tiled=True)
        a = lax.all_gather(lax.all_gather(a, "tensor"), "section")
        sources = [[a[0]], [a[1]]]

    batch = jnp.concatenate([both, halo], 1)
    x0 = nn(select, batch[0]).astype(BF16)
    cot = nn(select, batch[1]).astype(BF16)
    x0, cot = after(x0, cot)

    def call(l, phases, **given):
        return layer_call(phases, sources[l], functools.partial(load, l), store, out_shapes, scalars, given,
                          total, width, ff, piece)

    r0 = call(0, ["forward"], x=x0)
    low0 = r0["out"]
    if direct:
        low0, *rest = after(low0, *sources[1])
        sources[1] = firsts + rest + twins + [pt(a) for a in rest]
    r1 = call(1, ["forward", "back", "theirs"], x=low0, u=cot)
    if direct:
        got1 = pt(r1["g"][0])
    low_got = px(r1["give"])
    m1 = call(1, ["mine"], **r1)
    u = r1["in"]
    if direct:
        first, got1 = after(m1["g"][0], got1)
        sent1 = chip_sums([first] + m1["g"][1:], got1)
        u = after(u, sent1[1], sent1[3])[0]
        low_got = after(low_got, sent1[1], sent1[3])[0]
        low_tails = tails(r1["keep"], low_got)
        quad1 = cross_first(sent1)
    else:
        low_tails = tails(r1["keep"], low_got)
    b0 = call(0, ["back", "theirs"], **{**r0, "u": u})
    if direct:
        b0["dg"], b0["g"][0], low_tails, *quad1 = after(b0["dg"], b0["g"][0], low_tails, *quad1)
        got0 = pt(b0["g"][0])
        quad1 = cross_second(quad1)
    low_rows = placed(r1["keep"], low_got, low_tails)
    low_twin = pt(low_rows)
    in_got = px(b0["give"])
    m0 = call(0, ["mine"], **{**r0, **b0})

    if direct:
        first, got0, low_twin = after(m0["g"][0], got0, low_twin)
        sent0 = chip_sums([first] + m0["g"][1:], got0)
        in_got, *quad1 = after(in_got, *quad1, sent0[1], sent0[3])[:5]
        in_tails = tails(b0["keep"], in_got)
        quad0 = cross_second(after(*cross_first(sent0)))
        in_rows = placed(b0["keep"], in_got, in_tails)
        done1 = along_steps(crossed(quad1))
        in_twin, done1, *quad0 = after(pt(in_rows), done1, *quad0)
        done0 = along(crossed(quad0))
        done0, done1 = [jnp.concatenate([a[0], a[1]], 1) for a in (done0, done1)]
        mine = jnp.where(sec == 0, done0, done1)
        other = px(jnp.where(sec == 0, done1, done0).astype(BF16))
        g_gain, g_bias, g_qkv, g_qv, g_out, g_up, g_up_bias, g_down = finish(scalars, mine, other, ff // 2)
    else:
        in_rows = placed(b0["keep"], in_got, tails(b0["keep"], in_got))
        in_twin = pt(in_rows)

        def by_core(a, b):
            return jnp.where(ten == 0, jnp.stack([b, a]), jnp.stack([a, b]))

        g = jnp.stack([by_core(b0["g"][0], m0["g"][0]), by_core(r1["g"][0], m1["g"][0])])
        g = lax.psum_scatter(g.astype(F32), "section", scatter_dimension=0)
        g = lax.psum_scatter(g, "tensor", scatter_dimension=0)
        g = lax.psum_scatter(g, "dp", scatter_dimension=1, tiled=True)
        small = lax.psum(jnp.stack([b0["bsum"], r1["bsum"]]), ("section", "tensor", "dp"))
        small = lax.dynamic_index_in_dim(lax.dynamic_index_in_dim(small, sec, 0, False), ten, 0, False)
        g_gain, g_bias, g_qkv, _, g_out, g_up, _, g_down = parts(g[0], g[1], ff // 2)
        small = jnp.pad(small, ((0, 0), (MISC, HALF - MLP)))
        _, _, _, g_qv, _, _, g_up_bias, _ = parts(small, small, ff // 2)

    layer_outputs = ordered(low_rows, low_twin)
    input_grads = ordered(in_rows, in_twin).astype(F32)

    return (
        layer_outputs,
        input_grads,
        g_gain[None],
        g_bias[None],
        g_qkv.transpose(1, 0, 2)[None],
        g_qv[None],
        g_out.T[None],
        g_up[None],
        g_up_bias,
        g_down.T[None],
    )


def solution(mesh):
    in_specs = (
        P(None, "dp", None),
        P(),
        P(None, "dp", None),
        P("section", None, "dp"),
        P("section", None, "dp"),
        P("section", "dp", None, "tensor"),
        P("section", None, "tensor"),
        P("section", "tensor", "dp"),
        P("section", "dp", "tensor"),
        P("section", "tensor"),
        P("section", "tensor", "dp"),
    )
    out_specs = (
        P("section", None, "dp", None),
        P("section", None, "dp", None),
        P("section", None, "dp"),
        P("section", None, "dp"),
        P("section", "dp", None, "tensor"),
        P("section", None, "tensor"),
        P("section", "tensor", "dp"),
        P("section", "dp", "tensor"),
        P("section", "tensor"),
        P("section", "tensor", "dp"),
    )
    return jax.shard_map(shards, mesh=mesh, in_specs=in_specs, out_specs=out_specs, check_vma=False)
```

profile of v0, /device:TPU:0, one launch (start us, length us, event | category | flops | bytes accessed | tf_op | source)
XLA Modules:
  0.0 186.3 jit_solution(8795365648498236254)
XLA Ops:
  0.7 1.3 constant_dynamic-slice_fusion
  2.1 0.7 collective-permute-start.1
  3.5 3.0 %collective-permute-start = (bf16[48,1280]{1,0:T(8,128)(2,1)S(1)}, bf16[48,1280]{1,0:T(8,128)(2,1)S(1)}, u32[]{:S(2)}, u32[]{:S(2)}) collective-permute-start(bf16[48,1280]{1,0:T(8,128)(2,1)S(1)} %broadcast_select_fusion.3), channel_id=1, source_target_pairs={{0,16},{16,0},{1,17},{17,1},{2,18},{18,2},{3,19},{19,3},{4,20},{20... | collective-permute-start | bytes 368648 | tf_op jit(solution)/shard_map/ppermute | solution.py:411
  6.5 3.9 %collective-permute-done = bf16[48,1280]{1,0:T(8,128)(2,1)S(1)} collective-permute-done((bf16[48,1280]{1,0:T(8,128)(2,1)S(1)}, bf16[48,1280]{1,0:T(8,128)(2,1)S(1)}, u32[]{:S(2)}, u32[]{:S(2)}) %collective-permute-start) | collective-permute-done | bytes 122912 | tf_op jit(solution)/shard_map/ppermute | solution.py:411
  10.5 1.2 collective-permute-start.2
  11.7 2.6 %collective-permute-start.3 = (bf16[48,1280]{1,0:T(8,128)(2,1)S(1)}, bf16[48,1280]{1,0:T(8,128)(2,1)S(1)}, u32[]{:S(2)}, u32[]{:S(2)}) collective-permute-start(bf16[48,1280]{1,0:T(8,128)(2,1)S(1)} %get-tuple-element.226), channel_id=1, source_target_pairs={{0,8},{2,10},{4,12},{6,14},{8,0},{10,2},{12,4},{14,6},{1,9},{3,11}... | collective-permute-start | bytes 368648 | tf_op jit(solution)/shard_map/ppermute | solution.py:440
  14.3 0.7 collective-permute-start.4
  15.0 1.8 collective-permute-start.6
  16.8 1.7 collective-permute-start.7
  18.6 3.1 %collective-permute-start.8 = (bf16[2,48,1280]{2,1,0:T(8,128)(2,1)S(1)}, bf16[2,48,1280]{2,1,0:T(8,128)(2,1)S(1)}, u32[]{:S(2)}, u32[]{:S(2)}) collective-permute-start(bf16[2,48,1280]{2,1,0:T(8,128)(2,1)S(1)} %pad_maximum_fusion.10.refs_2_.refs_3_.refs_13_), channel_id=1, source_target_pairs={{0,18},{2,16},{4,22},{6,20},{8,26},{10,24},{12,30},{14,28},{16,2},... | collective-permute-start | bytes 737288 | tf_op jit(solution)/shard_map/ppermute | solution.py:417
  21.7 2.4 %collective-permute-done.3 = bf16[48,1280]{1,0:T(8,128)(2,1)S(1)} collective-permute-done((bf16[48,1280]{1,0:T(8,128)(2,1)S(1)}, bf16[48,1280]{1,0:T(8,128)(2,1)S(1)}, u32[]{:S(2)}, u32[]{:S(2)}) %collective-permute-start.3) | collective-permute-done | bytes 122912 | tf_op jit(solution)/shard_map/ppermute | solution.py:440
  24.1 3.1 %collective-permute-start.5 = (bf16[48,1280]{1,0:T(8,128)(2,1)S(1)}, bf16[48,1280]{1,0:T(8,128)(2,1)S(1)}, u32[]{:S(2)}, u32[]{:S(2)}) collective-permute-start(bf16[48,1280]{1,0:T(8,128)(2,1)S(1)} %get-tuple-element.114), channel_id=1, source_target_pairs={{0,4},{2,6},{4,0},{6,2},{8,12},{10,14},{12,8},{14,10},{1,5},{3,7},... | collective-permute-start | bytes 368648 | tf_op jit(solution)/shard_map/ppermute | solution.py:440
  27.3 3.5 %collective-permute-done.5 = bf16[48,1280]{1,0:T(8,128)(2,1)S(1)} collective-permute-done((bf16[48,1280]{1,0:T(8,128)(2,1)S(1)}, bf16[48,1280]{1,0:T(8,128)(2,1)S(1)}, u32[]{:S(2)}, u32[]{:S(2)}) %collective-permute-start.5) | collective-permute-done | bytes 122912 | tf_op jit(solution)/shard_map/ppermute | solution.py:440
  30.8 2.8 %collective-permute-start.9 = (bf16[2,48,1280]{2,1,0:T(8,128)(2,1)S(1)}, bf16[2,48,1280]{2,1,0:T(8,128)(2,1)S(1)}, u32[]{:S(2)}, u32[]{:S(2)}) collective-permute-start(bf16[2,48,1280]{2,1,0:T(8,128)(2,1)S(1)} %pad_maximum_fusion.11), channel_id=1, source_target_pairs={{0,8},{2,10},{4,12},{6,14},{8,0},{10,2},{12,4},{14,6},{1,9},{3,11}... | collective-permute-start | bytes 737288 | tf_op jit(solution)/shard_map/ppermute | solution.py:440
  33.6 0.6 dynamic_slice.11
  35.0 1.6 collective-permute-start.10
  36.5 2.4 %collective-permute-start.11 = (bf16[3,48,1280]{2,1,0:T(8,128)(2,1)S(1)}, bf16[3,48,1280]{2,1,0:T(8,128)(2,1)S(1)}, u32[]{:S(2)}, u32[]{:S(2)}) collective-permute-start(bf16[3,48,1280]{2,1,0:T(8,128)(2,1)S(1)} %pad_maximum_fusion.5.refs_6_.refs_17_), channel_id=1, source_target_pairs={{0,2},{2,0},{4,6},{6,4},{8,10},{10,8},{12,14},{14,12},{1,3},{3,1},... | collective-permute-start | bytes 1105928 | tf_op jit(solution)/shard_map/ppermute | solution.py:414
  38.9 5.3 %collective-permute-done.9 = bf16[2,48,1280]{2,1,0:T(8,128)(2,1)S(1)} collective-permute-done((bf16[2,48,1280]{2,1,0:T(8,128)(2,1)S(1)}, bf16[2,48,1280]{2,1,0:T(8,128)(2,1)S(1)}, u32[]{:S(2)}, u32[]{:S(2)}) %collective-permute-start.9) | collective-permute-done | bytes 245792 | tf_op jit(solution)/shard_map/ppermute | solution.py:440
  44.4 2.1 %collective-permute-done.10.refs_7_.refs_18_ = bf16[3,48,1280]{2,1,0:T(8,128)(2,1)S(1)} collective-permute-done((bf16[3,48,1280]{2,1,0:T(8,128)(2,1)S(1)}, bf16[3,48,1280]{2,1,0:T(8,128)(2,1)S(1)}, u32[]{:S(2)}, u32[]{:S(2)}) %collective-permute-start.10) | collective-permute-done | bytes 368672 | tf_op jit(solution)/shard_map/ppermute | solution.py:411
  46.5 6.9 %collective-permute-done.11.refs_8_.refs_19_ = bf16[3,48,1280]{2,1,0:T(8,128)(2,1)S(1)} collective-permute-done((bf16[3,48,1280]{2,1,0:T(8,128)(2,1)S(1)}, bf16[3,48,1280]{2,1,0:T(8,128)(2,1)S(1)}, u32[]{:S(2)}, u32[]{:S(2)}) %collective-permute-start.11) | collective-permute-done | bytes 368672 | tf_op jit(solution)/shard_map/ppermute | solution.py:414
  53.4 0.7 collective-permute-done.12.refs_9_.refs_20_
  55.2 0.5 convolution_convert_fusion.4.refs_2_
  55.9 0.5 convolution_convert_fusion.5.refs_1_
  56.4 1.3 collective-permute-done.16.refs_13_.refs_14_.refs_24_
  57.8 1.5 collective-permute-start.21
  59.2 0.8 collective-permute-start.22
  60.1 1.2 collective-permute-start.23
  61.3 8.6 %shard_map.186 = (bf16[416,384]{1,0:T(8,128)(2,1)S(1)}, f32[416,384]{1,0:T(8,128)S(1)}, f32[416,128]{1,0:T(8,128)S(1)}, bf16[416,384]{1,0:T(8,128)(2,1)S(1)}, bf...) custom-call(s32[5]{0:T(128)S(1)} %stack.116.refs_0_.sc, ...), custom_call_target="tpu_custom_call" | custom-call | flops 10000000000 | bytes 8388608 | tf_op jit(solution)/shard_map/pallas_call | solution.py:342
  69.9 6.0 %collective-permute-done.22.refs_9_ = bf16[3,48,1280]{2,1,0:T(8,128)(2,1)S(1)} collective-permute-done((bf16[3,48,1280]{2,1,0:T(8,128)(2,1)S(1)}, bf16[3,48,1280]{2,1,0:T(8,128)(2,1)S(1)}, u32[]{:S(2)}, u32[]{:S(2)}) %collective-permute-start.22) | collective-permute-done | bytes 368672 | tf_op jit(solution)/shard_map/ppermute | solution.py:414
  75.9 1.6 collective-permute-done.23.refs_10_
  78.5 0.7 collective-permute-done.24.refs_15_
  80.8 18.7 %shard_map.187 = (bf16[416,384]{1,0:T(8,128)(2,1)S(1)}, bf16[2,416,256]{2,1,0:T(8,128)(2,1)S(1)}, bf16[416,384]{1,0:T(8,128)(2,1)S(1)}, bf16[416,1536]{1,0:T(8,1...) custom-call(s32[5]{0:T(128)S(1)} %stack.116.refs_0_.sc, ...), custom_call_target="tpu_custom_call" | custom-call | flops 30000001024 | bytes 8388608 | tf_op jit(solution)/shard_map/pallas_call | solution.py:342
  100.0 0.6 collective-permute-start.29
  101.5 2.2 %shard_map.188 = (bf16[2,4,48,640]{3,2,1,0:T(8,128)(2,1)S(1)}, bf16[2,4,48,640]{3,2,1,0:T(8,128)(2,1)S(1)}, bf16[2,4,48,640]{3,2,1,0:T(8,128)(2,1)S(1)}, bf16[2,4,48,640]{3,2,1,0:T(8,128)(2,1)S(1)}) custom-call(s32[5]{0:T(128)S(1)} %stack.116.refs_0_.sc, bf16[416,384]{1,0:T(8,128)(2,1)S(1)} %get-tuple-element.135.refs_1_, ...), custom_call_target="tpu_custom_call" | custom-call | flops 10000000000 | bytes 8388608 | tf_op jit(solution)/shard_map/pallas_call | solution.py:342
  104.2 1.5 collective-permute-start.31
  105.7 0.8 collective-permute-start.32
  106.6 3.9 %collective-permute-done.29 = bf16[416,384]{1,0:T(8,128)(2,1)S(1)} collective-permute-done((bf16[416,384]{1,0:T(8,128)(2,1)S(1)}, bf16[416,384]{1,0:T(8,128)(2,1)S(1)}, u32[]{:S(2)}, u32[]{:S(2)}) %collective-permute-start.29) | collective-permute-done | bytes 319520 | tf_op jit(solution)/shard_map/ppermute | solution.py:411
  110.9 0.7 collective-permute-start.30
  111.6 11.9 %shard_map.189 = (bf16[416,384]{1,0:T(8,128)(2,1)S(1)}, bf16[416,384]{1,0:T(8,128)(2,1)S(1)}, bf16[416,384]{1,0:T(8,128)(2,1)S(1)}, bf16[416,1536]{1,0:T(8,128)(...) custom-call(s32[5]{0:T(128)S(1)} %stack.116.refs_0_.sc, ...), custom_call_target="tpu_custom_call" | custom-call | flops 20000000000 | bytes 8388608 | tf_op jit(solution)/shard_map/pallas_call | solution.py:342
  124.0 0.7 collective-permute-start.35
  125.8 1.5 collective-permute-start.34
  127.5 0.6 collective-permute-start.37
  128.2 1.2 collective-permute-start.36
  129.5 2.2 %shard_map.190 = (bf16[2,4,48,640]{3,2,1,0:T(8,128)(2,1)S(1)}, bf16[2,4,48,640]{3,2,1,0:T(8,128)(2,1)S(1)}, bf16[2,4,48,640]{3,2,1,0:T(8,128)(2,1)S(1)}, bf16[2,4,48,640]{3,2,1,0:T(8,128)(2,1)S(1)}) custom-call(s32[5]{0:T(128)S(1)} %stack.116.refs_0_.sc, bf16[416,384]{1,0:T(8,128)(2,1)S(1)} %get-tuple-element.153.refs_4_.refs_1_, ...), custom_call_target="tpu_custom_call" | custom-call | flops 10000000000 | bytes 8388608 | tf_op jit(solution)/shard_map/pallas_call | solution.py:342
  132.5 0.9 collective-permute-start.42
  133.4 1.3 collective-permute-start.43
  134.7 5.1 %collective-permute-done.37 = bf16[4,48,640]{2,1,0:T(8,128)(2,1)S(1)} collective-permute-done((bf16[4,48,640]{2,1,0:T(8,128)(2,1)S(1)}, bf16[4,48,640]{2,1,0:T(8,128)(2,1)S(1)}, u32[]{:S(2)}, u32[]{:S(2)}) %collective-permute-start.37) | collective-permute-done | bytes 245792 | tf_op jit(solution)/shard_map/ppermute | solution.py:411
  140.9 0.6 collective-permute-start.40
  141.6 0.7 collective-permute-start.38
  142.4 1.0 fusion.10
  143.4 5.0 %collective-permute-done.40 = bf16[2,2,48,640]{3,2,0,1:T(8,128)(2,1)S(1)} collective-permute-done((bf16[2,2,48,640]{3,2,0,1:T(8,128)(2,1)S(1)}, bf16[2,2,48,640]{3,2,0,1:T(8,128)(2,1)S(1)}, u32[]{:S(2)}, u32[]{:S(2)}) %collective-permute-start.40) | collective-permute-done | bytes 245792 | tf_op jit(solution)/shard_map/ppermute | solution.py:440
  149.4 6.7 %collective-permute-done.41 = bf16[2,48,640]{2,1,0:T(8,128)(2,1)S(1)} collective-permute-done((bf16[2,48,640]{2,1,0:T(8,128)(2,1)S(1)}, bf16[2,48,640]{2,1,0:T(8,128)(2,1)S(1)}, u32[]{:S(2)}, u32[]{:S(2)}) %collective-permute-start.41) | collective-permute-done | bytes 122912 | tf_op jit(solution)/shard_map/ppermute | solution.py:440
  156.2 2.7 %collective-permute-start.45 = (bf16[4,48,640]{2,1,0:T(8,128)(2,1)S(1)}, bf16[4,48,640]{2,1,0:T(8,128)(2,1)S(1)}, u32[]{:S(2)}, u32[]{:S(2)}) collective-permute-start(bf16[4,48,640]{2,1,0:T(8,128)(2,1)S(1)} %fusion.20), channel_id=1, source_target_pairs={{0,16},{16,0},{1,17},{17,1},{2,18},{18,2},{3,19},{19,3},{4,20},{20... | collective-permute-start | bytes 737288 | tf_op jit(solution)/shard_map/ppermute | solution.py:411
  159.2 5.8 %collective-permute-done.45 = bf16[4,48,640]{2,1,0:T(8,128)(2,1)S(1)} collective-permute-done((bf16[4,48,640]{2,1,0:T(8,128)(2,1)S(1)}, bf16[4,48,640]{2,1,0:T(8,128)(2,1)S(1)}, u32[]{:S(2)}, u32[]{:S(2)}) %collective-permute-start.45) | collective-permute-done | bytes 245792 | tf_op jit(solution)/shard_map/ppermute | solution.py:411
  165.1 1.7 collective-permute-done.44
  167.0 2.0 %collective-permute-start.47 = (bf16[2,48,640]{2,1,0:T(8,128)(2,1)S(1)}, bf16[2,48,640]{2,1,0:T(8,128)(2,1)S(1)}, u32[]{:S(2)}, u32[]{:S(2)}) collective-permute-start(bf16[2,48,640]{2,1,0:T(8,128)(2,1)S(1)} %get-tuple-element.224), channel_id=1, source_target_pairs={{0,8},{2,10},{4,12},{6,14},{8,0},{10,2},{12,4},{14,6},{1,9},{3,11}... | collective-permute-start | bytes 368648 | tf_op jit(solution)/shard_map/ppermute | solution.py:440
  169.0 2.4 %collective-permute-start.48 = (bf16[2,48,640]{2,1,0:T(8,128)(2,1)S(1)}, bf16[2,48,640]{2,1,0:T(8,128)(2,1)S(1)}, u32[]{:S(2)}, u32[]{:S(2)}) collective-permute-start(bf16[2,48,640]{2,1,0:T(8,128)(2,1)S(1)} %get-tuple-element.223), channel_id=1, source_target_pairs={{0,12},{2,14},{4,8},{6,10},{8,4},{10,6},{12,0},{14,2},{1,13},{3,15... | collective-permute-start | bytes 368648 | tf_op jit(solution)/shard_map/ppermute | solution.py:440
  171.5 1.2 fusion.12
  172.8 5.9 %collective-permute-done.47 = bf16[2,48,640]{2,1,0:T(8,128)(2,1)S(1)} collective-permute-done((bf16[2,48,640]{2,1,0:T(8,128)(2,1)S(1)}, bf16[2,48,640]{2,1,0:T(8,128)(2,1)S(1)}, u32[]{:S(2)}, u32[]{:S(2)}) %collective-permute-start.47) | collective-permute-done | bytes 122912 | tf_op jit(solution)/shard_map/ppermute | solution.py:440
  178.9 0.6 collective-permute-start.49
  179.5 0.7 fusion.27.mine_ref
  180.2 3.6 %collective-permute-done.49.other_ref = bf16[48,1280]{1,0:T(8,128)(2,1)S(1)} collective-permute-done((bf16[48,1280]{1,0:T(8,128)(2,1)S(1)}, bf16[48,1280]{1,0:T(8,128)(2,1)S(1)}, u32[]{:S(2)}, u32[]{:S(2)}) %collective-permute-start.49) | collective-permute-done | bytes 122912 | tf_op jit(solution)/shard_map/ppermute | solution.py:411
  183.8 0.7 copy-done.2
  184.5 1.9 %shard_map.191 = (f32[2,48]{1,0:T(2,128)}, f32[4,48]{1,0:T(4,128)}, f32[3,48,192]{2,1,0:T(8,128)}, f32[2,192]{1,0:T(2,128)}, f32[48,192]{1,0:T(8,128)}, /*index=...) custom-call(s32[5]{0:T(128)} %copy-done, f32[48,1280]{1,0:T(8,128)} %fusion.27.mine_ref, bf16[48,1280]{1,0:T(8,128)(2,1)} %copy-done.2), custom_call_target="tpu_custom_call" | custom-call | tf_op jit(solution)/shard_map/pallas_call | solution.py:385
  (151 shorter events, 13.1 us)
Async XLA Ops:
  0.7 2.1 %copy-start.5 = (bf16[1,192,48]{1,2,0:T(8,128)(2,1)S(1)}, bf16[1,192,48]{1,2,0:T(8,128)(2,1)}, u32[]{:S(2)}) copy-start(bf16[1,192,48]{1,2,0:T(8,128)(2,1)} %param.18) | copy-start | bytes 55300
  0.7 2.1 %copy-start.1 = (bf16[1,48,3,192]{3,1,2,0:T(8,128)(2,1)S(1)}, bf16[1,48,3,192]{3,1,2,0:T(8,128)(2,1)}, u32[]{:S(2)}) copy-start(bf16[1,48,3,192]{3,1,2,0:T(8,128)(2,1)} %param.16) | copy-start | bytes 165892
  0.7 2.2 %copy-start.8 = (bf16[1,4,48]{2,1,0:T(4,128)(2,1)S(1)}, bf16[1,4,48]{2,1,0:T(4,128)(2,1)}, u32[]{:S(2)}) copy-start(bf16[1,4,48]{2,1,0:T(4,128)(2,1)} %param.15) | copy-start | bytes 1156
  0.7 2.2 %copy-start.9 = (bf16[1,2,48]{2,1,0:T(2,128)(2,1)S(1)}, bf16[1,2,48]{2,1,0:T(2,128)(2,1)}, u32[]{:S(2)}) copy-start(bf16[1,2,48]{2,1,0:T(2,128)(2,1)} %param.14) | copy-start | bytes 580
  0.7 2.3 %copy-start.6 = (bf16[1,2,192]{2,1,0:T(2,128)(2,1)S(1)}, bf16[1,2,192]{2,1,0:T(2,128)(2,1)}, u32[]{:S(2)}) copy-start(bf16[1,2,192]{2,1,0:T(2,128)(2,1)} %param.17) | copy-start | bytes 2308
  0.7 2.4 %copy-start.7 = (bf16[1,768]{1,0:T(2,128)(2,1)S(1)}, bf16[1,768]{1,0:T(2,128)(2,1)}, u32[]{:S(2)}) copy-start(bf16[1,768]{1,0:T(2,128)(2,1)} %param.20) | copy-start | bytes 4612
  0.7 2.5 %copy-start.3 = (bf16[1,768,48]{1,2,0:T(8,128)(2,1)S(1)}, bf16[1,768,48]{1,2,0:T(8,128)(2,1)}, u32[]{:S(2)}) copy-start(bf16[1,768,48]{1,2,0:T(8,128)(2,1)} %param.21) | copy-start | bytes 221188
  0.7 2.6 %copy-start.4 = (bf16[1,48,768]{2,1,0:T(8,128)(2,1)S(1)}, bf16[1,48,768]{2,1,0:T(8,128)(2,1)}, u32[]{:S(2)}) copy-start(bf16[1,48,768]{2,1,0:T(8,128)(2,1)} %param.19) | copy-start | bytes 221188
  2.1 8.4 %collective-permute-start.1 = (bf16[2,208,384]{2,1,0:T(8,128)(2,1)S(1)}, bf16[2,208,384]{2,1,0:T(8,128)(2,1)S(1)}, u32[]{:S(2)}, u32[]{:S(2)}) collective-permute-start(bf16[2,208,384]{2,1,0:T(8,128)(2,1)S(1)} %pad_maximum_fusion.7), channel_id=1, source_target_pairs={{3,1},{5,3},{7,5},{9,7},{11,9},{13,11},{15,13},{19,17},{21,19},{23... | collective-permute-start | bytes 958472 | tf_op jit(solution)/shard_map/ppermute | solution.py:489
  3.5 30.1 %copy-start.10 = (s32[2]{0:T(128)S(1)}, s32[2]{0:T(128)}, u32[]{:S(2)}) copy-start(s32[2]{0:T(128)} %param.12) | copy-start | bytes 28
  3.5 7.0 %collective-permute-start = (bf16[48,1280]{1,0:T(8,128)(2,1)S(1)}, bf16[48,1280]{1,0:T(8,128)(2,1)S(1)}, u32[]{:S(2)}, u32[]{:S(2)}) collective-permute-start(bf16[48,1280]{1,0:T(8,128)(2,1)S(1)} %broadcast_select_fusion.3), channel_id=1, source_target_pairs={{0,16},{16,0},{1,17},{17,1},{2,18},{18,2},{3,19},{19,3},{4,20},{20... | collective-permute-start | bytes 368648 | tf_op jit(solution)/shard_map/ppermute | solution.py:411
  10.5 8.2 %collective-permute-start.2 = (bf16[48,1280]{1,0:T(8,128)(2,1)S(1)}, bf16[48,1280]{1,0:T(8,128)(2,1)S(1)}, u32[]{:S(2)}, u32[]{:S(2)}) collective-permute-start(bf16[48,1280]{1,0:T(8,128)(2,1)S(1)} %get-tuple-element.226), channel_id=1, source_target_pairs={{0,4},{2,6},{4,0},{6,2},{8,12},{10,14},{12,8},{14,10},{1,5},{3,7},... | collective-permute-start | bytes 368648 | tf_op jit(solution)/shard_map/ppermute | solution.py:440
  11.7 12.4 %collective-permute-start.3 = (bf16[48,1280]{1,0:T(8,128)(2,1)S(1)}, bf16[48,1280]{1,0:T(8,128)(2,1)S(1)}, u32[]{:S(2)}, u32[]{:S(2)}) collective-permute-start(bf16[48,1280]{1,0:T(8,128)(2,1)S(1)} %get-tuple-element.226), channel_id=1, source_target_pairs={{0,8},{2,10},{4,12},{6,14},{8,0},{10,2},{12,4},{14,6},{1,9},{3,11}... | collective-permute-start | bytes 368648 | tf_op jit(solution)/shard_map/ppermute | solution.py:440
  14.3 9.8 %collective-permute-start.4 = (bf16[48,1280]{1,0:T(8,128)(2,1)S(1)}, bf16[48,1280]{1,0:T(8,128)(2,1)S(1)}, u32[]{:S(2)}, u32[]{:S(2)}) collective-permute-start(bf16[48,1280]{1,0:T(8,128)(2,1)S(1)} %get-tuple-element.226), channel_id=1, source_target_pairs={{0,12},{2,14},{4,8},{6,10},{8,4},{10,6},{12,0},{14,2},{1,13},{3,15... | collective-permute-start | bytes 368648 | tf_op jit(solution)/shard_map/ppermute | solution.py:440
  15.0 15.8 %collective-permute-start.6 = (bf16[2,48,1280]{2,1,0:T(8,128)(2,1)S(1)}, bf16[2,48,1280]{2,1,0:T(8,128)(2,1)S(1)}, u32[]{:S(2)}, u32[]{:S(2)}) collective-permute-start(bf16[2,48,1280]{2,1,0:T(8,128)(2,1)S(1)} %pad_maximum_fusion.10.refs_2_.refs_3_.refs_13_), channel_id=1, source_target_pairs={{0,16},{16,0},{1,17},{17,1},{2,18},{18,2},{3,19},{19,3},{4,20},{20... | collective-permute-start | bytes 737288 | tf_op jit(solution)/shard_map/ppermute | solution.py:411
  16.8 14.0 %collective-permute-start.7 = (bf16[2,48,1280]{2,1,0:T(8,128)(2,1)S(1)}, bf16[2,48,1280]{2,1,0:T(8,128)(2,1)S(1)}, u32[]{:S(2)}, u32[]{:S(2)}) collective-permute-start(bf16[2,48,1280]{2,1,0:T(8,128)(2,1)S(1)} %pad_maximum_fusion.10.refs_2_.refs_3_.refs_13_), channel_id=1, source_target_pairs={{0,2},{2,0},{4,6},{6,4},{8,10},{10,8},{12,14},{14,12},{1,3},{3,1},... | collective-permute-start | bytes 737288 | tf_op jit(solution)/shard_map/ppermute | solution.py:414
  18.6 12.1 %collective-permute-start.8 = (bf16[2,48,1280]{2,1,0:T(8,128)(2,1)S(1)}, bf16[2,48,1280]{2,1,0:T(8,128)(2,1)S(1)}, u32[]{:S(2)}, u32[]{:S(2)}) collective-permute-start(bf16[2,48,1280]{2,1,0:T(8,128)(2,1)S(1)} %pad_maximum_fusion.10.refs_2_.refs_3_.refs_13_), channel_id=1, source_target_pairs={{0,18},{2,16},{4,22},{6,20},{8,26},{10,24},{12,30},{14,28},{16,2},... | collective-permute-start | bytes 737288 | tf_op jit(solution)/shard_map/ppermute | solution.py:417
  24.1 6.6 %collective-permute-start.5 = (bf16[48,1280]{1,0:T(8,128)(2,1)S(1)}, bf16[48,1280]{1,0:T(8,128)(2,1)S(1)}, u32[]{:S(2)}, u32[]{:S(2)}) collective-permute-start(bf16[48,1280]{1,0:T(8,128)(2,1)S(1)} %get-tuple-element.114), channel_id=1, source_target_pairs={{0,4},{2,6},{4,0},{6,2},{8,12},{10,14},{12,8},{14,10},{1,5},{3,7},... | collective-permute-start | bytes 368648 | tf_op jit(solution)/shard_map/ppermute | solution.py:440
  30.8 13.5 %collective-permute-start.9 = (bf16[2,48,1280]{2,1,0:T(8,128)(2,1)S(1)}, bf16[2,48,1280]{2,1,0:T(8,128)(2,1)S(1)}, u32[]{:S(2)}, u32[]{:S(2)}) collective-permute-start(bf16[2,48,1280]{2,1,0:T(8,128)(2,1)S(1)} %pad_maximum_fusion.11), channel_id=1, source_target_pairs={{0,8},{2,10},{4,12},{6,14},{8,0},{10,2},{12,4},{14,6},{1,9},{3,11}... | collective-permute-start | bytes 737288 | tf_op jit(solution)/shard_map/ppermute | solution.py:440
  34.9 94.6 %copy-start = (s32[5]{0:T(128)}, s32[5]{0:T(128)S(1)}, u32[]{:S(2)}) copy-start(s32[5]{0:T(128)S(1)} %stack.116.refs_0_.sc) | copy-start | bytes 64
  35.0 11.5 %collective-permute-start.10 = (bf16[3,48,1280]{2,1,0:T(8,128)(2,1)S(1)}, bf16[3,48,1280]{2,1,0:T(8,128)(2,1)S(1)}, u32[]{:S(2)}, u32[]{:S(2)}) collective-permute-start(bf16[3,48,1280]{2,1,0:T(8,128)(2,1)S(1)} %pad_maximum_fusion.5.refs_6_.refs_17_), channel_id=1, source_target_pairs={{0,16},{16,0},{1,17},{17,1},{2,18},{18,2},{3,19},{19,3},{4,20},{20... | collective-permute-start | bytes 1105928 | tf_op jit(solution)/shard_map/ppermute | solution.py:411
  36.5 16.9 %collective-permute-start.11 = (bf16[3,48,1280]{2,1,0:T(8,128)(2,1)S(1)}, bf16[3,48,1280]{2,1,0:T(8,128)(2,1)S(1)}, u32[]{:S(2)}, u32[]{:S(2)}) collective-permute-start(bf16[3,48,1280]{2,1,0:T(8,128)(2,1)S(1)} %pad_maximum_fusion.5.refs_6_.refs_17_), channel_id=1, source_target_pairs={{0,2},{2,0},{4,6},{6,4},{8,10},{10,8},{12,14},{14,12},{1,3},{3,1},... | collective-permute-start | bytes 1105928 | tf_op jit(solution)/shard_map/ppermute | solution.py:414
  38.9 15.2 %collective-permute-start.12 = (bf16[3,48,1280]{2,1,0:T(8,128)(2,1)S(1)}, bf16[3,48,1280]{2,1,0:T(8,128)(2,1)S(1)}, u32[]{:S(2)}, u32[]{:S(2)}) collective-permute-start(bf16[3,48,1280]{2,1,0:T(8,128)(2,1)S(1)} %pad_maximum_fusion.5.refs_6_.refs_17_), channel_id=1, source_target_pairs={{0,18},{2,16},{4,22},{6,20},{8,26},{10,24},{12,30},{14,28},{16,2},... | collective-permute-start | bytes 1105928 | tf_op jit(solution)/shard_map/ppermute | solution.py:417
  38.9 15.7 %collective-permute-start.13 = (bf16[2,48,1280]{2,1,0:T(8,128)(2,1)S(1)}, bf16[2,48,1280]{2,1,0:T(8,128)(2,1)S(1)}, u32[]{:S(2)}, u32[]{:S(2)}) collective-permute-start(bf16[2,48,1280]{2,1,0:T(8,128)(2,1)S(1)} %pad_maximum_fusion.10.refs_2_.refs_3_.refs_13_), channel_id=1, source_target_pairs={{0,1},{1,0},{2,3},{3,2},{4,5},{5,4},{6,7},{7,6},{8,9},{9,8},{10,11... | collective-permute-start | bytes 737288 | tf_op jit(solution)/shard_map/ppermute | solution.py:408
  44.2 10.4 %collective-permute-start.14 = (bf16[2,48,1280]{2,1,0:T(8,128)(2,1)S(1)}, bf16[2,48,1280]{2,1,0:T(8,128)(2,1)S(1)}, u32[]{:S(2)}, u32[]{:S(2)}) collective-permute-start(bf16[2,48,1280]{2,1,0:T(8,128)(2,1)S(1)} %collective-permute-done.6.refs_3_.refs_4_.refs_14_), channel_id=1, source_target_pairs={{0,1},{1,0},{2,3},{3,2},{4,5},{5,4},{6,7},{7,6},{8,9},{9,8},{10,11... | collective-permute-start | bytes 737288 | tf_op jit(solution)/shard_map/ppermute | solution.py:408
  46.5 9.3 %collective-permute-start.15 = (bf16[2,48,1280]{2,1,0:T(8,128)(2,1)S(1)}, bf16[2,48,1280]{2,1,0:T(8,128)(2,1)S(1)}, u32[]{:S(2)}, u32[]{:S(2)}) collective-permute-start(bf16[2,48,1280]{2,1,0:T(8,128)(2,1)S(1)} %collective-permute-done.7.refs_4_.refs_5_.refs_15_), channel_id=1, source_target_pairs={{0,1},{1,0},{2,3},{3,2},{4,5},{5,4},{6,7},{7,6},{8,9},{9,8},{10,11... | collective-permute-start | bytes 737288 | tf_op jit(solution)/shard_map/ppermute | solution.py:408
  54.2 5.1 %collective-permute-start.17 = (bf16[3,48,1280]{2,1,0:T(8,128)(2,1)S(1)}, bf16[3,48,1280]{2,1,0:T(8,128)(2,1)S(1)}, u32[]{:S(2)}, u32[]{:S(2)}) collective-permute-start(bf16[3,48,1280]{2,1,0:T(8,128)(2,1)S(1)} %pad_maximum_fusion.5.refs_6_.refs_17_), channel_id=1, source_target_pairs={{0,1},{1,0},{2,3},{3,2},{4,5},{5,4},{6,7},{7,6},{8,9},{9,8},{10,11... | collective-permute-start | bytes 1105928 | tf_op jit(solution)/shard_map/ppermute | solution.py:408
  54.2 5.9 %collective-permute-start.18 = (bf16[3,48,1280]{2,1,0:T(8,128)(2,1)S(1)}, bf16[3,48,1280]{2,1,0:T(8,128)(2,1)S(1)}, u32[]{:S(2)}, u32[]{:S(2)}) collective-permute-start(bf16[3,48,1280]{2,1,0:T(8,128)(2,1)S(1)} %collective-permute-done.10.refs_7_.refs_18_), channel_id=1, source_target_pairs={{0,1},{1,0},{2,3},{3,2},{4,5},{5,4},{6,7},{7,6},{8,9},{9,8},{10,11... | collective-permute-start | bytes 1105928 | tf_op jit(solution)/shard_map/ppermute | solution.py:408
  54.7 6.6 %collective-permute-start.19 = (bf16[3,48,1280]{2,1,0:T(8,128)(2,1)S(1)}, bf16[3,48,1280]{2,1,0:T(8,128)(2,1)S(1)}, u32[]{:S(2)}, u32[]{:S(2)}) collective-permute-start(bf16[3,48,1280]{2,1,0:T(8,128)(2,1)S(1)} %collective-permute-done.11.refs_8_.refs_19_), channel_id=1, source_target_pairs={{0,1},{1,0},{2,3},{3,2},{4,5},{5,4},{6,7},{7,6},{8,9},{9,8},{10,11... | collective-permute-start | bytes 1105928 | tf_op jit(solution)/shard_map/ppermute | solution.py:408
  54.7 6.6 %collective-permute-start.20 = (bf16[3,48,1280]{2,1,0:T(8,128)(2,1)S(1)}, bf16[3,48,1280]{2,1,0:T(8,128)(2,1)S(1)}, u32[]{:S(2)}, u32[]{:S(2)}) collective-permute-start(bf16[3,48,1280]{2,1,0:T(8,128)(2,1)S(1)} %collective-permute-done.12.refs_9_.refs_20_), channel_id=1, source_target_pairs={{0,1},{1,0},{2,3},{3,2},{4,5},{5,4},{6,7},{7,6},{8,9},{9,8},{10,11... | collective-permute-start | bytes 1105928 | tf_op jit(solution)/shard_map/ppermute | solution.py:408
  55.7 2.0 %collective-permute-start.16 = (bf16[2,48,1280]{2,1,0:T(8,128)(2,1)S(1)}, bf16[2,48,1280]{2,1,0:T(8,128)(2,1)S(1)}, u32[]{:S(2)}, u32[]{:S(2)}) collective-permute-start(bf16[2,48,1280]{2,1,0:T(8,128)(2,1)S(1)} %collective-permute-done.8.refs_5_.refs_6_.refs_16_), channel_id=1, source_target_pairs={{0,1},{1,0},{2,3},{3,2},{4,5},{5,4},{6,7},{7,6},{8,9},{9,8},{10,11... | collective-permute-start | bytes 737288 | tf_op jit(solution)/shard_map/ppermute | solution.py:408
  57.8 12.1 %collective-permute-start.21 = (bf16[3,48,1280]{2,1,0:T(8,128)(2,1)S(1)}, bf16[3,48,1280]{2,1,0:T(8,128)(2,1)S(1)}, u32[]{:S(2)}, u32[]{:S(2)}) collective-permute-start(bf16[3,48,1280]{2,1,0:T(8,128)(2,1)S(1)} %pad_maximum_fusion.6.refs_7_), channel_id=1, source_target_pairs={{0,16},{16,0},{1,17},{17,1},{2,18},{18,2},{3,19},{19,3},{4,20},{20... | collective-permute-start | bytes 1105928 | tf_op jit(solution)/shard_map/ppermute | solution.py:411
  59.2 16.6 %collective-permute-start.22 = (bf16[3,48,1280]{2,1,0:T(8,128)(2,1)S(1)}, bf16[3,48,1280]{2,1,0:T(8,128)(2,1)S(1)}, u32[]{:S(2)}, u32[]{:S(2)}) collective-permute-start(bf16[3,48,1280]{2,1,0:T(8,128)(2,1)S(1)} %pad_maximum_fusion.6.refs_7_), channel_id=1, source_target_pairs={{0,2},{2,0},{4,6},{6,4},{8,10},{10,8},{12,14},{14,12},{1,3},{3,1},... | collective-permute-start | bytes 1105928 | tf_op jit(solution)/shard_map/ppermute | solution.py:414
  60.1 17.4 %collective-permute-start.23 = (bf16[3,48,1280]{2,1,0:T(8,128)(2,1)S(1)}, bf16[3,48,1280]{2,1,0:T(8,128)(2,1)S(1)}, u32[]{:S(2)}, u32[]{:S(2)}) collective-permute-start(bf16[3,48,1280]{2,1,0:T(8,128)(2,1)S(1)} %pad_maximum_fusion.6.refs_7_), channel_id=1, source_target_pairs={{0,18},{2,16},{4,22},{6,20},{8,26},{10,24},{12,30},{14,28},{16,2},... | collective-permute-start | bytes 1105928 | tf_op jit(solution)/shard_map/ppermute | solution.py:417
  77.5 1.7 collective-permute-start.24
  77.5 2.2 %collective-permute-start.25 = (bf16[3,48,1280]{2,1,0:T(8,128)(2,1)S(1)}, bf16[3,48,1280]{2,1,0:T(8,128)(2,1)S(1)}, u32[]{:S(2)}, u32[]{:S(2)}) collective-permute-start(bf16[3,48,1280]{2,1,0:T(8,128)(2,1)S(1)} %collective-permute-done.21.refs_8_), channel_id=1, source_target_pairs={{0,1},{1,0},{2,3},{3,2},{4,5},{5,4},{6,7},{7,6},{8,9},{9,8},{10,11... | collective-permute-start | bytes 1105928 | tf_op jit(solution)/shard_map/ppermute | solution.py:408
  78.0 2.2 %collective-permute-start.26 = (bf16[3,48,1280]{2,1,0:T(8,128)(2,1)S(1)}, bf16[3,48,1280]{2,1,0:T(8,128)(2,1)S(1)}, u32[]{:S(2)}, u32[]{:S(2)}) collective-permute-start(bf16[3,48,1280]{2,1,0:T(8,128)(2,1)S(1)} %collective-permute-done.22.refs_9_), channel_id=1, source_target_pairs={{0,1},{1,0},{2,3},{3,2},{4,5},{5,4},{6,7},{7,6},{8,9},{9,8},{10,11... | collective-permute-start | bytes 1105928 | tf_op jit(solution)/shard_map/ppermute | solution.py:408
  78.0 2.8 %collective-permute-start.27 = (bf16[3,48,1280]{2,1,0:T(8,128)(2,1)S(1)}, bf16[3,48,1280]{2,1,0:T(8,128)(2,1)S(1)}, u32[]{:S(2)}, u32[]{:S(2)}) collective-permute-start(bf16[3,48,1280]{2,1,0:T(8,128)(2,1)S(1)} %collective-permute-done.23.refs_10_), channel_id=1, source_target_pairs={{0,1},{1,0},{2,3},{3,2},{4,5},{5,4},{6,7},{7,6},{8,9},{9,8},{10,11... | collective-permute-start | bytes 1105928 | tf_op jit(solution)/shard_map/ppermute | solution.py:408
  99.5 4.2 %collective-permute-start.28 = (bf16[2,2,2,4,48,640]{5,4,3,2,1,0:T(8,128)(2,1)S(1)}, bf16[2,2,2,4,48,640]{5,4,3,2,1,0:T(8,128)(2,1)S(1)}, u32[]{:S(2)}, u32[]{:S(2)}) collective-permute-start(bf16[2,2,2,4,48,640]{5,4,3,2,1,0:T(8,128)(2,1)S(1)} %get-tuple-element.147), channel_id=1, source_target_pairs={{0,1},{1,0},{2,3},{3,2},{4,5},{5,4},{6,7},{7,6},{8,9},{9,8},{10,11... | collective-permute-start | bytes 5898248 | tf_op jit(solution)/shard_map/ppermute | solution.py:408
  100.0 10.5 %collective-permute-start.29 = (bf16[416,384]{1,0:T(8,128)(2,1)S(1)}, bf16[416,384]{1,0:T(8,128)(2,1)S(1)}, u32[]{:S(2)}, u32[]{:S(2)}) collective-permute-start(bf16[416,384]{1,0:T(8,128)(2,1)S(1)} %get-tuple-element.164), channel_id=1, source_target_pairs={{0,16},{16,0},{1,17},{17,1},{2,18},{18,2},{3,19},{19,3},{4,20},{20... | collective-permute-start | bytes 958472 | tf_op jit(solution)/shard_map/ppermute | solution.py:411
  104.2 21.3 %collective-permute-start.31 = (bf16[2,4,48,640]{3,2,1,0:T(8,128)(2,1)S(1)}, bf16[2,4,48,640]{3,2,1,0:T(8,128)(2,1)S(1)}, u32[]{:S(2)}, u32[]{:S(2)}) collective-permute-start(bf16[2,4,48,640]{3,2,1,0:T(8,128)(2,1)S(1)} %get-tuple-element.221), channel_id=1, source_target_pairs={{0,16},{16,0},{1,17},{17,1},{2,18},{18,2},{3,19},{19,3},{4,20},{20... | collective-permute-start | bytes 1474568 | tf_op jit(solution)/shard_map/ppermute | solution.py:411
  105.7 19.8 %collective-permute-start.32 = (bf16[2,4,48,640]{3,2,1,0:T(8,128)(2,1)S(1)}, bf16[2,4,48,640]{3,2,1,0:T(8,128)(2,1)S(1)}, u32[]{:S(2)}, u32[]{:S(2)}) collective-permute-start(bf16[2,4,48,640]{3,2,1,0:T(8,128)(2,1)S(1)} %get-tuple-element.220), channel_id=1, source_target_pairs={{0,2},{2,0},{4,6},{6,4},{8,10},{10,8},{12,14},{14,12},{1,3},{3,1},... | collective-permute-start | bytes 1474568 | tf_op jit(solution)/shard_map/ppermute | solution.py:414
  110.9 14.7 %collective-permute-start.30 = (bf16[2,208,384]{2,1,0:T(8,128)(2,1)S(1)}, bf16[2,208,384]{2,1,0:T(8,128)(2,1)S(1)}, u32[]{:S(2)}, u32[]{:S(2)}) collective-permute-start(bf16[2,208,384]{2,1,0:T(8,128)(2,1)S(1)} %pad_maximum_fusion.8), channel_id=1, source_target_pairs={{1,3},{3,5},{5,7},{7,9},{9,11},{11,13},{13,15},{17,19},{19,21},{21... | collective-permute-start | bytes 958472 | tf_op jit(solution)/shard_map/ppermute | solution.py:452
  124.0 10.7 %collective-permute-start.35 = (bf16[416,384]{1,0:T(8,128)(2,1)S(1)}, bf16[416,384]{1,0:T(8,128)(2,1)S(1)}, u32[]{:S(2)}, u32[]{:S(2)}) collective-permute-start(bf16[416,384]{1,0:T(8,128)(2,1)S(1)} %get-tuple-element.179), channel_id=1, source_target_pairs={{0,16},{16,0},{1,17},{17,1},{2,18},{18,2},{3,19},{19,3},{4,20},{20... | collective-permute-start | bytes 958472 | tf_op jit(solution)/shard_map/ppermute | solution.py:411
  125.8 5.9 %collective-permute-start.34 = (bf16[2,512,384]{2,1,0:T(8,128)(2,1)S(1)}, bf16[2,512,384]{2,1,0:T(8,128)(2,1)S(1)}, u32[]{:S(2)}, u32[]{:S(2)}) collective-permute-start(bf16[2,512,384]{2,1,0:T(8,128)(2,1)S(1)} %pad_maximum_fusion.3), channel_id=1, source_target_pairs={{0,1},{1,0},{2,3},{3,2},{4,5},{5,4},{6,7},{7,6},{8,9},{9,8},{10,11... | collective-permute-start | bytes 2359304 | tf_op jit(solution)/shard_map/ppermute | solution.py:408
  127.3 4.7 %collective-permute-start.33 = (bf16[2,2,2,4,48,640]{5,4,3,2,1,0:T(8,128)(2,1)S(1)}, bf16[2,2,2,4,48,640]{5,4,3,2,1,0:T(8,128)(2,1)S(1)}, u32[]{:S(2)}, u32[]{:S(2)}) collective-permute-start(bf16[2,2,2,4,48,640]{5,4,3,2,1,0:T(8,128)(2,1)S(1)} %get-tuple-element.176), channel_id=1, source_target_pairs={{0,1},{1,0},{2,3},{3,2},{4,5},{5,4},{6,7},{7,6},{8,9},{9,8},{10,11... | collective-permute-start | bytes 5898248 | tf_op jit(solution)/shard_map/ppermute | solution.py:408
  127.5 12.2 %collective-permute-start.37 = (bf16[4,48,640]{2,1,0:T(8,128)(2,1)S(1)}, bf16[4,48,640]{2,1,0:T(8,128)(2,1)S(1)}, u32[]{:S(2)}, u32[]{:S(2)}) collective-permute-start(bf16[4,48,640]{2,1,0:T(8,128)(2,1)S(1)} %fusion.18), channel_id=1, source_target_pairs={{0,16},{16,0},{1,17},{17,1},{2,18},{18,2},{3,19},{19,3},{4,20},{20... | collective-permute-start | bytes 737288 | tf_op jit(solution)/shard_map/ppermute | solution.py:411
  128.2 11.5 %collective-permute-start.36 = (bf16[4,48,640]{2,1,0:T(8,128)(2,1)S(1)}, bf16[4,48,640]{2,1,0:T(8,128)(2,1)S(1)}, u32[]{:S(2)}, u32[]{:S(2)}) collective-permute-start(bf16[4,48,640]{2,1,0:T(8,128)(2,1)S(1)} %fusion.17), channel_id=1, source_target_pairs={{0,2},{2,0},{4,6},{6,4},{8,10},{10,8},{12,14},{14,12},{1,3},{3,1},... | collective-permute-start | bytes 737288 | tf_op jit(solution)/shard_map/ppermute | solution.py:414
  132.5 23.6 %collective-permute-start.42 = (bf16[2,4,48,640]{3,2,1,0:T(8,128)(2,1)S(1)}, bf16[2,4,48,640]{3,2,1,0:T(8,128)(2,1)S(1)}, u32[]{:S(2)}, u32[]{:S(2)}) collective-permute-start(bf16[2,4,48,640]{3,2,1,0:T(8,128)(2,1)S(1)} %get-tuple-element.217), channel_id=1, source_target_pairs={{0,16},{16,0},{1,17},{17,1},{2,18},{18,2},{3,19},{19,3},{4,20},{20... | collective-permute-start | bytes 1474568 | tf_op jit(solution)/shard_map/ppermute | solution.py:411
  133.4 22.7 %collective-permute-start.43 = (bf16[2,4,48,640]{3,2,1,0:T(8,128)(2,1)S(1)}, bf16[2,4,48,640]{3,2,1,0:T(8,128)(2,1)S(1)}, u32[]{:S(2)}, u32[]{:S(2)}) collective-permute-start(bf16[2,4,48,640]{3,2,1,0:T(8,128)(2,1)S(1)} %get-tuple-element.216), channel_id=1, source_target_pairs={{0,2},{2,0},{4,6},{6,4},{8,10},{10,8},{12,14},{14,12},{1,3},{3,1},... | collective-permute-start | bytes 1474568 | tf_op jit(solution)/shard_map/ppermute | solution.py:414
  140.9 7.6 %collective-permute-start.40 = (bf16[2,2,48,640]{3,2,0,1:T(8,128)(2,1)S(1)}, bf16[2,2,48,640]{3,2,0,1:T(8,128)(2,1)S(1)}, u32[]{:S(2)}, u32[]{:S(2)}) collective-permute-start(bf16[2,2,48,640]{3,2,0,1:T(8,128)(2,1)S(1)} %slice.227), channel_id=1, source_target_pairs={{0,4},{2,6},{4,0},{6,2},{8,12},{10,14},{12,8},{14,10},{1,5},{3,7},... | collective-permute-start | bytes 737288 | tf_op jit(solution)/shard_map/ppermute | solution.py:440
  141.6 7.5 %collective-permute-start.38 = (bf16[2,208,384]{2,1,0:T(8,128)(2,1)S(1)}, bf16[2,208,384]{2,1,0:T(8,128)(2,1)S(1)}, u32[]{:S(2)}, u32[]{:S(2)}) collective-permute-start(bf16[2,208,384]{2,1,0:T(8,128)(2,1)S(1)} %pad_maximum_fusion.9), channel_id=1, source_target_pairs={{1,3},{3,5},{5,7},{7,9},{9,11},{11,13},{13,15},{17,19},{19,21},{21... | collective-permute-start | bytes 958472 | tf_op jit(solution)/shard_map/ppermute | solution.py:452
  148.5 7.5 %collective-permute-start.41 = (bf16[2,48,640]{2,1,0:T(8,128)(2,1)S(1)}, bf16[2,48,640]{2,1,0:T(8,128)(2,1)S(1)}, u32[]{:S(2)}, u32[]{:S(2)}) collective-permute-start(bf16[2,48,640]{2,1,0:T(8,128)(2,1)S(1)} %fusion.34), channel_id=1, source_target_pairs={{0,8},{2,10},{4,12},{6,14},{8,0},{10,2},{12,4},{14,6},{1,9},{3,11}... | collective-permute-start | bytes 368648 | tf_op jit(solution)/shard_map/ppermute | solution.py:440
  149.3 17.4 %collective-permute-start.39 = (bf16[2,512,384]{2,1,0:T(8,128)(2,1)S(1)}, bf16[2,512,384]{2,1,0:T(8,128)(2,1)S(1)}, u32[]{:S(2)}, u32[]{:S(2)}) collective-permute-start(bf16[2,512,384]{2,1,0:T(8,128)(2,1)S(1)} %pad_maximum_fusion.4), channel_id=1, source_target_pairs={{0,1},{1,0},{2,3},{3,2},{4,5},{5,4},{6,7},{7,6},{8,9},{9,8},{10,11... | collective-permute-start | bytes 2359304 | tf_op jit(solution)/shard_map/ppermute | solution.py:408
  156.2 8.8 %collective-permute-start.45 = (bf16[4,48,640]{2,1,0:T(8,128)(2,1)S(1)}, bf16[4,48,640]{2,1,0:T(8,128)(2,1)S(1)}, u32[]{:S(2)}, u32[]{:S(2)}) collective-permute-start(bf16[4,48,640]{2,1,0:T(8,128)(2,1)S(1)} %fusion.20), channel_id=1, source_target_pairs={{0,16},{16,0},{1,17},{17,1},{2,18},{18,2},{3,19},{19,3},{4,20},{20... | collective-permute-start | bytes 737288 | tf_op jit(solution)/shard_map/ppermute | solution.py:411
  159.1 7.7 %collective-permute-start.44 = (bf16[4,48,640]{2,1,0:T(8,128)(2,1)S(1)}, bf16[4,48,640]{2,1,0:T(8,128)(2,1)S(1)}, u32[]{:S(2)}, u32[]{:S(2)}) collective-permute-start(bf16[4,48,640]{2,1,0:T(8,128)(2,1)S(1)} %fusion.19), channel_id=1, source_target_pairs={{0,2},{2,0},{4,6},{6,4},{8,10},{10,8},{12,14},{14,12},{1,3},{3,1},... | collective-permute-start | bytes 737288 | tf_op jit(solution)/shard_map/ppermute | solution.py:414
  167.0 5.8 %collective-permute-start.46 = (bf16[2,48,640]{2,1,0:T(8,128)(2,1)S(1)}, bf16[2,48,640]{2,1,0:T(8,128)(2,1)S(1)}, u32[]{:S(2)}, u32[]{:S(2)}) collective-permute-start(bf16[2,48,640]{2,1,0:T(8,128)(2,1)S(1)} %get-tuple-element.222), channel_id=1, source_target_pairs={{0,4},{2,6},{4,0},{6,2},{8,12},{10,14},{12,8},{14,10},{1,5},{3,7},... | collective-permute-start | bytes 368648 | tf_op jit(solution)/shard_map/ppermute | solution.py:440
  167.0 11.7 %collective-permute-start.47 = (bf16[2,48,640]{2,1,0:T(8,128)(2,1)S(1)}, bf16[2,48,640]{2,1,0:T(8,128)(2,1)S(1)}, u32[]{:S(2)}, u32[]{:S(2)}) collective-permute-start(bf16[2,48,640]{2,1,0:T(8,128)(2,1)S(1)} %get-tuple-element.224), channel_id=1, source_target_pairs={{0,8},{2,10},{4,12},{6,14},{8,0},{10,2},{12,4},{14,6},{1,9},{3,11}... | collective-permute-start | bytes 368648 | tf_op jit(solution)/shard_map/ppermute | solution.py:440
  169.0 9.7 %collective-permute-start.48 = (bf16[2,48,640]{2,1,0:T(8,128)(2,1)S(1)}, bf16[2,48,640]{2,1,0:T(8,128)(2,1)S(1)}, u32[]{:S(2)}, u32[]{:S(2)}) collective-permute-start(bf16[2,48,640]{2,1,0:T(8,128)(2,1)S(1)} %get-tuple-element.223), channel_id=1, source_target_pairs={{0,12},{2,14},{4,8},{6,10},{8,4},{10,6},{12,0},{14,2},{1,13},{3,15... | collective-permute-start | bytes 368648 | tf_op jit(solution)/shard_map/ppermute | solution.py:440
  178.9 4.9 %collective-permute-start.49 = (bf16[48,1280]{1,0:T(8,128)(2,1)S(1)}, bf16[48,1280]{1,0:T(8,128)(2,1)S(1)}, u32[]{:S(2)}, u32[]{:S(2)}) collective-permute-start(bf16[48,1280]{1,0:T(8,128)(2,1)S(1)} %select_convert_fusion), channel_id=1, source_target_pairs={{0,16},{16,0},{1,17},{17,1},{2,18},{18,2},{3,19},{19,3},{4,20},{20... | collective-permute-start | bytes 368648 | tf_op jit(solution)/shard_map/ppermute | solution.py:411
  183.8 0.7 copy-start.2
where the time goes:
time: 187 us; the launch traced here: 186 us
  waiting for transfers between devices  74.1 us (40%)
  starting transfers between devices  50.2 us (27%)
  Pallas kernels  45.5 us (24%)
  other arithmetic  6.33 us (3%)
  matrix products  4.51 us (2%)
  local copies, waits for them, and re-layouts  3.66 us (2%)
  between operations  2.12 us (1%)
    pallas_call x5, Pallas kernels, layer_call(): pl.pallas_call(body, out_shape=[jax.ShapeDtypeStruct(*o) for o in outs],...  43.6 us
    ppermute x10, waiting for transfers between devices, pz_to(): return lax.ppermute(a, 'dp', [(i, i ^ 2 * kk) for i in range(n_dp)])  28.9 us
    ppermute x11, waiting for transfers between devices, px(): return lax.ppermute(a, 'section', [(0, 1), (1, 0)])  24.4 us
    ppermute x10, starting transfers between devices, pz_to(): return lax.ppermute(a, 'dp', [(i, i ^ 2 * kk) for i in range(n_dp)])  16 us
    ppermute x11, starting transfers between devices, px(): return lax.ppermute(a, 'section', [(0, 1), (1, 0)])  15.5 us
    ppermute x7, waiting for transfers between devices, py(): return lax.ppermute(a, 'dp', [(i, i ^ 1) for i in range(n_dp)])  14.6 us
    ppermute x7, starting transfers between devices, py(): return lax.ppermute(a, 'dp', [(i, i ^ 1) for i in range(n_dp)])  8.36 us
    dot_general x10, matrix products, mm(): return lax.dot_general(a, b, (dims, ((), ())), preferred_element_type=F32)  4.51 us
  transfers between devices with their start and end apart: 50, of which 24 were waited for; matrix products, arithmetic and copies ran while one was open for 6% of the time, Pallas kernels for 13%

commit v1 on v0

--- a/solution.py
+++ b/solution.py
@@ -443,24 +443,23 @@
         low = quad.astype(BF16)
         return plus(quad[:, 0], *[pz_to(low[:, kk], kk) for kk in range(1, m)])
 
-    def along_steps(quad):
+    def along_steps(quad, *before):
         got = pz_to(quad[:, 1::2].astype(BF16), 1)
-        quad = plus(quad[:, 0::2], got)
+        quad = after(plus(quad[:, 0::2], got), *before)[0]
         return plus(quad[:, 0], pz_to(quad[:, 1].astype(BF16), 2))
 
     def pn(a):
         return lax.ppermute(a, ("dp", "tensor"), [(2 * i + 1, 2 * i + 3) for i in range(n_dp - 1)])
 
-    def tails(keep, got):
+    def placed(rows, *before):
         tail = select[:, local_rows:]
-        return pn(jnp.stack([tn(tail, keep), tn(tail, got)]).astype(BF16))
-
-    def placed(keep, got, tail):
+        tails = after(pn(jnp.stack([tn(tail, a) for a in rows]).astype(BF16)), *before)[0]
+
         def place(a, b):
             a = tn(select[:, :local_rows], a).astype(BF16)
             return jnp.concatenate([a[:IMG_PAD] + b, a[IMG_PAD:]], 0)
 
-        return jnp.stack([place(keep, tail[0]), place(got, tail[1])])
+        return jnp.stack([place(a, tails[i]) for i, a in enumerate(rows)])
 
     def ordered(a, b):
         a = a + b
@@ -587,38 +586,32 @@
         first, got1 = after(m1["g"][0], got1)
         sent1 = chip_sums([first] + m1["g"][1:], got1)
         u = after(u, sent1[1], sent1[3])[0]
-        low_got = after(low_got, sent1[1], sent1[3])[0]
-        low_tails = tails(r1["keep"], low_got)
         quad1 = cross_first(sent1)
-    else:
-        low_tails = tails(r1["keep"], low_got)
     b0 = call(0, ["back", "theirs"], **{**r0, "u": u})
     if direct:
-        b0["dg"], b0["g"][0], low_tails, *quad1 = after(b0["dg"], b0["g"][0], low_tails, *quad1)
+        b0["dg"], b0["g"][0], *quad1 = after(b0["dg"], b0["g"][0], *quad1)
         got0 = pt(b0["g"][0])
         quad1 = cross_second(quad1)
-    low_rows = placed(r1["keep"], low_got, low_tails)
-    low_twin = pt(low_rows)
     in_got = px(b0["give"])
     m0 = call(0, ["mine"], **{**r0, **b0})
 
     if direct:
-        first, got0, low_twin = after(m0["g"][0], got0, low_twin)
+        first, got0 = after(m0["g"][0], got0)
         sent0 = chip_sums([first] + m0["g"][1:], got0)
-        in_got, *quad1 = after(in_got, *quad1, sent0[1], sent0[3])[:5]
-        in_tails = tails(b0["keep"], in_got)
-        quad0 = cross_second(after(*cross_first(sent0)))
-        in_rows = placed(b0["keep"], in_got, in_tails)
-        done1 = along_steps(crossed(quad1))
-        in_twin, done1, *quad0 = after(pt(in_rows), done1, *quad0)
-        done0 = along(crossed(quad0))
+        in_got, low_got, *quad1 = after(in_got, low_got, *quad1, sent0[1], sent0[3])[:6]
+        quad0 = after(*cross_first(sent0))
+        rows = placed([r1["keep"], low_got, b0["keep"], in_got], quad0[1], quad0[3])
+        done1 = along_steps(crossed(quad1), quad0[1], quad0[3])
+        quad0 = cross_second(quad0)
+        done1, *quad0 = after(done1, *quad0)
+        twin, done0 = after(pt(rows), along(crossed(quad0)))
         done0, done1 = [jnp.concatenate([a[0], a[1]], 1) for a in (done0, done1)]
         mine = jnp.where(sec == 0, done0, done1)
         other = px(jnp.where(sec == 0, done1, done0).astype(BF16))
         g_gain, g_bias, g_qkv, g_qv, g_out, g_up, g_up_bias, g_down = finish(scalars, mine, other, ff // 2)
     else:
-        in_rows = placed(b0["keep"], in_got, tails(b0["keep"], in_got))
-        in_twin = pt(in_rows)
+        rows = placed([r1["keep"], low_got, b0["keep"], in_got])
+        twin = pt(rows)
 
         def by_core(a, b):
             return jnp.where(ten == 0, jnp.stack([b, a]), jnp.stack([a, b]))
@@ -633,8 +626,8 @@
         small = jnp.pad(small, ((0, 0), (MISC, HALF - MLP)))
         _, _, _, g_qv, _, _, g_up_bias, _ = parts(small, small, ff // 2)
 
-    layer_outputs = ordered(low_rows, low_twin)
-    input_grads = ordered(in_rows, in_twin).astype(F32)
+    layer_outputs = ordered(rows[:2], twin[:2])
+    input_grads = ordered(rows[2:], twin[2:]).astype(F32)
 
     return (
         layer_outputs,

time: 187 us -> 175 us (0.936)
  waiting for transfers between devices: 74.1 us -> 59.1 us
  starting transfers between devices: 50.2 us -> 52.7 us
    ppermute x11, waiting for transfers between devices: 24.4 us -> 13.6 us  [px(): return lax.ppermute(a, 'section', [(0, 1), (1, 0)])]
    ppermute x10, starting transfers between devices: 16 us -> 19.7 us  [pz_to(): return lax.ppermute(a, 'dp', [(i, i ^ 2 * kk) for i in range(n_dp)])]
    ppermute x10, waiting for transfers between devices: 28.9 us -> 26.6 us  [pz_to(): return lax.ppermute(a, 'dp', [(i, i ^ 2 * kk) for i in range(n_dp)])]
    ppermute x16 -> x15, starting transfers between devices: 3.97 us -> 2.51 us  [pt(): return lax.ppermute(a, 'tensor', [(0, 1), (1, 0)])]
    ppermute x16 -> x15, waiting for transfers between devices: 3.84 us -> 3.61 us  [pt(): return lax.ppermute(a, 'tensor', [(0, 1), (1, 0)])]
  transfers between devices with their start and end apart: 50 -> 48, of which waited for: 24 -> 23; matrix products, arithmetic and copies ran while one was open for 6% -> 7% of each run, Pallas kernels for 13% -> 14%
where the time goes in v1:
time: 175 us
  waiting for transfers between devices  59.1 us (34%)
  starting transfers between devices  52.7 us (30%)
  Pallas kernels  45.4 us (26%)
  other arithmetic  6.4 us (4%)
  local copies, waits for them, and re-layouts  4.51 us (3%)
  matrix products  4.5 us (3%)
  between operations  2.09 us (1%)
    pallas_call x5, Pallas kernels, layer_call(): pl.pallas_call(body, out_shape=[jax.ShapeDtypeStruct(*o) for o in outs],...  43.5 us
    ppermute x10, waiting for transfers between devices, pz_to(): return lax.ppermute(a, 'dp', [(i, i ^ 2 * kk) for i in range(n_dp)])  26.6 us
    ppermute x10, starting transfers between devices, pz_to(): return lax.ppermute(a, 'dp', [(i, i ^ 2 * kk) for i in range(n_dp)])  19.7 us
    ppermute x11, starting transfers between devices, px(): return lax.ppermute(a, 'section', [(0, 1), (1, 0)])  14.9 us
    ppermute x11, waiting for transfers between devices, px(): return lax.ppermute(a, 'section', [(0, 1), (1, 0)])  13.6 us
    ppermute x7, waiting for transfers between devices, py(): return lax.ppermute(a, 'dp', [(i, i ^ 1) for i in range(n_dp)])  12.9 us
    ppermute x7, starting transfers between devices, py(): return lax.ppermute(a, 'dp', [(i, i ^ 1) for i in range(n_dp)])  9.88 us
    dot_general x10, matrix products, mm(): return lax.dot_general(a, b, (dims, ((), ())), preferred_element_type=F32)  4.5 us
  transfers between devices with their start and end apart: 48, of which 23 were waited for; matrix products, arithmetic and copies ran while one was open for 7% of the time, Pallas kernels for 14%

profile of v1, /device:TPU:0, one launch (start us, length us, event | category | flops | bytes accessed | tf_op | source)
XLA Modules:
  0.0 174.7 jit_solution(14504022783216862223)
XLA Ops:
  0.7 1.3 constant_dynamic-slice_fusion
  2.1 0.7 collective-permute-start.1
  3.5 3.0 %collective-permute-start = (bf16[48,1280]{1,0:T(8,128)(2,1)S(1)}, bf16[48,1280]{1,0:T(8,128)(2,1)S(1)}, u32[]{:S(2)}, u32[]{:S(2)}) collective-permute-start(bf16[48,1280]{1,0:T(8,128)(2,1)S(1)} %broadcast_select_fusion.3), channel_id=1, source_target_pairs={{0,16},{16,0},{1,17},{17,1},{2,18},{18,2},{3,19},{19,3},{4,20},{20... | collective-permute-start | bytes 368648 | tf_op jit(solution)/shard_map/ppermute | solution.py:411
  6.5 3.9 %collective-permute-done = bf16[48,1280]{1,0:T(8,128)(2,1)S(1)} collective-permute-done((bf16[48,1280]{1,0:T(8,128)(2,1)S(1)}, bf16[48,1280]{1,0:T(8,128)(2,1)S(1)}, u32[]{:S(2)}, u32[]{:S(2)}) %collective-permute-start) | collective-permute-done | bytes 122912 | tf_op jit(solution)/shard_map/ppermute | solution.py:411
  10.5 1.2 collective-permute-start.2
  11.7 2.6 %collective-permute-start.3 = (bf16[48,1280]{1,0:T(8,128)(2,1)S(1)}, bf16[48,1280]{1,0:T(8,128)(2,1)S(1)}, u32[]{:S(2)}, u32[]{:S(2)}) collective-permute-start(bf16[48,1280]{1,0:T(8,128)(2,1)S(1)} %get-tuple-element.234), channel_id=1, source_target_pairs={{0,8},{2,10},{4,12},{6,14},{8,0},{10,2},{12,4},{14,6},{1,9},{3,11}... | collective-permute-start | bytes 368648 | tf_op jit(solution)/shard_map/ppermute | solution.py:440
  14.3 0.7 collective-permute-start.4
  15.0 1.8 %collective-permute-start.6 = (bf16[2,48,1280]{2,1,0:T(8,128)(2,1)S(1)}, bf16[2,48,1280]{2,1,0:T(8,128)(2,1)S(1)}, u32[]{:S(2)}, u32[]{:S(2)}) collective-permute-start(bf16[2,48,1280]{2,1,0:T(8,128)(2,1)S(1)} %pad_maximum_fusion.8.refs_2_.refs_3_.refs_13_), channel_id=1, source_target_pairs={{0,16},{16,0},{1,17},{17,1},{2,18},{18,2},{3,19},{19,3},{4,20},{20... | collective-permute-start | bytes 737288 | tf_op jit(solution)/shard_map/ppermute | solution.py:411
  16.8 1.7 collective-permute-start.7
  18.6 3.1 %collective-permute-start.8 = (bf16[2,48,1280]{2,1,0:T(8,128)(2,1)S(1)}, bf16[2,48,1280]{2,1,0:T(8,128)(2,1)S(1)}, u32[]{:S(2)}, u32[]{:S(2)}) collective-permute-start(bf16[2,48,1280]{2,1,0:T(8,128)(2,1)S(1)} %pad_maximum_fusion.8.refs_2_.refs_3_.refs_13_), channel_id=1, source_target_pairs={{0,18},{2,16},{4,22},{6,20},{8,26},{10,24},{12,30},{14,28},{16,2},... | collective-permute-start | bytes 737288 | tf_op jit(solution)/shard_map/ppermute | solution.py:417
  21.7 2.4 %collective-permute-done.3 = bf16[48,1280]{1,0:T(8,128)(2,1)S(1)} collective-permute-done((bf16[48,1280]{1,0:T(8,128)(2,1)S(1)}, bf16[48,1280]{1,0:T(8,128)(2,1)S(1)}, u32[]{:S(2)}, u32[]{:S(2)}) %collective-permute-start.3) | collective-permute-done | bytes 122912 | tf_op jit(solution)/shard_map/ppermute | solution.py:440
  24.1 3.1 %collective-permute-start.5 = (bf16[48,1280]{1,0:T(8,128)(2,1)S(1)}, bf16[48,1280]{1,0:T(8,128)(2,1)S(1)}, u32[]{:S(2)}, u32[]{:S(2)}) collective-permute-start(bf16[48,1280]{1,0:T(8,128)(2,1)S(1)} %get-tuple-element.115), channel_id=1, source_target_pairs={{0,4},{2,6},{4,0},{6,2},{8,12},{10,14},{12,8},{14,10},{1,5},{3,7},... | collective-permute-start | bytes 368648 | tf_op jit(solution)/shard_map/ppermute | solution.py:440
  27.3 3.5 %collective-permute-done.5 = bf16[48,1280]{1,0:T(8,128)(2,1)S(1)} collective-permute-done((bf16[48,1280]{1,0:T(8,128)(2,1)S(1)}, bf16[48,1280]{1,0:T(8,128)(2,1)S(1)}, u32[]{:S(2)}, u32[]{:S(2)}) %collective-permute-start.5) | collective-permute-done | bytes 122912 | tf_op jit(solution)/shard_map/ppermute | solution.py:440
  30.8 2.8 %collective-permute-start.9 = (bf16[2,48,1280]{2,1,0:T(8,128)(2,1)S(1)}, bf16[2,48,1280]{2,1,0:T(8,128)(2,1)S(1)}, u32[]{:S(2)}, u32[]{:S(2)}) collective-permute-start(bf16[2,48,1280]{2,1,0:T(8,128)(2,1)S(1)} %pad_maximum_fusion.9), channel_id=1, source_target_pairs={{0,8},{2,10},{4,12},{6,14},{8,0},{10,2},{12,4},{14,6},{1,9},{3,11}... | collective-permute-start | bytes 737288 | tf_op jit(solution)/shard_map/ppermute | solution.py:440
  33.6 0.6 dynamic_slice.11
  35.0 1.6 collective-permute-start.10
  36.5 2.4 %collective-permute-start.11 = (bf16[3,48,1280]{2,1,0:T(8,128)(2,1)S(1)}, bf16[3,48,1280]{2,1,0:T(8,128)(2,1)S(1)}, u32[]{:S(2)}, u32[]{:S(2)}) collective-permute-start(bf16[3,48,1280]{2,1,0:T(8,128)(2,1)S(1)} %pad_maximum_fusion.5.refs_6_.refs_17_), channel_id=1, source_target_pairs={{0,2},{2,0},{4,6},{6,4},{8,10},{10,8},{12,14},{14,12},{1,3},{3,1},... | collective-permute-start | bytes 1105928 | tf_op jit(solution)/shard_map/ppermute | solution.py:414
  38.9 5.3 %collective-permute-done.9 = bf16[2,48,1280]{2,1,0:T(8,128)(2,1)S(1)} collective-permute-done((bf16[2,48,1280]{2,1,0:T(8,128)(2,1)S(1)}, bf16[2,48,1280]{2,1,0:T(8,128)(2,1)S(1)}, u32[]{:S(2)}, u32[]{:S(2)}) %collective-permute-start.9) | collective-permute-done | bytes 245792 | tf_op jit(solution)/shard_map/ppermute | solution.py:440
  44.4 2.1 %collective-permute-done.10.refs_7_.refs_18_ = bf16[3,48,1280]{2,1,0:T(8,128)(2,1)S(1)} collective-permute-done((bf16[3,48,1280]{2,1,0:T(8,128)(2,1)S(1)}, bf16[3,48,1280]{2,1,0:T(8,128)(2,1)S(1)}, u32[]{:S(2)}, u32[]{:S(2)}) %collective-permute-start.10) | collective-permute-done | bytes 368672 | tf_op jit(solution)/shard_map/ppermute | solution.py:411
  46.5 6.9 %collective-permute-done.11.refs_8_.refs_19_ = bf16[3,48,1280]{2,1,0:T(8,128)(2,1)S(1)} collective-permute-done((bf16[3,48,1280]{2,1,0:T(8,128)(2,1)S(1)}, bf16[3,48,1280]{2,1,0:T(8,128)(2,1)S(1)}, u32[]{:S(2)}, u32[]{:S(2)}) %collective-permute-start.11) | collective-permute-done | bytes 368672 | tf_op jit(solution)/shard_map/ppermute | solution.py:414
  53.4 0.7 collective-permute-done.12.refs_9_.refs_20_
  55.9 0.5 convolution_convert_fusion.5.refs_1_
  56.4 1.3 collective-permute-done.16.refs_13_.refs_14_.refs_24_
  57.8 1.5 collective-permute-start.21
  59.2 0.8 collective-permute-start.22
  60.1 1.2 collective-permute-start.23
  61.3 8.6 %shard_map.186 = (bf16[416,384]{1,0:T(8,128)(2,1)S(1)}, f32[416,384]{1,0:T(8,128)S(1)}, f32[416,128]{1,0:T(8,128)S(1)}, bf16[416,384]{1,0:T(8,128)(2,1)S(1)}, bf...) custom-call(s32[5]{0:T(128)S(1)} %stack.113.refs_0_.sc, ...), custom_call_target="tpu_custom_call" | custom-call | flops 10000000000 | bytes 8388608 | tf_op jit(solution)/shard_map/pallas_call | solution.py:342
  69.9 6.0 %collective-permute-done.22.refs_9_ = bf16[3,48,1280]{2,1,0:T(8,128)(2,1)S(1)} collective-permute-done((bf16[3,48,1280]{2,1,0:T(8,128)(2,1)S(1)}, bf16[3,48,1280]{2,1,0:T(8,128)(2,1)S(1)}, u32[]{:S(2)}, u32[]{:S(2)}) %collective-permute-start.22) | collective-permute-done | bytes 368672 | tf_op jit(solution)/shard_map/ppermute | solution.py:414
  75.9 1.6 collective-permute-done.23.refs_10_
  78.5 0.7 collective-permute-done.24.refs_15_
  80.8 18.7 %shard_map.187 = (bf16[416,384]{1,0:T(8,128)(2,1)S(1)}, bf16[2,416,256]{2,1,0:T(8,128)(2,1)S(1)}, bf16[416,384]{1,0:T(8,128)(2,1)S(1)}, bf16[416,1536]{1,0:T(8,1...) custom-call(s32[5]{0:T(128)S(1)} %stack.113.refs_0_.sc, ...), custom_call_target="tpu_custom_call" | custom-call | flops 30000001024 | bytes 8388608 | tf_op jit(solution)/shard_map/pallas_call | solution.py:342
  100.0 0.6 collective-permute-start.30
  101.5 2.2 %shard_map.188 = (bf16[2,4,48,640]{3,2,1,0:T(8,128)(2,1)S(1)}, bf16[2,4,48,640]{3,2,1,0:T(8,128)(2,1)S(1)}, bf16[2,4,48,640]{3,2,1,0:T(8,128)(2,1)S(1)}, bf16[2,4,48,640]{3,2,1,0:T(8,128)(2,1)S(1)}) custom-call(s32[5]{0:T(128)S(1)} %stack.113.refs_0_.sc, bf16[416,384]{1,0:T(8,128)(2,1)S(1)} %get-tuple-element.136.refs_1_, ...), custom_call_target="tpu_custom_call" | custom-call | flops 10000000000 | bytes 8388608 | tf_op jit(solution)/shard_map/pallas_call | solution.py:342
  104.2 1.5 collective-permute-start.31
  105.8 0.8 collective-permute-start.32
  106.6 11.8 %shard_map.189 = (bf16[416,384]{1,0:T(8,128)(2,1)S(1)}, bf16[416,384]{1,0:T(8,128)(2,1)S(1)}, bf16[416,384]{1,0:T(8,128)(2,1)S(1)}, bf16[416,1536]{1,0:T(8,128)(...) custom-call(s32[5]{0:T(128)S(1)} %stack.113.refs_0_.sc, ...), custom_call_target="tpu_custom_call" | custom-call | flops 20000000000 | bytes 8388608 | tf_op jit(solution)/shard_map/pallas_call | solution.py:342
  118.4 1.5 collective-permute-start.29
  121.1 0.6 collective-permute-start.34
  121.8 1.7 collective-permute-start.33
  123.6 2.2 %shard_map.190 = (bf16[2,4,48,640]{3,2,1,0:T(8,128)(2,1)S(1)}, bf16[2,4,48,640]{3,2,1,0:T(8,128)(2,1)S(1)}, bf16[2,4,48,640]{3,2,1,0:T(8,128)(2,1)S(1)}, bf16[2,4,48,640]{3,2,1,0:T(8,128)(2,1)S(1)}) custom-call(s32[5]{0:T(128)S(1)} %stack.113.refs_0_.sc, bf16[416,384]{1,0:T(8,128)(2,1)S(1)} %get-tuple-element.154.refs_4_.refs_1_, ...), custom_call_target="tpu_custom_call" | custom-call | flops 10000000000 | bytes 8388608 | tf_op jit(solution)/shard_map/pallas_call | solution.py:342
  126.5 1.7 collective-permute-start.38
  128.2 0.7 collective-permute-done.29
  128.9 5.3 %collective-permute-done.34 = bf16[4,48,640]{2,1,0:T(8,128)(2,1)S(1)} collective-permute-done((bf16[4,48,640]{2,1,0:T(8,128)(2,1)S(1)}, bf16[4,48,640]{2,1,0:T(8,128)(2,1)S(1)}, u32[]{:S(2)}, u32[]{:S(2)}) %collective-permute-start.34) | collective-permute-done | bytes 245792 | tf_op jit(solution)/shard_map/ppermute | solution.py:411
  136.1 0.6 collective-permute-start.40
  136.8 0.7 collective-permute-start.36
  137.7 4.7 %collective-permute-done.40 = bf16[2,2,48,640]{3,2,0,1:T(8,128)(2,1)S(1)} collective-permute-done((bf16[2,2,48,640]{3,2,0,1:T(8,128)(2,1)S(1)}, bf16[2,2,48,640]{3,2,0,1:T(8,128)(2,1)S(1)}, u32[]{:S(2)}, u32[]{:S(2)}) %collective-permute-start.40) | collective-permute-done | bytes 245792 | tf_op jit(solution)/shard_map/ppermute | solution.py:440
  142.4 0.8 collective-permute-done.37
  143.4 1.6 collective-permute-start.43
  145.1 0.7 collective-permute-start.42
  145.8 4.2 %collective-permute-start.41 = (bf16[2,48,640]{2,1,0:T(8,128)(2,1)S(1)}, bf16[2,48,640]{2,1,0:T(8,128)(2,1)S(1)}, u32[]{:S(2)}, u32[]{:S(2)}) collective-permute-start(bf16[2,48,640]{2,1,0:T(8,128)(2,1)S(1)} %fusion.31), channel_id=1, source_target_pairs={{0,8},{2,10},{4,12},{6,14},{8,0},{10,2},{12,4},{14,6},{1,9},{3,11}... | collective-permute-start | bytes 368648 | tf_op jit(solution)/shard_map/ppermute | solution.py:440
  150.4 0.8 slice-done
  151.7 2.2 %collective-permute-done.41 = bf16[2,48,640]{2,1,0:T(8,128)(2,1)S(1)} collective-permute-done((bf16[2,48,640]{2,1,0:T(8,128)(2,1)S(1)}, bf16[2,48,640]{2,1,0:T(8,128)(2,1)S(1)}, u32[]{:S(2)}, u32[]{:S(2)}) %collective-permute-start.41) | collective-permute-done | bytes 122912 | tf_op jit(solution)/shard_map/ppermute | solution.py:440
  154.1 1.5 collective-permute-start.44
  155.7 0.8 collective-permute-start.45
  156.5 2.1 %collective-permute-start.46 = (bf16[2,48,640]{2,1,0:T(8,128)(2,1)S(1)}, bf16[2,48,640]{2,1,0:T(8,128)(2,1)S(1)}, u32[]{:S(2)}, u32[]{:S(2)}) collective-permute-start(bf16[2,48,640]{2,1,0:T(8,128)(2,1)S(1)} %get-tuple-element.231), channel_id=1, source_target_pairs={{0,12},{2,14},{4,8},{6,10},{8,4},{10,6},{12,0},{14,2},{1,13},{3,15... | collective-permute-start | bytes 368648 | tf_op jit(solution)/shard_map/ppermute | solution.py:440
  158.6 0.8 collective-permute-done.44
  159.4 7.7 %collective-permute-done.45 = bf16[2,48,640]{2,1,0:T(8,128)(2,1)S(1)} collective-permute-done((bf16[2,48,640]{2,1,0:T(8,128)(2,1)S(1)}, bf16[2,48,640]{2,1,0:T(8,128)(2,1)S(1)}, u32[]{:S(2)}, u32[]{:S(2)}) %collective-permute-start.45) | collective-permute-done | bytes 122912 | tf_op jit(solution)/shard_map/ppermute | solution.py:440
  167.2 0.9 collective-permute-start.47
  168.4 1.2 fusion.12
  169.6 1.0 fusion.10
  170.6 0.7 fusion.26.mine_ref
  171.4 0.8 collective-permute-done.47.other_ref
  172.2 0.6 copy-done.4
  172.8 1.9 %shard_map.191 = (f32[2,48]{1,0:T(2,128)}, f32[4,48]{1,0:T(4,128)}, f32[3,48,192]{2,1,0:T(8,128)}, f32[2,192]{1,0:T(2,128)}, f32[48,192]{1,0:T(8,128)}, /*index=...) custom-call(s32[5]{0:T(128)} %copy-done, f32[48,1280]{1,0:T(8,128)} %fusion.26.mine_ref, bf16[48,1280]{1,0:T(8,128)(2,1)} %copy-done.4), custom_call_target="tpu_custom_call" | custom-call | tf_op jit(solution)/shard_map/pallas_call | solution.py:385
  (149 shorter events, 13.1 us)
Async XLA Ops:
  0.7 2.1 %copy-start.7 = (bf16[1,192,48]{1,2,0:T(8,128)(2,1)S(1)}, bf16[1,192,48]{1,2,0:T(8,128)(2,1)}, u32[]{:S(2)}) copy-start(bf16[1,192,48]{1,2,0:T(8,128)(2,1)} %param.18) | copy-start | bytes 55300
  0.7 2.1 %copy-start.3 = (bf16[1,48,3,192]{3,1,2,0:T(8,128)(2,1)S(1)}, bf16[1,48,3,192]{3,1,2,0:T(8,128)(2,1)}, u32[]{:S(2)}) copy-start(bf16[1,48,3,192]{3,1,2,0:T(8,128)(2,1)} %param.16) | copy-start | bytes 165892
  0.7 2.2 %copy-start.10 = (bf16[1,4,48]{2,1,0:T(4,128)(2,1)S(1)}, bf16[1,4,48]{2,1,0:T(4,128)(2,1)}, u32[]{:S(2)}) copy-start(bf16[1,4,48]{2,1,0:T(4,128)(2,1)} %param.15) | copy-start | bytes 1156
  0.7 2.2 %copy-start.11 = (bf16[1,2,48]{2,1,0:T(2,128)(2,1)S(1)}, bf16[1,2,48]{2,1,0:T(2,128)(2,1)}, u32[]{:S(2)}) copy-start(bf16[1,2,48]{2,1,0:T(2,128)(2,1)} %param.14) | copy-start | bytes 580
  0.7 2.3 %copy-start.8 = (bf16[1,2,192]{2,1,0:T(2,128)(2,1)S(1)}, bf16[1,2,192]{2,1,0:T(2,128)(2,1)}, u32[]{:S(2)}) copy-start(bf16[1,2,192]{2,1,0:T(2,128)(2,1)} %param.17) | copy-start | bytes 2308
  0.7 2.4 %copy-start.9 = (bf16[1,768]{1,0:T(2,128)(2,1)S(1)}, bf16[1,768]{1,0:T(2,128)(2,1)}, u32[]{:S(2)}) copy-start(bf16[1,768]{1,0:T(2,128)(2,1)} %param.20) | copy-start | bytes 4612
  0.7 2.5 %copy-start.5 = (bf16[1,768,48]{1,2,0:T(8,128)(2,1)S(1)}, bf16[1,768,48]{1,2,0:T(8,128)(2,1)}, u32[]{:S(2)}) copy-start(bf16[1,768,48]{1,2,0:T(8,128)(2,1)} %param.21) | copy-start | bytes 221188
  0.7 2.6 %copy-start.6 = (bf16[1,48,768]{2,1,0:T(8,128)(2,1)S(1)}, bf16[1,48,768]{2,1,0:T(8,128)(2,1)}, u32[]{:S(2)}) copy-start(bf16[1,48,768]{2,1,0:T(8,128)(2,1)} %param.19) | copy-start | bytes 221188
  2.1 8.4 %collective-permute-start.1 = (bf16[2,208,384]{2,1,0:T(8,128)(2,1)S(1)}, bf16[2,208,384]{2,1,0:T(8,128)(2,1)S(1)}, u32[]{:S(2)}, u32[]{:S(2)}) collective-permute-start(bf16[2,208,384]{2,1,0:T(8,128)(2,1)S(1)} %pad_maximum_fusion.7), channel_id=1, source_target_pairs={{3,1},{5,3},{7,5},{9,7},{11,9},{13,11},{15,13},{19,17},{21,19},{23... | collective-permute-start | bytes 958472 | tf_op jit(solution)/shard_map/ppermute | solution.py:488
  3.5 30.1 %copy-start.12 = (s32[2]{0:T(128)S(1)}, s32[2]{0:T(128)}, u32[]{:S(2)}) copy-start(s32[2]{0:T(128)} %param.12) | copy-start | bytes 28
  3.5 7.0 %collective-permute-start = (bf16[48,1280]{1,0:T(8,128)(2,1)S(1)}, bf16[48,1280]{1,0:T(8,128)(2,1)S(1)}, u32[]{:S(2)}, u32[]{:S(2)}) collective-permute-start(bf16[48,1280]{1,0:T(8,128)(2,1)S(1)} %broadcast_select_fusion.3), channel_id=1, source_target_pairs={{0,16},{16,0},{1,17},{17,1},{2,18},{18,2},{3,19},{19,3},{4,20},{20... | collective-permute-start | bytes 368648 | tf_op jit(solution)/shard_map/ppermute | solution.py:411
  10.5 8.2 %collective-permute-start.2 = (bf16[48,1280]{1,0:T(8,128)(2,1)S(1)}, bf16[48,1280]{1,0:T(8,128)(2,1)S(1)}, u32[]{:S(2)}, u32[]{:S(2)}) collective-permute-start(bf16[48,1280]{1,0:T(8,128)(2,1)S(1)} %get-tuple-element.234), channel_id=1, source_target_pairs={{0,4},{2,6},{4,0},{6,2},{8,12},{10,14},{12,8},{14,10},{1,5},{3,7},... | collective-permute-start | bytes 368648 | tf_op jit(solution)/shard_map/ppermute | solution.py:440
  11.7 12.4 %collective-permute-start.3 = (bf16[48,1280]{1,0:T(8,128)(2,1)S(1)}, bf16[48,1280]{1,0:T(8,128)(2,1)S(1)}, u32[]{:S(2)}, u32[]{:S(2)}) collective-permute-start(bf16[48,1280]{1,0:T(8,128)(2,1)S(1)} %get-tuple-element.234), channel_id=1, source_target_pairs={{0,8},{2,10},{4,12},{6,14},{8,0},{10,2},{12,4},{14,6},{1,9},{3,11}... | collective-permute-start | bytes 368648 | tf_op jit(solution)/shard_map/ppermute | solution.py:440
  14.3 9.8 %collective-permute-start.4 = (bf16[48,1280]{1,0:T(8,128)(2,1)S(1)}, bf16[48,1280]{1,0:T(8,128)(2,1)S(1)}, u32[]{:S(2)}, u32[]{:S(2)}) collective-permute-start(bf16[48,1280]{1,0:T(8,128)(2,1)S(1)} %get-tuple-element.234), channel_id=1, source_target_pairs={{0,12},{2,14},{4,8},{6,10},{8,4},{10,6},{12,0},{14,2},{1,13},{3,15... | collective-permute-start | bytes 368648 | tf_op jit(solution)/shard_map/ppermute | solution.py:440
  15.0 15.8 %collective-permute-start.6 = (bf16[2,48,1280]{2,1,0:T(8,128)(2,1)S(1)}, bf16[2,48,1280]{2,1,0:T(8,128)(2,1)S(1)}, u32[]{:S(2)}, u32[]{:S(2)}) collective-permute-start(bf16[2,48,1280]{2,1,0:T(8,128)(2,1)S(1)} %pad_maximum_fusion.8.refs_2_.refs_3_.refs_13_), channel_id=1, source_target_pairs={{0,16},{16,0},{1,17},{17,1},{2,18},{18,2},{3,19},{19,3},{4,20},{20... | collective-permute-start | bytes 737288 | tf_op jit(solution)/shard_map/ppermute | solution.py:411
  16.8 14.0 %collective-permute-start.7 = (bf16[2,48,1280]{2,1,0:T(8,128)(2,1)S(1)}, bf16[2,48,1280]{2,1,0:T(8,128)(2,1)S(1)}, u32[]{:S(2)}, u32[]{:S(2)}) collective-permute-start(bf16[2,48,1280]{2,1,0:T(8,128)(2,1)S(1)} %pad_maximum_fusion.8.refs_2_.refs_3_.refs_13_), channel_id=1, source_target_pairs={{0,2},{2,0},{4,6},{6,4},{8,10},{10,8},{12,14},{14,12},{1,3},{3,1},... | collective-permute-start | bytes 737288 | tf_op jit(solution)/shard_map/ppermute | solution.py:414
  18.6 12.1 %collective-permute-start.8 = (bf16[2,48,1280]{2,1,0:T(8,128)(2,1)S(1)}, bf16[2,48,1280]{2,1,0:T(8,128)(2,1)S(1)}, u32[]{:S(2)}, u32[]{:S(2)}) collective-permute-start(bf16[2,48,1280]{2,1,0:T(8,128)(2,1)S(1)} %pad_maximum_fusion.8.refs_2_.refs_3_.refs_13_), channel_id=1, source_target_pairs={{0,18},{2,16},{4,22},{6,20},{8,26},{10,24},{12,30},{14,28},{16,2},... | collective-permute-start | bytes 737288 | tf_op jit(solution)/shard_map/ppermute | solution.py:417
  24.1 6.6 %collective-permute-start.5 = (bf16[48,1280]{1,0:T(8,128)(2,1)S(1)}, bf16[48,1280]{1,0:T(8,128)(2,1)S(1)}, u32[]{:S(2)}, u32[]{:S(2)}) collective-permute-start(bf16[48,1280]{1,0:T(8,128)(2,1)S(1)} %get-tuple-element.115), channel_id=1, source_target_pairs={{0,4},{2,6},{4,0},{6,2},{8,12},{10,14},{12,8},{14,10},{1,5},{3,7},... | collective-permute-start | bytes 368648 | tf_op jit(solution)/shard_map/ppermute | solution.py:440
  30.8 13.5 %collective-permute-start.9 = (bf16[2,48,1280]{2,1,0:T(8,128)(2,1)S(1)}, bf16[2,48,1280]{2,1,0:T(8,128)(2,1)S(1)}, u32[]{:S(2)}, u32[]{:S(2)}) collective-permute-start(bf16[2,48,1280]{2,1,0:T(8,128)(2,1)S(1)} %pad_maximum_fusion.9), channel_id=1, source_target_pairs={{0,8},{2,10},{4,12},{6,14},{8,0},{10,2},{12,4},{14,6},{1,9},{3,11}... | collective-permute-start | bytes 737288 | tf_op jit(solution)/shard_map/ppermute | solution.py:440
  34.9 88.6 %copy-start = (s32[5]{0:T(128)}, s32[5]{0:T(128)S(1)}, u32[]{:S(2)}) copy-start(s32[5]{0:T(128)S(1)} %stack.113.refs_0_.sc) | copy-start | bytes 64
  35.0 11.5 %collective-permute-start.10 = (bf16[3,48,1280]{2,1,0:T(8,128)(2,1)S(1)}, bf16[3,48,1280]{2,1,0:T(8,128)(2,1)S(1)}, u32[]{:S(2)}, u32[]{:S(2)}) collective-permute-start(bf16[3,48,1280]{2,1,0:T(8,128)(2,1)S(1)} %pad_maximum_fusion.5.refs_6_.refs_17_), channel_id=1, source_target_pairs={{0,16},{16,0},{1,17},{17,1},{2,18},{18,2},{3,19},{19,3},{4,20},{20... | collective-permute-start | bytes 1105928 | tf_op jit(solution)/shard_map/ppermute | solution.py:411
  36.5 16.9 %collective-permute-start.11 = (bf16[3,48,1280]{2,1,0:T(8,128)(2,1)S(1)}, bf16[3,48,1280]{2,1,0:T(8,128)(2,1)S(1)}, u32[]{:S(2)}, u32[]{:S(2)}) collective-permute-start(bf16[3,48,1280]{2,1,0:T(8,128)(2,1)S(1)} %pad_maximum_fusion.5.refs_6_.refs_17_), channel_id=1, source_target_pairs={{0,2},{2,0},{4,6},{6,4},{8,10},{10,8},{12,14},{14,12},{1,3},{3,1},... | collective-permute-start | bytes 1105928 | tf_op jit(solution)/shard_map/ppermute | solution.py:414
  38.9 15.2 %collective-permute-start.12 = (bf16[3,48,1280]{2,1,0:T(8,128)(2,1)S(1)}, bf16[3,48,1280]{2,1,0:T(8,128)(2,1)S(1)}, u32[]{:S(2)}, u32[]{:S(2)}) collective-permute-start(bf16[3,48,1280]{2,1,0:T(8,128)(2,1)S(1)} %pad_maximum_fusion.5.refs_6_.refs_17_), channel_id=1, source_target_pairs={{0,18},{2,16},{4,22},{6,20},{8,26},{10,24},{12,30},{14,28},{16,2},... | collective-permute-start | bytes 1105928 | tf_op jit(solution)/shard_map/ppermute | solution.py:417
  38.9 15.7 %collective-permute-start.13 = (bf16[2,48,1280]{2,1,0:T(8,128)(2,1)S(1)}, bf16[2,48,1280]{2,1,0:T(8,128)(2,1)S(1)}, u32[]{:S(2)}, u32[]{:S(2)}) collective-permute-start(bf16[2,48,1280]{2,1,0:T(8,128)(2,1)S(1)} %pad_maximum_fusion.8.refs_2_.refs_3_.refs_13_), channel_id=1, source_target_pairs={{0,1},{1,0},{2,3},{3,2},{4,5},{5,4},{6,7},{7,6},{8,9},{9,8},{10,11... | collective-permute-start | bytes 737288 | tf_op jit(solution)/shard_map/ppermute | solution.py:408
  44.2 10.4 %collective-permute-start.14 = (bf16[2,48,1280]{2,1,0:T(8,128)(2,1)S(1)}, bf16[2,48,1280]{2,1,0:T(8,128)(2,1)S(1)}, u32[]{:S(2)}, u32[]{:S(2)}) collective-permute-start(bf16[2,48,1280]{2,1,0:T(8,128)(2,1)S(1)} %collective-permute-done.6.refs_3_.refs_4_.refs_14_), channel_id=1, source_target_pairs={{0,1},{1,0},{2,3},{3,2},{4,5},{5,4},{6,7},{7,6},{8,9},{9,8},{10,11... | collective-permute-start | bytes 737288 | tf_op jit(solution)/shard_map/ppermute | solution.py:408
  46.5 9.3 %collective-permute-start.15 = (bf16[2,48,1280]{2,1,0:T(8,128)(2,1)S(1)}, bf16[2,48,1280]{2,1,0:T(8,128)(2,1)S(1)}, u32[]{:S(2)}, u32[]{:S(2)}) collective-permute-start(bf16[2,48,1280]{2,1,0:T(8,128)(2,1)S(1)} %collective-permute-done.7.refs_4_.refs_5_.refs_15_), channel_id=1, source_target_pairs={{0,1},{1,0},{2,3},{3,2},{4,5},{5,4},{6,7},{7,6},{8,9},{9,8},{10,11... | collective-permute-start | bytes 737288 | tf_op jit(solution)/shard_map/ppermute | solution.py:408
  54.2 5.1 %collective-permute-start.17 = (bf16[3,48,1280]{2,1,0:T(8,128)(2,1)S(1)}, bf16[3,48,1280]{2,1,0:T(8,128)(2,1)S(1)}, u32[]{:S(2)}, u32[]{:S(2)}) collective-permute-start(bf16[3,48,1280]{2,1,0:T(8,128)(2,1)S(1)} %pad_maximum_fusion.5.refs_6_.refs_17_), channel_id=1, source_target_pairs={{0,1},{1,0},{2,3},{3,2},{4,5},{5,4},{6,7},{7,6},{8,9},{9,8},{10,11... | collective-permute-start | bytes 1105928 | tf_op jit(solution)/shard_map/ppermute | solution.py:408
  54.2 5.9 %collective-permute-start.18 = (bf16[3,48,1280]{2,1,0:T(8,128)(2,1)S(1)}, bf16[3,48,1280]{2,1,0:T(8,128)(2,1)S(1)}, u32[]{:S(2)}, u32[]{:S(2)}) collective-permute-start(bf16[3,48,1280]{2,1,0:T(8,128)(2,1)S(1)} %collective-permute-done.10.refs_7_.refs_18_), channel_id=1, source_target_pairs={{0,1},{1,0},{2,3},{3,2},{4,5},{5,4},{6,7},{7,6},{8,9},{9,8},{10,11... | collective-permute-start | bytes 1105928 | tf_op jit(solution)/shard_map/ppermute | solution.py:408
  54.7 6.6 %collective-permute-start.19 = (bf16[3,48,1280]{2,1,0:T(8,128)(2,1)S(1)}, bf16[3,48,1280]{2,1,0:T(8,128)(2,1)S(1)}, u32[]{:S(2)}, u32[]{:S(2)}) collective-permute-start(bf16[3,48,1280]{2,1,0:T(8,128)(2,1)S(1)} %collective-permute-done.11.refs_8_.refs_19_), channel_id=1, source_target_pairs={{0,1},{1,0},{2,3},{3,2},{4,5},{5,4},{6,7},{7,6},{8,9},{9,8},{10,11... | collective-permute-start | bytes 1105928 | tf_op jit(solution)/shard_map/ppermute | solution.py:408
  54.7 6.6 %collective-permute-start.20 = (bf16[3,48,1280]{2,1,0:T(8,128)(2,1)S(1)}, bf16[3,48,1280]{2,1,0:T(8,128)(2,1)S(1)}, u32[]{:S(2)}, u32[]{:S(2)}) collective-permute-start(bf16[3,48,1280]{2,1,0:T(8,128)(2,1)S(1)} %collective-permute-done.12.refs_9_.refs_20_), channel_id=1, source_target_pairs={{0,1},{1,0},{2,3},{3,2},{4,5},{5,4},{6,7},{7,6},{8,9},{9,8},{10,11... | collective-permute-start | bytes 1105928 | tf_op jit(solution)/shard_map/ppermute | solution.py:408
  55.7 2.0 %collective-permute-start.16 = (bf16[2,48,1280]{2,1,0:T(8,128)(2,1)S(1)}, bf16[2,48,1280]{2,1,0:T(8,128)(2,1)S(1)}, u32[]{:S(2)}, u32[]{:S(2)}) collective-permute-start(bf16[2,48,1280]{2,1,0:T(8,128)(2,1)S(1)} %collective-permute-done.8.refs_5_.refs_6_.refs_16_), channel_id=1, source_target_pairs={{0,1},{1,0},{2,3},{3,2},{4,5},{5,4},{6,7},{7,6},{8,9},{9,8},{10,11... | collective-permute-start | bytes 737288 | tf_op jit(solution)/shard_map/ppermute | solution.py:408
  57.8 12.1 %collective-permute-start.21 = (bf16[3,48,1280]{2,1,0:T(8,128)(2,1)S(1)}, bf16[3,48,1280]{2,1,0:T(8,128)(2,1)S(1)}, u32[]{:S(2)}, u32[]{:S(2)}) collective-permute-start(bf16[3,48,1280]{2,1,0:T(8,128)(2,1)S(1)} %pad_maximum_fusion.6.refs_7_), channel_id=1, source_target_pairs={{0,16},{16,0},{1,17},{17,1},{2,18},{18,2},{3,19},{19,3},{4,20},{20... | collective-permute-start | bytes 1105928 | tf_op jit(solution)/shard_map/ppermute | solution.py:411
  59.2 16.6 %collective-permute-start.22 = (bf16[3,48,1280]{2,1,0:T(8,128)(2,1)S(1)}, bf16[3,48,1280]{2,1,0:T(8,128)(2,1)S(1)}, u32[]{:S(2)}, u32[]{:S(2)}) collective-permute-start(bf16[3,48,1280]{2,1,0:T(8,128)(2,1)S(1)} %pad_maximum_fusion.6.refs_7_), channel_id=1, source_target_pairs={{0,2},{2,0},{4,6},{6,4},{8,10},{10,8},{12,14},{14,12},{1,3},{3,1},... | collective-permute-start | bytes 1105928 | tf_op jit(solution)/shard_map/ppermute | solution.py:414
  60.1 17.4 %collective-permute-start.23 = (bf16[3,48,1280]{2,1,0:T(8,128)(2,1)S(1)}, bf16[3,48,1280]{2,1,0:T(8,128)(2,1)S(1)}, u32[]{:S(2)}, u32[]{:S(2)}) collective-permute-start(bf16[3,48,1280]{2,1,0:T(8,128)(2,1)S(1)} %pad_maximum_fusion.6.refs_7_), channel_id=1, source_target_pairs={{0,18},{2,16},{4,22},{6,20},{8,26},{10,24},{12,30},{14,28},{16,2},... | collective-permute-start | bytes 1105928 | tf_op jit(solution)/shard_map/ppermute | solution.py:417
  77.5 1.7 collective-permute-start.24
  77.5 2.2 %collective-permute-start.25 = (bf16[3,48,1280]{2,1,0:T(8,128)(2,1)S(1)}, bf16[3,48,1280]{2,1,0:T(8,128)(2,1)S(1)}, u32[]{:S(2)}, u32[]{:S(2)}) collective-permute-start(bf16[3,48,1280]{2,1,0:T(8,128)(2,1)S(1)} %collective-permute-done.21.refs_8_), channel_id=1, source_target_pairs={{0,1},{1,0},{2,3},{3,2},{4,5},{5,4},{6,7},{7,6},{8,9},{9,8},{10,11... | collective-permute-start | bytes 1105928 | tf_op jit(solution)/shard_map/ppermute | solution.py:408
  78.0 2.2 %collective-permute-start.26 = (bf16[3,48,1280]{2,1,0:T(8,128)(2,1)S(1)}, bf16[3,48,1280]{2,1,0:T(8,128)(2,1)S(1)}, u32[]{:S(2)}, u32[]{:S(2)}) collective-permute-start(bf16[3,48,1280]{2,1,0:T(8,128)(2,1)S(1)} %collective-permute-done.22.refs_9_), channel_id=1, source_target_pairs={{0,1},{1,0},{2,3},{3,2},{4,5},{5,4},{6,7},{7,6},{8,9},{9,8},{10,11... | collective-permute-start | bytes 1105928 | tf_op jit(solution)/shard_map/ppermute | solution.py:408
  78.0 2.8 %collective-permute-start.27 = (bf16[3,48,1280]{2,1,0:T(8,128)(2,1)S(1)}, bf16[3,48,1280]{2,1,0:T(8,128)(2,1)S(1)}, u32[]{:S(2)}, u32[]{:S(2)}) collective-permute-start(bf16[3,48,1280]{2,1,0:T(8,128)(2,1)S(1)} %collective-permute-done.23.refs_10_), channel_id=1, source_target_pairs={{0,1},{1,0},{2,3},{3,2},{4,5},{5,4},{6,7},{7,6},{8,9},{9,8},{10,11... | collective-permute-start | bytes 1105928 | tf_op jit(solution)/shard_map/ppermute | solution.py:408
  99.5 4.2 %collective-permute-start.28 = (bf16[2,2,2,4,48,640]{5,4,3,2,1,0:T(8,128)(2,1)S(1)}, bf16[2,2,2,4,48,640]{5,4,3,2,1,0:T(8,128)(2,1)S(1)}, u32[]{:S(2)}, u32[]{:S(2)}) collective-permute-start(bf16[2,2,2,4,48,640]{5,4,3,2,1,0:T(8,128)(2,1)S(1)} %get-tuple-element.148), channel_id=1, source_target_pairs={{0,1},{1,0},{2,3},{3,2},{4,5},{5,4},{6,7},{7,6},{8,9},{9,8},{10,11... | collective-permute-start | bytes 5898248 | tf_op jit(solution)/shard_map/ppermute | solution.py:408
  100.0 26.5 %collective-permute-start.30 = (bf16[416,384]{1,0:T(8,128)(2,1)S(1)}, bf16[416,384]{1,0:T(8,128)(2,1)S(1)}, u32[]{:S(2)}, u32[]{:S(2)}) collective-permute-start(bf16[416,384]{1,0:T(8,128)(2,1)S(1)} %get-tuple-element.164), channel_id=1, source_target_pairs={{0,16},{16,0},{1,17},{17,1},{2,18},{18,2},{3,19},{19,3},{4,20},{20... | collective-permute-start | bytes 958472 | tf_op jit(solution)/shard_map/ppermute | solution.py:411
  104.2 16.6 %collective-permute-start.31 = (bf16[2,4,48,640]{3,2,1,0:T(8,128)(2,1)S(1)}, bf16[2,4,48,640]{3,2,1,0:T(8,128)(2,1)S(1)}, u32[]{:S(2)}, u32[]{:S(2)}) collective-permute-start(bf16[2,4,48,640]{3,2,1,0:T(8,128)(2,1)S(1)} %get-tuple-element.223), channel_id=1, source_target_pairs={{0,16},{16,0},{1,17},{17,1},{2,18},{18,2},{3,19},{19,3},{4,20},{20... | collective-permute-start | bytes 1474568 | tf_op jit(solution)/shard_map/ppermute | solution.py:411
  105.8 15.1 %collective-permute-start.32 = (bf16[2,4,48,640]{3,2,1,0:T(8,128)(2,1)S(1)}, bf16[2,4,48,640]{3,2,1,0:T(8,128)(2,1)S(1)}, u32[]{:S(2)}, u32[]{:S(2)}) collective-permute-start(bf16[2,4,48,640]{3,2,1,0:T(8,128)(2,1)S(1)} %get-tuple-element.222), channel_id=1, source_target_pairs={{0,2},{2,0},{4,6},{6,4},{8,10},{10,8},{12,14},{14,12},{1,3},{3,1},... | collective-permute-start | bytes 1474568 | tf_op jit(solution)/shard_map/ppermute | solution.py:414
  118.4 10.5 %collective-permute-start.29 = (bf16[416,384]{1,0:T(8,128)(2,1)S(1)}, bf16[416,384]{1,0:T(8,128)(2,1)S(1)}, u32[]{:S(2)}, u32[]{:S(2)}) collective-permute-start(bf16[416,384]{1,0:T(8,128)(2,1)S(1)} %get-tuple-element.163), channel_id=1, source_target_pairs={{0,16},{16,0},{1,17},{17,1},{2,18},{18,2},{3,19},{19,3},{4,20},{20... | collective-permute-start | bytes 958472 | tf_op jit(solution)/shard_map/ppermute | solution.py:411
  120.4 29.7 %copy-start.1 = (bf16[512,384]{1,0:T(8,128)(2,1)}, bf16[512,384]{1,0:T(8,128)(2,1)S(1)}, u32[]{:S(2)}) copy-start(bf16[512,384]{1,0:T(8,128)(2,1)S(1)} %convolution_convert_fusion.1) | copy-start | bytes 1179652
  120.8 5.0 %collective-permute-start.35 = (bf16[2,2,2,4,48,640]{5,4,3,2,1,0:T(8,128)(2,1)S(1)}, bf16[2,2,2,4,48,640]{5,4,3,2,1,0:T(8,128)(2,1)S(1)}, u32[]{:S(2)}, u32[]{:S(2)}) collective-permute-start(bf16[2,2,2,4,48,640]{5,4,3,2,1,0:T(8,128)(2,1)S(1)} %get-tuple-element.181), channel_id=1, source_target_pairs={{0,1},{1,0},{2,3},{3,2},{4,5},{5,4},{6,7},{7,6},{8,9},{9,8},{10,11... | collective-permute-start | bytes 5898248 | tf_op jit(solution)/shard_map/ppermute | solution.py:408
  121.1 13.1 %collective-permute-start.34 = (bf16[4,48,640]{2,1,0:T(8,128)(2,1)S(1)}, bf16[4,48,640]{2,1,0:T(8,128)(2,1)S(1)}, u32[]{:S(2)}, u32[]{:S(2)}) collective-permute-start(bf16[4,48,640]{2,1,0:T(8,128)(2,1)S(1)} %fusion.18), channel_id=1, source_target_pairs={{0,16},{16,0},{1,17},{17,1},{2,18},{18,2},{3,19},{19,3},{4,20},{20... | collective-permute-start | bytes 737288 | tf_op jit(solution)/shard_map/ppermute | solution.py:411
  121.8 12.3 %collective-permute-start.33 = (bf16[4,48,640]{2,1,0:T(8,128)(2,1)S(1)}, bf16[4,48,640]{2,1,0:T(8,128)(2,1)S(1)}, u32[]{:S(2)}, u32[]{:S(2)}) collective-permute-start(bf16[4,48,640]{2,1,0:T(8,128)(2,1)S(1)} %fusion.17), channel_id=1, source_target_pairs={{0,2},{2,0},{4,6},{6,4},{8,10},{10,8},{12,14},{14,12},{1,3},{3,1},... | collective-permute-start | bytes 737288 | tf_op jit(solution)/shard_map/ppermute | solution.py:414
  126.3 17.0 %collective-permute-start.37 = (bf16[2,4,48,640]{3,2,1,0:T(8,128)(2,1)S(1)}, bf16[2,4,48,640]{3,2,1,0:T(8,128)(2,1)S(1)}, u32[]{:S(2)}, u32[]{:S(2)}) collective-permute-start(bf16[2,4,48,640]{3,2,1,0:T(8,128)(2,1)S(1)} %get-tuple-element.219), channel_id=1, source_target_pairs={{0,16},{16,0},{1,17},{17,1},{2,18},{18,2},{3,19},{19,3},{4,20},{20... | collective-permute-start | bytes 1474568 | tf_op jit(solution)/shard_map/ppermute | solution.py:411
  126.5 16.7 %collective-permute-start.38 = (bf16[2,4,48,640]{3,2,1,0:T(8,128)(2,1)S(1)}, bf16[2,4,48,640]{3,2,1,0:T(8,128)(2,1)S(1)}, u32[]{:S(2)}, u32[]{:S(2)}) collective-permute-start(bf16[2,4,48,640]{3,2,1,0:T(8,128)(2,1)S(1)} %get-tuple-element.218), channel_id=1, source_target_pairs={{0,2},{2,0},{4,6},{6,4},{8,10},{10,8},{12,14},{14,12},{1,3},{3,1},... | collective-permute-start | bytes 1474568 | tf_op jit(solution)/shard_map/ppermute | solution.py:414
  135.9 14.3 %copy-start.2 = (bf16[512,384]{1,0:T(8,128)(2,1)}, bf16[512,384]{1,0:T(8,128)(2,1)S(1)}, u32[]{:S(2)}) copy-start(bf16[512,384]{1,0:T(8,128)(2,1)S(1)} %convolution_convert_fusion) | copy-start | bytes 1179652
  136.1 6.3 %collective-permute-start.40 = (bf16[2,2,48,640]{3,2,0,1:T(8,128)(2,1)S(1)}, bf16[2,2,48,640]{3,2,0,1:T(8,128)(2,1)S(1)}, u32[]{:S(2)}, u32[]{:S(2)}) collective-permute-start(bf16[2,2,48,640]{3,2,0,1:T(8,128)(2,1)S(1)} %slice.238), channel_id=1, source_target_pairs={{0,4},{2,6},{4,0},{6,2},{8,12},{10,14},{12,8},{14,10},{1,5},{3,7},... | collective-permute-start | bytes 737288 | tf_op jit(solution)/shard_map/ppermute | solution.py:440
  136.8 13.3 %collective-permute-start.36 = (bf16[4,208,384]{2,1,0:T(8,128)(2,1)S(1)}, bf16[4,208,384]{2,1,0:T(8,128)(2,1)S(1)}, u32[]{:S(2)}, u32[]{:S(2)}) collective-permute-start(bf16[4,208,384]{2,1,0:T(8,128)(2,1)S(1)} %pad_maximum_fusion.4), channel_id=1, source_target_pairs={{1,3},{3,5},{5,7},{7,9},{9,11},{11,13},{13,15},{17,19},{19,21},{21... | collective-permute-start | bytes 1916936 | tf_op jit(solution)/shard_map/ppermute | solution.py:452
  143.4 10.5 %collective-permute-start.43 = (bf16[4,48,640]{2,1,0:T(8,128)(2,1)S(1)}, bf16[4,48,640]{2,1,0:T(8,128)(2,1)S(1)}, u32[]{:S(2)}, u32[]{:S(2)}) collective-permute-start(bf16[4,48,640]{2,1,0:T(8,128)(2,1)S(1)} %fusion.20), channel_id=1, source_target_pairs={{0,16},{16,0},{1,17},{17,1},{2,18},{18,2},{3,19},{19,3},{4,20},{20... | collective-permute-start | bytes 737288 | tf_op jit(solution)/shard_map/ppermute | solution.py:411
  145.1 8.8 %collective-permute-start.42 = (bf16[4,48,640]{2,1,0:T(8,128)(2,1)S(1)}, bf16[4,48,640]{2,1,0:T(8,128)(2,1)S(1)}, u32[]{:S(2)}, u32[]{:S(2)}) collective-permute-start(bf16[4,48,640]{2,1,0:T(8,128)(2,1)S(1)} %fusion.19), channel_id=1, source_target_pairs={{0,2},{2,0},{4,6},{6,4},{8,10},{10,8},{12,14},{14,12},{1,3},{3,1},... | collective-permute-start | bytes 737288 | tf_op jit(solution)/shard_map/ppermute | solution.py:414
  145.8 8.1 %collective-permute-start.41 = (bf16[2,48,640]{2,1,0:T(8,128)(2,1)S(1)}, bf16[2,48,640]{2,1,0:T(8,128)(2,1)S(1)}, u32[]{:S(2)}, u32[]{:S(2)}) collective-permute-start(bf16[2,48,640]{2,1,0:T(8,128)(2,1)S(1)} %fusion.31), channel_id=1, source_target_pairs={{0,8},{2,10},{4,12},{6,14},{8,0},{10,2},{12,4},{14,6},{1,9},{3,11}... | collective-permute-start | bytes 368648 | tf_op jit(solution)/shard_map/ppermute | solution.py:440
  150.2 0.9 slice-start
  150.3 1.0 slice-start.1
  151.6 15.5 %collective-permute-start.39 = (bf16[4,512,384]{2,1,0:T(8,128)(2,1)S(1)}, bf16[4,512,384]{2,1,0:T(8,128)(2,1)S(1)}, u32[]{:S(2)}, u32[]{:S(2)}) collective-permute-start(bf16[4,512,384]{2,1,0:T(8,128)(2,1)S(1)} %pad_maximum_fusion), channel_id=1, source_target_pairs={{0,1},{1,0},{2,3},{3,2},{4,5},{5,4},{6,7},{7,6},{8,9},{9,8},{10,11... | collective-permute-start | bytes 4718600 | tf_op jit(solution)/shard_map/ppermute | solution.py:408
  154.1 5.3 %collective-permute-start.44 = (bf16[2,48,640]{2,1,0:T(8,128)(2,1)S(1)}, bf16[2,48,640]{2,1,0:T(8,128)(2,1)S(1)}, u32[]{:S(2)}, u32[]{:S(2)}) collective-permute-start(bf16[2,48,640]{2,1,0:T(8,128)(2,1)S(1)} %get-tuple-element.230), channel_id=1, source_target_pairs={{0,4},{2,6},{4,0},{6,2},{8,12},{10,14},{12,8},{14,10},{1,5},{3,7},... | collective-permute-start | bytes 368648 | tf_op jit(solution)/shard_map/ppermute | solution.py:440
  155.7 11.4 %collective-permute-start.45 = (bf16[2,48,640]{2,1,0:T(8,128)(2,1)S(1)}, bf16[2,48,640]{2,1,0:T(8,128)(2,1)S(1)}, u32[]{:S(2)}, u32[]{:S(2)}) collective-permute-start(bf16[2,48,640]{2,1,0:T(8,128)(2,1)S(1)} %get-tuple-element.232), channel_id=1, source_target_pairs={{0,8},{2,10},{4,12},{6,14},{8,0},{10,2},{12,4},{14,6},{1,9},{3,11}... | collective-permute-start | bytes 368648 | tf_op jit(solution)/shard_map/ppermute | solution.py:440
  156.5 10.6 %collective-permute-start.46 = (bf16[2,48,640]{2,1,0:T(8,128)(2,1)S(1)}, bf16[2,48,640]{2,1,0:T(8,128)(2,1)S(1)}, u32[]{:S(2)}, u32[]{:S(2)}) collective-permute-start(bf16[2,48,640]{2,1,0:T(8,128)(2,1)S(1)} %get-tuple-element.231), channel_id=1, source_target_pairs={{0,12},{2,14},{4,8},{6,10},{8,4},{10,6},{12,0},{14,2},{1,13},{3,15... | collective-permute-start | bytes 368648 | tf_op jit(solution)/shard_map/ppermute | solution.py:440
  167.2 4.9 %collective-permute-start.47 = (bf16[48,1280]{1,0:T(8,128)(2,1)S(1)}, bf16[48,1280]{1,0:T(8,128)(2,1)S(1)}, u32[]{:S(2)}, u32[]{:S(2)}) collective-permute-start(bf16[48,1280]{1,0:T(8,128)(2,1)S(1)} %select_convert_fusion), channel_id=1, source_target_pairs={{0,16},{16,0},{1,17},{17,1},{2,18},{18,2},{3,19},{19,3},{4,20},{20... | collective-permute-start | bytes 368648 | tf_op jit(solution)/shard_map/ppermute | solution.py:411
  172.2 0.6 copy-start.4

commit v2 on v1

--- a/solution.py
+++ b/solution.py
@@ -507,15 +507,23 @@
         def load(l, sc, src, w, sem, c):
             copies = []
             cols = slice(0, MLP) if c == 0 else slice(MLP, HALF)
+            early, late = src[8:10]
             for side in range(2):
                 t = jnp.where(sc[1] == 0, side, 1 - side)
-                own = src[side * 8:side * 8 + 8]
                 for kk in range(m):
                     z = lax.bitwise_xor(sc[3], kk)
                     near = pl.ds(pl.multiple_of((2 * z + sc[4]) * piece, 16), piece)
                     far = pl.ds(pl.multiple_of((2 * z + 1 - sc[4]) * piece, 16), piece)
                     for i, (h, r) in enumerate(((sc[2], near), (1 - sc[2], near), (sc[2], far), (1 - sc[2], far))):
-                        a = own[i].at[l, :, cols] if kk == 0 else own[4 + i].at[kk - 1, :, cols]
+                        if side == 0:
+                            a, at = (src[i], l) if kk == 0 else (src[4 + i], kk - 1)
+                        elif kk == 0:
+                            a, at = early, 2 * i + l
+                        elif i == 0:
+                            a, at = (early, 7 + kk) if l == 0 else (src[10], kk - 1)
+                        else:
+                            a, at = late, (i - 1) * (m - 1) + kk - 1
+                        a = a.at[at, :, cols]
                         copies.append(pltpu.make_async_copy(a, w.at[t, h, r, cols], sem.at[c]))
             return copies
 
@@ -546,10 +554,11 @@
         columns[0], near, *firsts = after(columns[0], near, *firsts)
         rest = [columns[0], px(columns[0]), py(columns[0]), pd(columns[0])]
         columns.append(jnp.concatenate([near[None], pz_to(jnp.stack([start[1], near]), 2)]))
-        columns[1], *rest = after(columns[1], *rest)
-        twins = [pt(a) for a in firsts]
-        sources = [firsts + rest + twins + [pt(a) for a in rest]]
-        sources.append(columns[1:] + [px(columns[1]), py(columns[1]), pd(columns[1])])
+        early = pt(jnp.concatenate(firsts + columns[:1]))
+        early, *rest = after(early, *rest, columns[1])[:-1]
+        sources = [firsts + rest + [early, pt(jnp.concatenate(rest[1:]))]]
+        rest = [px(columns[1]), py(columns[1]), pd(columns[1])]
+        column_twin = pt(columns[1])
     else:
         def load(l, sc, src, w, sem, c):
             return [pltpu.make_async_copy(src[0], w, sem.at[c])] if c == 0 else []
@@ -566,16 +575,18 @@
     x0 = nn(select, batch[0]).astype(BF16)
     cot = nn(select, batch[1]).astype(BF16)
     x0, cot = after(x0, cot)
+    if direct:
+        x0, column_twin = after(x0, column_twin)
 
     def call(l, phases, **given):
-        return layer_call(phases, sources[l], functools.partial(load, l), store, out_shapes, scalars, given,
+        return layer_call(phases, sources[l] if phases[0] != "mine" else [], functools.partial(load, l), store, out_shapes, scalars, given,
                           total, width, ff, piece)
 
     r0 = call(0, ["forward"], x=x0)
     low0 = r0["out"]
     if direct:
-        low0, *rest = after(low0, *sources[1])
-        sources[1] = firsts + rest + twins + [pt(a) for a in rest]
+        low0, *rest = after(low0, *rest)
+        sources.append(firsts + columns[1:] + rest + [early, pt(jnp.concatenate(rest)), column_twin])
     r1 = call(1, ["forward", "back", "theirs"], x=low0, u=cot)
     if direct:
         got1 = pt(r1["g"][0])
@@ -603,7 +614,6 @@
         rows = placed([r1["keep"], low_got, b0["keep"], in_got], quad0[1], quad0[3])
         done1 = along_steps(crossed(quad1), quad0[1], quad0[3])
         quad0 = cross_second(quad0)
-        done1, *quad0 = after(done1, *quad0)
         twin, done0 = after(pt(rows), along(crossed(quad0)))
         done0, done1 = [jnp.concatenate([a[0], a[1]], 1) for a in (done0, done1)]
         mine = jnp.where(sec == 0, done0, done1)

time: 175 us -> 178 us (1.017)
  starting transfers between devices: 52.7 us -> 50 us
  other arithmetic: 6.4 us -> 8.65 us
  local copies, waits for them, and re-layouts: 4.51 us -> 6.36 us
    ppermute x7, waiting for transfers between devices: 12.9 us -> 15.1 us  [py(): return lax.ppermute(a, 'dp', [(i, i ^ 1) for i in range(n_dp)])]
    unnamed x26 -> x36, local copies, waits for them, and re-layouts: 0.7 us -> 2.6 us
    ppermute x15 -> x7, waiting for transfers between devices: 3.61 us -> 2.74 us  [pt(): return lax.ppermute(a, 'tensor', [(0, 1), (1, 0)])]
  transfers between devices with their start and end apart: 48 -> 40, of which waited for: 23 -> 19; matrix products, arithmetic and copies ran while one was open for 7% -> 7% of each run, Pallas kernels for 14% -> 14%
where the time goes in v2:
time: 178 us
  waiting for transfers between devices  60.2 us (34%)
  starting transfers between devices  50 us (28%)
  Pallas kernels  46.3 us (26%)
  other arithmetic  8.65 us (5%)
  local copies, waits for them, and re-layouts  6.36 us (4%)
  matrix products  4.52 us (3%)
  between operations  2.16 us (1%)
    pallas_call x5, Pallas kernels, layer_call(): pl.pallas_call(body, out_shape=[jax.ShapeDtypeStruct(*o) for o in outs],...  44.4 us
    ppermute x10, waiting for transfers between devices, pz_to(): return lax.ppermute(a, 'dp', [(i, i ^ 2 * kk) for i in range(n_dp)])  25.1 us
    ppermute x10, starting transfers between devices, pz_to(): return lax.ppermute(a, 'dp', [(i, i ^ 2 * kk) for i in range(n_dp)])  19.6 us
    ppermute x7, waiting for transfers between devices, py(): return lax.ppermute(a, 'dp', [(i, i ^ 1) for i in range(n_dp)])  15.1 us
    ppermute x11, starting transfers between devices, px(): return lax.ppermute(a, 'section', [(0, 1), (1, 0)])  14.9 us
    ppermute x11, waiting for transfers between devices, px(): return lax.ppermute(a, 'section', [(0, 1), (1, 0)])  14.8 us
    ppermute x7, starting transfers between devices, py(): return lax.ppermute(a, 'dp', [(i, i ^ 1) for i in range(n_dp)])  8.88 us
    dot_general x10, matrix products, mm(): return lax.dot_general(a, b, (dims, ((), ())), preferred_element_type=F32)  4.52 us
  transfers between devices with their start and end apart: 40, of which 19 were waited for; matrix products, arithmetic and copies ran while one was open for 7% of the time, Pallas kernels for 14%

profile of v2, /device:TPU:0, one launch (start us, length us, event | category | flops | bytes accessed | tf_op | source)
XLA Modules:
  0.0 178.1 jit_solution(5337660913209660302)
XLA Ops:
  0.7 1.3 constant_dynamic-slice_fusion
  2.0 0.7 copy-done.3
  2.8 0.7 collective-permute-start.1
  4.2 3.0 %collective-permute-start = (bf16[48,1280]{1,0:T(8,128)(2,1)S(1)}, bf16[48,1280]{1,0:T(8,128)(2,1)S(1)}, u32[]{:S(2)}, u32[]{:S(2)}) collective-permute-start(bf16[48,1280]{1,0:T(8,128)(2,1)S(1)} %broadcast_select_fusion.3), channel_id=1, source_target_pairs={{0,16},{16,0},{1,17},{17,1},{2,18},{18,2},{3,19},{19,3},{4,20},{20... | collective-permute-start | bytes 368648 | tf_op jit(solution)/shard_map/ppermute | solution.py:411
  7.2 3.9 %collective-permute-done = bf16[48,1280]{1,0:T(8,128)(2,1)S(1)} collective-permute-done((bf16[48,1280]{1,0:T(8,128)(2,1)S(1)}, bf16[48,1280]{1,0:T(8,128)(2,1)S(1)}, u32[]{:S(2)}, u32[]{:S(2)}) %collective-permute-start) | collective-permute-done | bytes 122912 | tf_op jit(solution)/shard_map/ppermute | solution.py:411
  11.2 1.2 collective-permute-start.2
  12.4 2.6 %collective-permute-start.3 = (bf16[48,1280]{1,0:T(8,128)(2,1)S(1)}, bf16[48,1280]{1,0:T(8,128)(2,1)S(1)}, u32[]{:S(2)}, u32[]{:S(2)}) collective-permute-start(bf16[48,1280]{1,0:T(8,128)(2,1)S(1)} %get-tuple-element.226), channel_id=1, source_target_pairs={{0,8},{2,10},{4,12},{6,14},{8,0},{10,2},{12,4},{14,6},{1,9},{3,11}... | collective-permute-start | bytes 368648 | tf_op jit(solution)/shard_map/ppermute | solution.py:440
  15.0 0.7 collective-permute-start.4
  15.7 1.8 %collective-permute-start.6 = (bf16[2,48,1280]{2,1,0:T(8,128)(2,1)S(1)}, bf16[2,48,1280]{2,1,0:T(8,128)(2,1)S(1)}, u32[]{:S(2)}, u32[]{:S(2)}) collective-permute-start(bf16[2,48,1280]{2,1,0:T(8,128)(2,1)S(1)} %pad_maximum_fusion.10.refs_2_.refs_3_.refs_13_), channel_id=1, source_target_pairs={{0,16},{16,0},{1,17},{17,1},{2,18},{18,2},{3,19},{19,3},{4,20},{20... | collective-permute-start | bytes 737288 | tf_op jit(solution)/shard_map/ppermute | solution.py:411
  17.5 1.7 collective-permute-start.7
  19.4 3.0 %collective-permute-start.8 = (bf16[2,48,1280]{2,1,0:T(8,128)(2,1)S(1)}, bf16[2,48,1280]{2,1,0:T(8,128)(2,1)S(1)}, u32[]{:S(2)}, u32[]{:S(2)}) collective-permute-start(bf16[2,48,1280]{2,1,0:T(8,128)(2,1)S(1)} %pad_maximum_fusion.10.refs_2_.refs_3_.refs_13_), channel_id=1, source_target_pairs={{0,18},{2,16},{4,22},{6,20},{8,26},{10,24},{12,30},{14,28},{16,2},... | collective-permute-start | bytes 737288 | tf_op jit(solution)/shard_map/ppermute | solution.py:417
  22.4 2.4 %collective-permute-done.3 = bf16[48,1280]{1,0:T(8,128)(2,1)S(1)} collective-permute-done((bf16[48,1280]{1,0:T(8,128)(2,1)S(1)}, bf16[48,1280]{1,0:T(8,128)(2,1)S(1)}, u32[]{:S(2)}, u32[]{:S(2)}) %collective-permute-start.3) | collective-permute-done | bytes 122912 | tf_op jit(solution)/shard_map/ppermute | solution.py:440
  24.9 3.1 %collective-permute-start.5 = (bf16[48,1280]{1,0:T(8,128)(2,1)S(1)}, bf16[48,1280]{1,0:T(8,128)(2,1)S(1)}, u32[]{:S(2)}, u32[]{:S(2)}) collective-permute-start(bf16[48,1280]{1,0:T(8,128)(2,1)S(1)} %get-tuple-element.111), channel_id=1, source_target_pairs={{0,4},{2,6},{4,0},{6,2},{8,12},{10,14},{12,8},{14,10},{1,5},{3,7},... | collective-permute-start | bytes 368648 | tf_op jit(solution)/shard_map/ppermute | solution.py:440
  28.0 3.5 %collective-permute-done.5 = bf16[48,1280]{1,0:T(8,128)(2,1)S(1)} collective-permute-done((bf16[48,1280]{1,0:T(8,128)(2,1)S(1)}, bf16[48,1280]{1,0:T(8,128)(2,1)S(1)}, u32[]{:S(2)}, u32[]{:S(2)}) %collective-permute-start.5) | collective-permute-done | bytes 122912 | tf_op jit(solution)/shard_map/ppermute | solution.py:440
  31.7 2.8 %collective-permute-start.9 = (bf16[2,48,1280]{2,1,0:T(8,128)(2,1)S(1)}, bf16[2,48,1280]{2,1,0:T(8,128)(2,1)S(1)}, u32[]{:S(2)}, u32[]{:S(2)}) collective-permute-start(bf16[2,48,1280]{2,1,0:T(8,128)(2,1)S(1)} %pad_maximum_fusion.11), channel_id=1, source_target_pairs={{0,8},{2,10},{4,12},{6,14},{8,0},{10,2},{12,4},{14,6},{1,9},{3,11}... | collective-permute-start | bytes 737288 | tf_op jit(solution)/shard_map/ppermute | solution.py:440
  34.5 1.5 collective-permute-start.12
  36.0 2.4 %collective-permute-start.13 = (bf16[3,48,1280]{2,1,0:T(8,128)(2,1)S(1)}, bf16[3,48,1280]{2,1,0:T(8,128)(2,1)S(1)}, u32[]{:S(2)}, u32[]{:S(2)}) collective-permute-start(bf16[3,48,1280]{2,1,0:T(8,128)(2,1)S(1)} %pad_maximum_fusion.7.refs_6_.refs_17_), channel_id=1, source_target_pairs={{0,2},{2,0},{4,6},{6,4},{8,10},{10,8},{12,14},{14,12},{1,3},{3,1},... | collective-permute-start | bytes 1105928 | tf_op jit(solution)/shard_map/ppermute | solution.py:414
  38.5 8.0 %collective-permute-done.9 = bf16[2,48,1280]{2,1,0:T(8,128)(2,1)S(1)} collective-permute-done((bf16[2,48,1280]{2,1,0:T(8,128)(2,1)S(1)}, bf16[2,48,1280]{2,1,0:T(8,128)(2,1)S(1)}, u32[]{:S(2)}, u32[]{:S(2)}) %collective-permute-start.9) | collective-permute-done | bytes 245792 | tf_op jit(solution)/shard_map/ppermute | solution.py:440
  46.5 7.8 %collective-permute-done.13.refs_8_.refs_19_ = bf16[3,48,1280]{2,1,0:T(8,128)(2,1)S(1)} collective-permute-done((bf16[3,48,1280]{2,1,0:T(8,128)(2,1)S(1)}, bf16[3,48,1280]{2,1,0:T(8,128)(2,1)S(1)}, u32[]{:S(2)}, u32[]{:S(2)}) %collective-permute-start.13) | collective-permute-done | bytes 368672 | tf_op jit(solution)/shard_map/ppermute | solution.py:414
  54.3 0.7 collective-permute-done.14.refs_9_.refs_20_
  55.1 1.1 copy-done.1
  56.1 1.2 pad_maximum_fusion.3
  57.3 0.6 dynamic_slice.11
  58.7 1.1 pad_maximum_fusion.2
  59.8 0.6 collective-permute-start.10
  60.9 0.5 convolution_convert_fusion.5.refs_1_
  61.5 1.5 collective-permute-start.16
  63.0 0.8 collective-permute-start.17
  63.8 1.2 collective-permute-start.18
  65.1 8.8 %shard_map.186 = (bf16[416,384]{1,0:T(8,128)(2,1)S(1)}, f32[416,384]{1,0:T(8,128)S(1)}, f32[416,128]{1,0:T(8,128)S(1)}, bf16[416,384]{1,0:T(8,128)(2,1)S(1)}, bf...) custom-call(s32[5]{0:T(128)S(1)} %stack.113.refs_0_.sc, ...), custom_call_target="tpu_custom_call" | custom-call | flops 10000000000 | bytes 8388608 | tf_op jit(solution)/shard_map/pallas_call | solution.py:342
  73.9 5.7 %collective-permute-done.17.refs_9_ = bf16[3,48,1280]{2,1,0:T(8,128)(2,1)S(1)} collective-permute-done((bf16[3,48,1280]{2,1,0:T(8,128)(2,1)S(1)}, bf16[3,48,1280]{2,1,0:T(8,128)(2,1)S(1)}, u32[]{:S(2)}, u32[]{:S(2)}) %collective-permute-start.17) | collective-permute-done | bytes 368672 | tf_op jit(solution)/shard_map/ppermute | solution.py:414
  79.5 1.6 collective-permute-done.18.refs_10_
  81.4 2.7 %collective-permute-done.19.refs_12_ = bf16[9,48,1280]{2,1,0:T(8,128)(2,1)S(1)} collective-permute-done((bf16[9,48,1280]{2,1,0:T(8,128)(2,1)S(1)}, bf16[9,48,1280]{2,1,0:T(8,128)(2,1)S(1)}, u32[]{:S(2)}, u32[]{:S(2)}) %collective-permute-start.19) | collective-permute-done | bytes 1105952 | tf_op jit(solution)/shard_map/ppermute | solution.py:408
  84.1 18.7 %shard_map.187 = (bf16[416,384]{1,0:T(8,128)(2,1)S(1)}, bf16[2,416,256]{2,1,0:T(8,128)(2,1)S(1)}, bf16[416,384]{1,0:T(8,128)(2,1)S(1)}, bf16[416,1536]{1,0:T(8,1...) custom-call(s32[5]{0:T(128)S(1)} %stack.113.refs_0_.sc, ...), custom_call_target="tpu_custom_call" | custom-call | flops 30000001024 | bytes 8388608 | tf_op jit(solution)/shard_map/pallas_call | solution.py:342
  103.3 0.6 collective-permute-start.22
  104.8 2.2 %shard_map.188 = (bf16[2,4,48,640]{3,2,1,0:T(8,128)(2,1)S(1)}, bf16[2,4,48,640]{3,2,1,0:T(8,128)(2,1)S(1)}, bf16[2,4,48,640]{3,2,1,0:T(8,128)(2,1)S(1)}, bf16[2,4,48,640]{3,2,1,0:T(8,128)(2,1)S(1)}) custom-call(s32[5]{0:T(128)S(1)} %stack.113.refs_0_.sc, bf16[416,384]{1,0:T(8,128)(2,1)S(1)} %get-tuple-element.133.refs_1_, ...), custom_call_target="tpu_custom_call" | custom-call | flops 10000000000 | bytes 8388608 | tf_op jit(solution)/shard_map/pallas_call | solution.py:342
  107.5 1.5 collective-permute-start.23
  109.0 0.8 collective-permute-start.24
  109.9 12.5 %shard_map.189 = (bf16[416,384]{1,0:T(8,128)(2,1)S(1)}, bf16[416,384]{1,0:T(8,128)(2,1)S(1)}, bf16[416,384]{1,0:T(8,128)(2,1)S(1)}, bf16[416,1536]{1,0:T(8,128)(...) custom-call(s32[5]{0:T(128)S(1)} %stack.113.refs_0_.sc, ...), custom_call_target="tpu_custom_call" | custom-call | flops 20000000000 | bytes 8388608 | tf_op jit(solution)/shard_map/pallas_call | solution.py:342
  122.4 1.5 collective-permute-start.21
  125.0 0.6 collective-permute-start.26
  125.8 1.2 collective-permute-start.25
  127.1 2.2 %shard_map.190 = (bf16[2,4,48,640]{3,2,1,0:T(8,128)(2,1)S(1)}, bf16[2,4,48,640]{3,2,1,0:T(8,128)(2,1)S(1)}, bf16[2,4,48,640]{3,2,1,0:T(8,128)(2,1)S(1)}, bf16[2,4,48,640]{3,2,1,0:T(8,128)(2,1)S(1)}) custom-call(s32[5]{0:T(128)S(1)} %stack.113.refs_0_.sc, bf16[416,384]{1,0:T(8,128)(2,1)S(1)} %get-tuple-element.151.refs_4_.refs_1_, ...), custom_call_target="tpu_custom_call" | custom-call | flops 10000000000 | bytes 8388608 | tf_op jit(solution)/shard_map/pallas_call | solution.py:342
  129.8 0.6 collective-permute-start.29
  130.4 1.8 collective-permute-start.30
  132.2 0.7 collective-permute-done.21
  132.8 5.3 %collective-permute-done.26 = bf16[4,48,640]{2,1,0:T(8,128)(2,1)S(1)} collective-permute-done((bf16[4,48,640]{2,1,0:T(8,128)(2,1)S(1)}, bf16[4,48,640]{2,1,0:T(8,128)(2,1)S(1)}, u32[]{:S(2)}, u32[]{:S(2)}) %collective-permute-start.26) | collective-permute-done | bytes 245792 | tf_op jit(solution)/shard_map/ppermute | solution.py:411
  140.5 0.7 collective-permute-start.28
  141.3 5.0 %collective-permute-done.37 = bf16[2,2,48,640]{3,2,0,1:T(8,128)(2,1)S(1)} collective-permute-done((bf16[2,2,48,640]{3,2,0,1:T(8,128)(2,1)S(1)}, bf16[2,2,48,640]{3,2,0,1:T(8,128)(2,1)S(1)}, u32[]{:S(2)}, u32[]{:S(2)}) %collective-permute-start.37) | collective-permute-done | bytes 245792 | tf_op jit(solution)/shard_map/ppermute | solution.py:440
  146.4 0.8 collective-permute-done.29
  147.3 4.5 %collective-permute-start.38 = (bf16[2,48,640]{2,1,0:T(8,128)(2,1)S(1)}, bf16[2,48,640]{2,1,0:T(8,128)(2,1)S(1)}, u32[]{:S(2)}, u32[]{:S(2)}) collective-permute-start(bf16[2,48,640]{2,1,0:T(8,128)(2,1)S(1)} %fusion.35), channel_id=1, source_target_pairs={{0,8},{2,10},{4,12},{6,14},{8,0},{10,2},{12,4},{14,6},{1,9},{3,11}... | collective-permute-start | bytes 368648 | tf_op jit(solution)/shard_map/ppermute | solution.py:440
  151.9 1.5 collective-permute-start.33
  153.9 0.8 slice-done
  155.2 2.9 %collective-permute-done.33 = bf16[4,48,640]{2,1,0:T(8,128)(2,1)S(1)} collective-permute-done((bf16[4,48,640]{2,1,0:T(8,128)(2,1)S(1)}, bf16[4,48,640]{2,1,0:T(8,128)(2,1)S(1)}, u32[]{:S(2)}, u32[]{:S(2)}) %collective-permute-start.33) | collective-permute-done | bytes 245792 | tf_op jit(solution)/shard_map/ppermute | solution.py:411
  158.2 1.6 collective-permute-done.32
  160.5 4.0 %collective-permute-start.36 = (bf16[2,48,640]{2,1,0:T(8,128)(2,1)S(1)}, bf16[2,48,640]{2,1,0:T(8,128)(2,1)S(1)}, u32[]{:S(2)}, u32[]{:S(2)}) collective-permute-start(bf16[2,48,640]{2,1,0:T(8,128)(2,1)S(1)} %get-tuple-element.223), channel_id=1, source_target_pairs={{0,12},{2,14},{4,8},{6,10},{8,4},{10,6},{12,0},{14,2},{1,13},{3,15... | collective-permute-start | bytes 368648 | tf_op jit(solution)/shard_map/ppermute | solution.py:440
  164.5 2.8 %collective-permute-done.34 = bf16[2,48,640]{2,1,0:T(8,128)(2,1)S(1)} collective-permute-done((bf16[2,48,640]{2,1,0:T(8,128)(2,1)S(1)}, bf16[2,48,640]{2,1,0:T(8,128)(2,1)S(1)}, u32[]{:S(2)}, u32[]{:S(2)}) %collective-permute-start.34) | collective-permute-done | bytes 122912 | tf_op jit(solution)/shard_map/ppermute | solution.py:440
  167.2 3.3 %collective-permute-done.35 = bf16[2,48,640]{2,1,0:T(8,128)(2,1)S(1)} collective-permute-done((bf16[2,48,640]{2,1,0:T(8,128)(2,1)S(1)}, bf16[2,48,640]{2,1,0:T(8,128)(2,1)S(1)}, u32[]{:S(2)}, u32[]{:S(2)}) %collective-permute-start.35) | collective-permute-done | bytes 122912 | tf_op jit(solution)/shard_map/ppermute | solution.py:440
  171.4 1.2 fusion.12
  172.6 1.0 fusion.10
  173.7 0.7 fusion.30.mine_ref
  174.4 1.2 collective-permute-done.39.other_ref
  175.6 0.6 copy-done.7
  176.2 1.9 %shard_map.191 = (f32[2,48]{1,0:T(2,128)}, f32[4,48]{1,0:T(4,128)}, f32[3,48,192]{2,1,0:T(8,128)}, f32[2,192]{1,0:T(2,128)}, f32[48,192]{1,0:T(8,128)}, /*index=...) custom-call(s32[5]{0:T(128)} %copy-done, f32[48,1280]{1,0:T(8,128)} %fusion.30.mine_ref, bf16[48,1280]{1,0:T(8,128)(2,1)} %copy-done.7), custom_call_target="tpu_custom_call" | custom-call | tf_op jit(solution)/shard_map/pallas_call | solution.py:385
  (144 shorter events, 10.6 us)
Async XLA Ops:
  0.6 2.9 %copy-start.10 = (bf16[1,192,48]{1,2,0:T(8,128)(2,1)S(1)}, bf16[1,192,48]{1,2,0:T(8,128)(2,1)}, u32[]{:S(2)}) copy-start(bf16[1,192,48]{1,2,0:T(8,128)(2,1)} %param.18) | copy-start | bytes 55300
  0.7 2.9 %copy-start.6 = (bf16[1,48,3,192]{3,1,2,0:T(8,128)(2,1)S(1)}, bf16[1,48,3,192]{3,1,2,0:T(8,128)(2,1)}, u32[]{:S(2)}) copy-start(bf16[1,48,3,192]{3,1,2,0:T(8,128)(2,1)} %param.16) | copy-start | bytes 165892
  0.7 3.0 %copy-start.13 = (bf16[1,4,48]{2,1,0:T(4,128)(2,1)S(1)}, bf16[1,4,48]{2,1,0:T(4,128)(2,1)}, u32[]{:S(2)}) copy-start(bf16[1,4,48]{2,1,0:T(4,128)(2,1)} %param.15) | copy-start | bytes 1156
  0.7 3.0 %copy-start.14 = (bf16[1,2,48]{2,1,0:T(2,128)(2,1)S(1)}, bf16[1,2,48]{2,1,0:T(2,128)(2,1)}, u32[]{:S(2)}) copy-start(bf16[1,2,48]{2,1,0:T(2,128)(2,1)} %param.14) | copy-start | bytes 580
  0.7 3.1 %copy-start.11 = (bf16[1,2,192]{2,1,0:T(2,128)(2,1)S(1)}, bf16[1,2,192]{2,1,0:T(2,128)(2,1)}, u32[]{:S(2)}) copy-start(bf16[1,2,192]{2,1,0:T(2,128)(2,1)} %param.17) | copy-start | bytes 2308
  0.7 3.1 %copy-start.12 = (bf16[1,768]{1,0:T(2,128)(2,1)S(1)}, bf16[1,768]{1,0:T(2,128)(2,1)}, u32[]{:S(2)}) copy-start(bf16[1,768]{1,0:T(2,128)(2,1)} %param.20) | copy-start | bytes 4612
  0.7 3.3 %copy-start.8 = (bf16[1,768,48]{1,2,0:T(8,128)(2,1)S(1)}, bf16[1,768,48]{1,2,0:T(8,128)(2,1)}, u32[]{:S(2)}) copy-start(bf16[1,768,48]{1,2,0:T(8,128)(2,1)} %param.21) | copy-start | bytes 221188
  0.7 3.3 %copy-start.9 = (bf16[1,48,768]{2,1,0:T(8,128)(2,1)S(1)}, bf16[1,48,768]{2,1,0:T(8,128)(2,1)}, u32[]{:S(2)}) copy-start(bf16[1,48,768]{2,1,0:T(8,128)(2,1)} %param.19) | copy-start | bytes 221188
  2.0 0.7 copy-start.3
  2.8 8.4 %collective-permute-start.1 = (bf16[2,208,384]{2,1,0:T(8,128)(2,1)S(1)}, bf16[2,208,384]{2,1,0:T(8,128)(2,1)S(1)}, u32[]{:S(2)}, u32[]{:S(2)}) collective-permute-start(bf16[2,208,384]{2,1,0:T(8,128)(2,1)S(1)} %pad_maximum_fusion.9), channel_id=1, source_target_pairs={{3,1},{5,3},{7,5},{9,7},{11,9},{13,11},{15,13},{19,17},{21,19},{23... | collective-permute-start | bytes 958472 | tf_op jit(solution)/shard_map/ppermute | solution.py:488
  4.2 7.0 %collective-permute-start = (bf16[48,1280]{1,0:T(8,128)(2,1)S(1)}, bf16[48,1280]{1,0:T(8,128)(2,1)S(1)}, u32[]{:S(2)}, u32[]{:S(2)}) collective-permute-start(bf16[48,1280]{1,0:T(8,128)(2,1)S(1)} %broadcast_select_fusion.3), channel_id=1, source_target_pairs={{0,16},{16,0},{1,17},{17,1},{2,18},{18,2},{3,19},{19,3},{4,20},{20... | collective-permute-start | bytes 368648 | tf_op jit(solution)/shard_map/ppermute | solution.py:411
  11.2 8.2 %collective-permute-start.2 = (bf16[48,1280]{1,0:T(8,128)(2,1)S(1)}, bf16[48,1280]{1,0:T(8,128)(2,1)S(1)}, u32[]{:S(2)}, u32[]{:S(2)}) collective-permute-start(bf16[48,1280]{1,0:T(8,128)(2,1)S(1)} %get-tuple-element.226), channel_id=1, source_target_pairs={{0,4},{2,6},{4,0},{6,2},{8,12},{10,14},{12,8},{14,10},{1,5},{3,7},... | collective-permute-start | bytes 368648 | tf_op jit(solution)/shard_map/ppermute | solution.py:440
  12.4 12.4 %collective-permute-start.3 = (bf16[48,1280]{1,0:T(8,128)(2,1)S(1)}, bf16[48,1280]{1,0:T(8,128)(2,1)S(1)}, u32[]{:S(2)}, u32[]{:S(2)}) collective-permute-start(bf16[48,1280]{1,0:T(8,128)(2,1)S(1)} %get-tuple-element.226), channel_id=1, source_target_pairs={{0,8},{2,10},{4,12},{6,14},{8,0},{10,2},{12,4},{14,6},{1,9},{3,11}... | collective-permute-start | bytes 368648 | tf_op jit(solution)/shard_map/ppermute | solution.py:440
  15.0 9.8 %collective-permute-start.4 = (bf16[48,1280]{1,0:T(8,128)(2,1)S(1)}, bf16[48,1280]{1,0:T(8,128)(2,1)S(1)}, u32[]{:S(2)}, u32[]{:S(2)}) collective-permute-start(bf16[48,1280]{1,0:T(8,128)(2,1)S(1)} %get-tuple-element.226), channel_id=1, source_target_pairs={{0,12},{2,14},{4,8},{6,10},{8,4},{10,6},{12,0},{14,2},{1,13},{3,15... | collective-permute-start | bytes 368648 | tf_op jit(solution)/shard_map/ppermute | solution.py:440
  15.7 15.8 %collective-permute-start.6 = (bf16[2,48,1280]{2,1,0:T(8,128)(2,1)S(1)}, bf16[2,48,1280]{2,1,0:T(8,128)(2,1)S(1)}, u32[]{:S(2)}, u32[]{:S(2)}) collective-permute-start(bf16[2,48,1280]{2,1,0:T(8,128)(2,1)S(1)} %pad_maximum_fusion.10.refs_2_.refs_3_.refs_13_), channel_id=1, source_target_pairs={{0,16},{16,0},{1,17},{17,1},{2,18},{18,2},{3,19},{19,3},{4,20},{20... | collective-permute-start | bytes 737288 | tf_op jit(solution)/shard_map/ppermute | solution.py:411
  17.5 14.0 %collective-permute-start.7 = (bf16[2,48,1280]{2,1,0:T(8,128)(2,1)S(1)}, bf16[2,48,1280]{2,1,0:T(8,128)(2,1)S(1)}, u32[]{:S(2)}, u32[]{:S(2)}) collective-permute-start(bf16[2,48,1280]{2,1,0:T(8,128)(2,1)S(1)} %pad_maximum_fusion.10.refs_2_.refs_3_.refs_13_), channel_id=1, source_target_pairs={{0,2},{2,0},{4,6},{6,4},{8,10},{10,8},{12,14},{14,12},{1,3},{3,1},... | collective-permute-start | bytes 737288 | tf_op jit(solution)/shard_map/ppermute | solution.py:414
  19.4 12.1 %collective-permute-start.8 = (bf16[2,48,1280]{2,1,0:T(8,128)(2,1)S(1)}, bf16[2,48,1280]{2,1,0:T(8,128)(2,1)S(1)}, u32[]{:S(2)}, u32[]{:S(2)}) collective-permute-start(bf16[2,48,1280]{2,1,0:T(8,128)(2,1)S(1)} %pad_maximum_fusion.10.refs_2_.refs_3_.refs_13_), channel_id=1, source_target_pairs={{0,18},{2,16},{4,22},{6,20},{8,26},{10,24},{12,30},{14,28},{16,2},... | collective-permute-start | bytes 737288 | tf_op jit(solution)/shard_map/ppermute | solution.py:417
  24.9 6.6 %collective-permute-start.5 = (bf16[48,1280]{1,0:T(8,128)(2,1)S(1)}, bf16[48,1280]{1,0:T(8,128)(2,1)S(1)}, u32[]{:S(2)}, u32[]{:S(2)}) collective-permute-start(bf16[48,1280]{1,0:T(8,128)(2,1)S(1)} %get-tuple-element.111), channel_id=1, source_target_pairs={{0,4},{2,6},{4,0},{6,2},{8,12},{10,14},{12,8},{14,10},{1,5},{3,7},... | collective-permute-start | bytes 368648 | tf_op jit(solution)/shard_map/ppermute | solution.py:440
  31.6 23.4 %collective-permute-start.11 = (bf16[11,48,1280]{2,1,0:T(8,128)(2,1)S(1)}, bf16[11,48,1280]{2,1,0:T(8,128)(2,1)S(1)}, u32[]{:S(2)}, u32[]{:S(2)}) collective-permute-start(bf16[11,48,1280]{2,1,0:T(8,128)(2,1)S(1)} %constant_dynamic-update-slice_fusion), channel_id=1, source_target_pairs={{0,1},{1,0},{2,3},{3,2},{4,5},{5,4},{6,7},{7,6},{8,9},{9,8},{10,11... | collective-permute-start | bytes 4055048 | tf_op jit(solution)/shard_map/ppermute | solution.py:408
  31.7 25.6 %copy-start.15 = (s32[2]{0:T(128)S(1)}, s32[2]{0:T(128)}, u32[]{:S(2)}) copy-start(s32[2]{0:T(128)} %param.12) | copy-start | bytes 28
  31.7 14.7 %collective-permute-start.9 = (bf16[2,48,1280]{2,1,0:T(8,128)(2,1)S(1)}, bf16[2,48,1280]{2,1,0:T(8,128)(2,1)S(1)}, u32[]{:S(2)}, u32[]{:S(2)}) collective-permute-start(bf16[2,48,1280]{2,1,0:T(8,128)(2,1)S(1)} %pad_maximum_fusion.11), channel_id=1, source_target_pairs={{0,8},{2,10},{4,12},{6,14},{8,0},{10,2},{12,4},{14,6},{1,9},{3,11}... | collective-permute-start | bytes 737288 | tf_op jit(solution)/shard_map/ppermute | solution.py:440
  34.5 11.9 %collective-permute-start.12 = (bf16[3,48,1280]{2,1,0:T(8,128)(2,1)S(1)}, bf16[3,48,1280]{2,1,0:T(8,128)(2,1)S(1)}, u32[]{:S(2)}, u32[]{:S(2)}) collective-permute-start(bf16[3,48,1280]{2,1,0:T(8,128)(2,1)S(1)} %pad_maximum_fusion.7.refs_6_.refs_17_), channel_id=1, source_target_pairs={{0,16},{16,0},{1,17},{17,1},{2,18},{18,2},{3,19},{19,3},{4,20},{20... | collective-permute-start | bytes 1105928 | tf_op jit(solution)/shard_map/ppermute | solution.py:411
  36.0 18.3 %collective-permute-start.13 = (bf16[3,48,1280]{2,1,0:T(8,128)(2,1)S(1)}, bf16[3,48,1280]{2,1,0:T(8,128)(2,1)S(1)}, u32[]{:S(2)}, u32[]{:S(2)}) collective-permute-start(bf16[3,48,1280]{2,1,0:T(8,128)(2,1)S(1)} %pad_maximum_fusion.7.refs_6_.refs_17_), channel_id=1, source_target_pairs={{0,2},{2,0},{4,6},{6,4},{8,10},{10,8},{12,14},{14,12},{1,3},{3,1},... | collective-permute-start | bytes 1105928 | tf_op jit(solution)/shard_map/ppermute | solution.py:414
  38.5 16.6 %collective-permute-start.14 = (bf16[3,48,1280]{2,1,0:T(8,128)(2,1)S(1)}, bf16[3,48,1280]{2,1,0:T(8,128)(2,1)S(1)}, u32[]{:S(2)}, u32[]{:S(2)}) collective-permute-start(bf16[3,48,1280]{2,1,0:T(8,128)(2,1)S(1)} %pad_maximum_fusion.7.refs_6_.refs_17_), channel_id=1, source_target_pairs={{0,18},{2,16},{4,22},{6,20},{8,26},{10,24},{12,30},{14,28},{16,2},... | collective-permute-start | bytes 1105928 | tf_op jit(solution)/shard_map/ppermute | solution.py:417
  55.1 1.1 copy-start.1
  57.3 7.8 %collective-permute-start.15 = (bf16[9,48,1280]{2,1,0:T(8,128)(2,1)}, bf16[9,48,1280]{2,1,0:T(8,128)(2,1)}, u32[]{:S(2)}, u32[]{:S(2)}) collective-permute-start(bf16[9,48,1280]{2,1,0:T(8,128)(2,1)} %pad_maximum_fusion.3), channel_id=1, source_target_pairs={{0,1},{1,0},{2,3},{3,2},{4,5},{5,4},{6,7},{7,6},{8,9},{9,8},{10,11... | collective-permute-start | bytes 3317768 | tf_op jit(solution)/shard_map/ppermute | solution.py:408
  58.6 68.4 %copy-start = (s32[5]{0:T(128)}, s32[5]{0:T(128)S(1)}, u32[]{:S(2)}) copy-start(s32[5]{0:T(128)S(1)} %stack.113.refs_0_.sc) | copy-start | bytes 64
  59.8 5.3 %collective-permute-start.10 = (bf16[3,48,1280]{2,1,0:T(8,128)(2,1)S(1)}, bf16[3,48,1280]{2,1,0:T(8,128)(2,1)S(1)}, u32[]{:S(2)}, u32[]{:S(2)}) collective-permute-start(bf16[3,48,1280]{2,1,0:T(8,128)(2,1)S(1)} %pad_maximum_fusion.8.refs_7_), channel_id=1, source_target_pairs={{0,1},{1,0},{2,3},{3,2},{4,5},{5,4},{6,7},{7,6},{8,9},{9,8},{10,11... | collective-permute-start | bytes 1105928 | tf_op jit(solution)/shard_map/ppermute | solution.py:408
  60.9 4.1 %copy-start.2 = (bf16[11,48,1280]{2,1,0:T(8,128)(2,1)S(1)}, bf16[11,48,1280]{2,1,0:T(8,128)(2,1)}, u32[]{:S(2)}) copy-start(bf16[11,48,1280]{2,1,0:T(8,128)(2,1)} %copy-done.1) | copy-start | bytes 4055044
  61.5 12.4 %collective-permute-start.16 = (bf16[3,48,1280]{2,1,0:T(8,128)(2,1)S(1)}, bf16[3,48,1280]{2,1,0:T(8,128)(2,1)S(1)}, u32[]{:S(2)}, u32[]{:S(2)}) collective-permute-start(bf16[3,48,1280]{2,1,0:T(8,128)(2,1)S(1)} %pad_maximum_fusion.8.refs_7_), channel_id=1, source_target_pairs={{0,16},{16,0},{1,17},{17,1},{2,18},{18,2},{3,19},{19,3},{4,20},{20... | collective-permute-start | bytes 1105928 | tf_op jit(solution)/shard_map/ppermute | solution.py:411
  63.0 16.5 %collective-permute-start.17 = (bf16[3,48,1280]{2,1,0:T(8,128)(2,1)S(1)}, bf16[3,48,1280]{2,1,0:T(8,128)(2,1)S(1)}, u32[]{:S(2)}, u32[]{:S(2)}) collective-permute-start(bf16[3,48,1280]{2,1,0:T(8,128)(2,1)S(1)} %pad_maximum_fusion.8.refs_7_), channel_id=1, source_target_pairs={{0,2},{2,0},{4,6},{6,4},{8,10},{10,8},{12,14},{14,12},{1,3},{3,1},... | collective-permute-start | bytes 1105928 | tf_op jit(solution)/shard_map/ppermute | solution.py:414
  63.8 17.3 %collective-permute-start.18 = (bf16[3,48,1280]{2,1,0:T(8,128)(2,1)S(1)}, bf16[3,48,1280]{2,1,0:T(8,128)(2,1)S(1)}, u32[]{:S(2)}, u32[]{:S(2)}) collective-permute-start(bf16[3,48,1280]{2,1,0:T(8,128)(2,1)S(1)} %pad_maximum_fusion.8.refs_7_), channel_id=1, source_target_pairs={{0,18},{2,16},{4,22},{6,20},{8,26},{10,24},{12,30},{14,28},{16,2},... | collective-permute-start | bytes 1105928 | tf_op jit(solution)/shard_map/ppermute | solution.py:417
  81.3 2.8 %collective-permute-start.19 = (bf16[9,48,1280]{2,1,0:T(8,128)(2,1)S(1)}, bf16[9,48,1280]{2,1,0:T(8,128)(2,1)S(1)}, u32[]{:S(2)}, u32[]{:S(2)}) collective-permute-start(bf16[9,48,1280]{2,1,0:T(8,128)(2,1)S(1)} %pad_maximum_fusion.4), channel_id=1, source_target_pairs={{0,1},{1,0},{2,3},{3,2},{4,5},{5,4},{6,7},{7,6},{8,9},{9,8},{10,11... | collective-permute-start | bytes 3317768 | tf_op jit(solution)/shard_map/ppermute | solution.py:408
  102.8 4.2 %collective-permute-start.20 = (bf16[2,2,2,4,48,640]{5,4,3,2,1,0:T(8,128)(2,1)S(1)}, bf16[2,2,2,4,48,640]{5,4,3,2,1,0:T(8,128)(2,1)S(1)}, u32[]{:S(2)}, u32[]{:S(2)}) collective-permute-start(bf16[2,2,2,4,48,640]{5,4,3,2,1,0:T(8,128)(2,1)S(1)} %get-tuple-element.145), channel_id=1, source_target_pairs={{0,1},{1,0},{2,3},{3,2},{4,5},{5,4},{6,7},{7,6},{8,9},{9,8},{10,11... | collective-permute-start | bytes 5898248 | tf_op jit(solution)/shard_map/ppermute | solution.py:408
  103.3 27.2 %collective-permute-start.22 = (bf16[416,384]{1,0:T(8,128)(2,1)S(1)}, bf16[416,384]{1,0:T(8,128)(2,1)S(1)}, u32[]{:S(2)}, u32[]{:S(2)}) collective-permute-start(bf16[416,384]{1,0:T(8,128)(2,1)S(1)} %get-tuple-element.161), channel_id=1, source_target_pairs={{0,16},{16,0},{1,17},{17,1},{2,18},{18,2},{3,19},{19,3},{4,20},{20... | collective-permute-start | bytes 958472 | tf_op jit(solution)/shard_map/ppermute | solution.py:411
  107.5 17.3 %collective-permute-start.23 = (bf16[2,4,48,640]{3,2,1,0:T(8,128)(2,1)S(1)}, bf16[2,4,48,640]{3,2,1,0:T(8,128)(2,1)S(1)}, u32[]{:S(2)}, u32[]{:S(2)}) collective-permute-start(bf16[2,4,48,640]{3,2,1,0:T(8,128)(2,1)S(1)} %get-tuple-element.215), channel_id=1, source_target_pairs={{0,16},{16,0},{1,17},{17,1},{2,18},{18,2},{3,19},{19,3},{4,20},{20... | collective-permute-start | bytes 1474568 | tf_op jit(solution)/shard_map/ppermute | solution.py:411
  109.0 15.8 %collective-permute-start.24 = (bf16[2,4,48,640]{3,2,1,0:T(8,128)(2,1)S(1)}, bf16[2,4,48,640]{3,2,1,0:T(8,128)(2,1)S(1)}, u32[]{:S(2)}, u32[]{:S(2)}) collective-permute-start(bf16[2,4,48,640]{3,2,1,0:T(8,128)(2,1)S(1)} %get-tuple-element.214), channel_id=1, source_target_pairs={{0,2},{2,0},{4,6},{6,4},{8,10},{10,8},{12,14},{14,12},{1,3},{3,1},... | collective-permute-start | bytes 1474568 | tf_op jit(solution)/shard_map/ppermute | solution.py:414
  122.4 10.5 %collective-permute-start.21 = (bf16[416,384]{1,0:T(8,128)(2,1)S(1)}, bf16[416,384]{1,0:T(8,128)(2,1)S(1)}, u32[]{:S(2)}, u32[]{:S(2)}) collective-permute-start(bf16[416,384]{1,0:T(8,128)(2,1)S(1)} %get-tuple-element.160), channel_id=1, source_target_pairs={{0,16},{16,0},{1,17},{17,1},{2,18},{18,2},{3,19},{19,3},{4,20},{20... | collective-permute-start | bytes 958472 | tf_op jit(solution)/shard_map/ppermute | solution.py:411
  124.4 29.2 %copy-start.4 = (bf16[512,384]{1,0:T(8,128)(2,1)}, bf16[512,384]{1,0:T(8,128)(2,1)S(1)}, u32[]{:S(2)}) copy-start(bf16[512,384]{1,0:T(8,128)(2,1)S(1)} %convolution_convert_fusion.1) | copy-start | bytes 1179652
  124.8 4.5 %collective-permute-start.27 = (bf16[2,2,2,4,48,640]{5,4,3,2,1,0:T(8,128)(2,1)S(1)}, bf16[2,2,2,4,48,640]{5,4,3,2,1,0:T(8,128)(2,1)S(1)}, u32[]{:S(2)}, u32[]{:S(2)}) collective-permute-start(bf16[2,2,2,4,48,640]{5,4,3,2,1,0:T(8,128)(2,1)S(1)} %get-tuple-element.178), channel_id=1, source_target_pairs={{0,1},{1,0},{2,3},{3,2},{4,5},{5,4},{6,7},{7,6},{8,9},{9,8},{10,11... | collective-permute-start | bytes 5898248 | tf_op jit(solution)/shard_map/ppermute | solution.py:408
  125.0 13.1 %collective-permute-start.26 = (bf16[4,48,640]{2,1,0:T(8,128)(2,1)S(1)}, bf16[4,48,640]{2,1,0:T(8,128)(2,1)S(1)}, u32[]{:S(2)}, u32[]{:S(2)}) collective-permute-start(bf16[4,48,640]{2,1,0:T(8,128)(2,1)S(1)} %fusion.22), channel_id=1, source_target_pairs={{0,16},{16,0},{1,17},{17,1},{2,18},{18,2},{3,19},{19,3},{4,20},{20... | collective-permute-start | bytes 737288 | tf_op jit(solution)/shard_map/ppermute | solution.py:411
  125.8 12.3 %collective-permute-start.25 = (bf16[4,48,640]{2,1,0:T(8,128)(2,1)S(1)}, bf16[4,48,640]{2,1,0:T(8,128)(2,1)S(1)}, u32[]{:S(2)}, u32[]{:S(2)}) collective-permute-start(bf16[4,48,640]{2,1,0:T(8,128)(2,1)S(1)} %fusion.21), channel_id=1, source_target_pairs={{0,2},{2,0},{4,6},{6,4},{8,10},{10,8},{12,14},{14,12},{1,3},{3,1},... | collective-permute-start | bytes 737288 | tf_op jit(solution)/shard_map/ppermute | solution.py:414
  129.8 17.5 %collective-permute-start.29 = (bf16[2,4,48,640]{3,2,1,0:T(8,128)(2,1)S(1)}, bf16[2,4,48,640]{3,2,1,0:T(8,128)(2,1)S(1)}, u32[]{:S(2)}, u32[]{:S(2)}) collective-permute-start(bf16[2,4,48,640]{3,2,1,0:T(8,128)(2,1)S(1)} %get-tuple-element.211), channel_id=1, source_target_pairs={{0,16},{16,0},{1,17},{17,1},{2,18},{18,2},{3,19},{19,3},{4,20},{20... | collective-permute-start | bytes 1474568 | tf_op jit(solution)/shard_map/ppermute | solution.py:411
  130.4 16.8 %collective-permute-start.30 = (bf16[2,4,48,640]{3,2,1,0:T(8,128)(2,1)S(1)}, bf16[2,4,48,640]{3,2,1,0:T(8,128)(2,1)S(1)}, u32[]{:S(2)}, u32[]{:S(2)}) collective-permute-start(bf16[2,4,48,640]{3,2,1,0:T(8,128)(2,1)S(1)} %get-tuple-element.210), channel_id=1, source_target_pairs={{0,2},{2,0},{4,6},{6,4},{8,10},{10,8},{12,14},{14,12},{1,3},{3,1},... | collective-permute-start | bytes 1474568 | tf_op jit(solution)/shard_map/ppermute | solution.py:414
  139.8 13.8 %copy-start.5 = (bf16[512,384]{1,0:T(8,128)(2,1)}, bf16[512,384]{1,0:T(8,128)(2,1)S(1)}, u32[]{:S(2)}) copy-start(bf16[512,384]{1,0:T(8,128)(2,1)S(1)} %convolution_convert_fusion) | copy-start | bytes 1179652
  140.1 6.3 %collective-permute-start.37 = (bf16[2,2,48,640]{3,2,0,1:T(8,128)(2,1)S(1)}, bf16[2,2,48,640]{3,2,0,1:T(8,128)(2,1)S(1)}, u32[]{:S(2)}, u32[]{:S(2)}) collective-permute-start(bf16[2,2,48,640]{3,2,0,1:T(8,128)(2,1)S(1)} %slice.250), channel_id=1, source_target_pairs={{0,4},{2,6},{4,0},{6,2},{8,12},{10,14},{12,8},{14,10},{1,5},{3,7},... | collective-permute-start | bytes 737288 | tf_op jit(solution)/shard_map/ppermute | solution.py:440
  140.5 13.1 %collective-permute-start.28 = (bf16[4,208,384]{2,1,0:T(8,128)(2,1)S(1)}, bf16[4,208,384]{2,1,0:T(8,128)(2,1)S(1)}, u32[]{:S(2)}, u32[]{:S(2)}) collective-permute-start(bf16[4,208,384]{2,1,0:T(8,128)(2,1)S(1)} %pad_maximum_fusion.6), channel_id=1, source_target_pairs={{1,3},{3,5},{5,7},{7,9},{9,11},{11,13},{13,15},{17,19},{19,21},{21... | collective-permute-start | bytes 1916936 | tf_op jit(solution)/shard_map/ppermute | solution.py:452
  147.3 7.9 %collective-permute-start.38 = (bf16[2,48,640]{2,1,0:T(8,128)(2,1)S(1)}, bf16[2,48,640]{2,1,0:T(8,128)(2,1)S(1)}, u32[]{:S(2)}, u32[]{:S(2)}) collective-permute-start(bf16[2,48,640]{2,1,0:T(8,128)(2,1)S(1)} %fusion.35), channel_id=1, source_target_pairs={{0,8},{2,10},{4,12},{6,14},{8,0},{10,2},{12,4},{14,6},{1,9},{3,11}... | collective-permute-start | bytes 368648 | tf_op jit(solution)/shard_map/ppermute | solution.py:440
  151.9 6.3 %collective-permute-start.33 = (bf16[4,48,640]{2,1,0:T(8,128)(2,1)S(1)}, bf16[4,48,640]{2,1,0:T(8,128)(2,1)S(1)}, u32[]{:S(2)}, u32[]{:S(2)}) collective-permute-start(bf16[4,48,640]{2,1,0:T(8,128)(2,1)S(1)} %fusion.24), channel_id=1, source_target_pairs={{0,16},{16,0},{1,17},{17,1},{2,18},{18,2},{3,19},{19,3},{4,20},{20... | collective-permute-start | bytes 737288 | tf_op jit(solution)/shard_map/ppermute | solution.py:411
  153.5 6.3 %collective-permute-start.32 = (bf16[4,48,640]{2,1,0:T(8,128)(2,1)S(1)}, bf16[4,48,640]{2,1,0:T(8,128)(2,1)S(1)}, u32[]{:S(2)}, u32[]{:S(2)}) collective-permute-start(bf16[4,48,640]{2,1,0:T(8,128)(2,1)S(1)} %fusion.23), channel_id=1, source_target_pairs={{0,2},{2,0},{4,6},{6,4},{8,10},{10,8},{12,14},{14,12},{1,3},{3,1},... | collective-permute-start | bytes 737288 | tf_op jit(solution)/shard_map/ppermute | solution.py:414
  153.8 0.9 slice-start
  153.8 1.0 slice-start.1
  155.1 15.5 %collective-permute-start.31 = (bf16[4,512,384]{2,1,0:T(8,128)(2,1)S(1)}, bf16[4,512,384]{2,1,0:T(8,128)(2,1)S(1)}, u32[]{:S(2)}, u32[]{:S(2)}) collective-permute-start(bf16[4,512,384]{2,1,0:T(8,128)(2,1)S(1)} %pad_maximum_fusion), channel_id=1, source_target_pairs={{0,1},{1,0},{2,3},{3,2},{4,5},{5,4},{6,7},{7,6},{8,9},{9,8},{10,11... | collective-permute-start | bytes 4718600 | tf_op jit(solution)/shard_map/ppermute | solution.py:408
  160.0 7.3 %collective-permute-start.34 = (bf16[2,48,640]{2,1,0:T(8,128)(2,1)S(1)}, bf16[2,48,640]{2,1,0:T(8,128)(2,1)S(1)}, u32[]{:S(2)}, u32[]{:S(2)}) collective-permute-start(bf16[2,48,640]{2,1,0:T(8,128)(2,1)S(1)} %get-tuple-element.222), channel_id=1, source_target_pairs={{0,4},{2,6},{4,0},{6,2},{8,12},{10,14},{12,8},{14,10},{1,5},{3,7},... | collective-permute-start | bytes 368648 | tf_op jit(solution)/shard_map/ppermute | solution.py:440
  160.1 10.4 %collective-permute-start.35 = (bf16[2,48,640]{2,1,0:T(8,128)(2,1)S(1)}, bf16[2,48,640]{2,1,0:T(8,128)(2,1)S(1)}, u32[]{:S(2)}, u32[]{:S(2)}) collective-permute-start(bf16[2,48,640]{2,1,0:T(8,128)(2,1)S(1)} %get-tuple-element.224), channel_id=1, source_target_pairs={{0,8},{2,10},{4,12},{6,14},{8,0},{10,2},{12,4},{14,6},{1,9},{3,11}... | collective-permute-start | bytes 368648 | tf_op jit(solution)/shard_map/ppermute | solution.py:440
  160.5 10.0 %collective-permute-start.36 = (bf16[2,48,640]{2,1,0:T(8,128)(2,1)S(1)}, bf16[2,48,640]{2,1,0:T(8,128)(2,1)S(1)}, u32[]{:S(2)}, u32[]{:S(2)}) collective-permute-start(bf16[2,48,640]{2,1,0:T(8,128)(2,1)S(1)} %get-tuple-element.223), channel_id=1, source_target_pairs={{0,12},{2,14},{4,8},{6,10},{8,4},{10,6},{12,0},{14,2},{1,13},{3,15... | collective-permute-start | bytes 368648 | tf_op jit(solution)/shard_map/ppermute | solution.py:440
  170.6 4.9 %collective-permute-start.39 = (bf16[48,1280]{1,0:T(8,128)(2,1)S(1)}, bf16[48,1280]{1,0:T(8,128)(2,1)S(1)}, u32[]{:S(2)}, u32[]{:S(2)}) collective-permute-start(bf16[48,1280]{1,0:T(8,128)(2,1)S(1)} %select_convert_fusion), channel_id=1, source_target_pairs={{0,16},{16,0},{1,17},{17,1},{2,18},{18,2},{3,19},{19,3},{4,20},{20... | collective-permute-start | bytes 368648 | tf_op jit(solution)/shard_map/ppermute | solution.py:411
  175.6 0.7 copy-start.7

commit v3 on v1

--- a/solution.py
+++ b/solution.py
@@ -439,9 +439,10 @@
     def pz_to(a, kk):
         return lax.ppermute(a, "dp", [(i, i ^ (2 * kk)) for i in range(n_dp)])
 
-    def along(quad):
+    def along(quad, *before):
         low = quad.astype(BF16)
-        return plus(quad[:, 0], *[pz_to(low[:, kk], kk) for kk in range(1, m)])
+        got = [pz_to(low[:, kk], kk) for kk in range(1, m)]
+        return plus(quad[:, 0], *after(*got, *before)[:m - 1])
 
     def along_steps(quad, *before):
         got = pz_to(quad[:, 1::2].astype(BF16), 1)
@@ -600,10 +601,10 @@
         sent0 = chip_sums([first] + m0["g"][1:], got0)
         in_got, low_got, *quad1 = after(in_got, low_got, *quad1, sent0[1], sent0[3])[:6]
         quad0 = after(*cross_first(sent0))
-        rows = placed([r1["keep"], low_got, b0["keep"], in_got], quad0[1], quad0[3])
-        done1 = along_steps(crossed(quad1), quad0[1], quad0[3])
+        in_got, low_got = after(in_got, low_got, quad0[1], quad0[3])[:2]
+        rows = placed([r1["keep"], low_got, b0["keep"], in_got])
         quad0 = cross_second(quad0)
-        done1, *quad0 = after(done1, *quad0)
+        done1 = along(crossed(quad1), quad0[1], quad0[3])
         twin, done0 = after(pt(rows), along(crossed(quad0)))
         done0, done1 = [jnp.concatenate([a[0], a[1]], 1) for a in (done0, done1)]
         mine = jnp.where(sec == 0, done0, done1)

time: 175 us -> 184 us (1.051)
  waiting for transfers between devices: 59.1 us -> 64.6 us
  starting transfers between devices: 52.7 us -> 56.9 us
    ppermute x11, waiting for transfers between devices: 13.6 us -> 19.1 us  [px(): return lax.ppermute(a, 'section', [(0, 1), (1, 0)])]
    ppermute x10 -> x11, waiting for transfers between devices: 26.6 us -> 21.1 us  [pz_to(): return lax.ppermute(a, 'dp', [(i, i ^ 2 * kk) for i in range(n_dp)])]
    ppermute x7, waiting for transfers between devices: 12.9 us -> 18.4 us  [py(): return lax.ppermute(a, 'dp', [(i, i ^ 1) for i in range(n_dp)])]
    ppermute x15, starting transfers between devices: 2.51 us -> 6.59 us  [pt(): return lax.ppermute(a, 'tensor', [(0, 1), (1, 0)])]
    ppermute x10 -> x11, starting transfers between devices: 19.7 us -> 20.2 us  [pz_to(): return lax.ppermute(a, 'dp', [(i, i ^ 2 * kk) for i in range(n_dp)])]
  transfers between devices with their start and end apart: 48 -> 49, of which waited for: 23 -> 23; matrix products, arithmetic and copies ran while one was open for 7% -> 6% of each run, Pallas kernels for 14% -> 13%
where the time goes in v3:
time: 184 us
  waiting for transfers between devices  64.6 us (35%)
  starting transfers between devices  56.9 us (31%)
  Pallas kernels  45.4 us (25%)
  other arithmetic  6.28 us (3%)
  matrix products  4.52 us (2%)
  local copies, waits for them, and re-layouts  4.43 us (2%)
  between operations  2.07 us (1%)
    pallas_call x5, Pallas kernels, layer_call(): pl.pallas_call(body, out_shape=[jax.ShapeDtypeStruct(*o) for o in outs],...  43.5 us
    ppermute x11, waiting for transfers between devices, pz_to(): return lax.ppermute(a, 'dp', [(i, i ^ 2 * kk) for i in range(n_dp)])  21.1 us
    ppermute x11, starting transfers between devices, pz_to(): return lax.ppermute(a, 'dp', [(i, i ^ 2 * kk) for i in range(n_dp)])  20.2 us
    ppermute x11, waiting for transfers between devices, px(): return lax.ppermute(a, 'section', [(0, 1), (1, 0)])  19.1 us
    ppermute x7, waiting for transfers between devices, py(): return lax.ppermute(a, 'dp', [(i, i ^ 1) for i in range(n_dp)])  18.4 us
    ppermute x11, starting transfers between devices, px(): return lax.ppermute(a, 'section', [(0, 1), (1, 0)])  14.6 us
    ppermute x7, starting transfers between devices, py(): return lax.ppermute(a, 'dp', [(i, i ^ 1) for i in range(n_dp)])  9.9 us
    ppermute x15, starting transfers between devices, pt(): return lax.ppermute(a, 'tensor', [(0, 1), (1, 0)])  6.59 us
  transfers between devices with their start and end apart: 49, of which 23 were waited for; matrix products, arithmetic and copies ran while one was open for 6% of the time, Pallas kernels for 13%

profile of v3, /device:TPU:0, one launch (start us, length us, event | category | flops | bytes accessed | tf_op | source)
XLA Modules:
  0.0 184.2 jit_solution(293210218333651702)
XLA Ops:
  0.7 1.3 constant_dynamic-slice_fusion
  2.1 0.7 collective-permute-start.1
  3.5 3.0 %collective-permute-start = (bf16[48,1280]{1,0:T(8,128)(2,1)S(1)}, bf16[48,1280]{1,0:T(8,128)(2,1)S(1)}, u32[]{:S(2)}, u32[]{:S(2)}) collective-permute-start(bf16[48,1280]{1,0:T(8,128)(2,1)S(1)} %broadcast_select_fusion.3), channel_id=1, source_target_pairs={{0,16},{16,0},{1,17},{17,1},{2,18},{18,2},{3,19},{19,3},{4,20},{20... | collective-permute-start | bytes 368648 | tf_op jit(solution)/shard_map/ppermute | solution.py:411
  6.5 3.9 %collective-permute-done = bf16[48,1280]{1,0:T(8,128)(2,1)S(1)} collective-permute-done((bf16[48,1280]{1,0:T(8,128)(2,1)S(1)}, bf16[48,1280]{1,0:T(8,128)(2,1)S(1)}, u32[]{:S(2)}, u32[]{:S(2)}) %collective-permute-start) | collective-permute-done | bytes 122912 | tf_op jit(solution)/shard_map/ppermute | solution.py:411
  10.5 1.2 collective-permute-start.2
  11.7 2.6 %collective-permute-start.3 = (bf16[48,1280]{1,0:T(8,128)(2,1)S(1)}, bf16[48,1280]{1,0:T(8,128)(2,1)S(1)}, u32[]{:S(2)}, u32[]{:S(2)}) collective-permute-start(bf16[48,1280]{1,0:T(8,128)(2,1)S(1)} %get-tuple-element.239), channel_id=1, source_target_pairs={{0,8},{2,10},{4,12},{6,14},{8,0},{10,2},{12,4},{14,6},{1,9},{3,11}... | collective-permute-start | bytes 368648 | tf_op jit(solution)/shard_map/ppermute | solution.py:440
  14.3 0.7 collective-permute-start.4
  15.0 1.8 collective-permute-start.6
  16.8 1.7 collective-permute-start.7
  18.6 3.1 %collective-permute-start.8 = (bf16[2,48,1280]{2,1,0:T(8,128)(2,1)S(1)}, bf16[2,48,1280]{2,1,0:T(8,128)(2,1)S(1)}, u32[]{:S(2)}, u32[]{:S(2)}) collective-permute-start(bf16[2,48,1280]{2,1,0:T(8,128)(2,1)S(1)} %pad_maximum_fusion.8.refs_2_.refs_3_.refs_13_), channel_id=1, source_target_pairs={{0,18},{2,16},{4,22},{6,20},{8,26},{10,24},{12,30},{14,28},{16,2},... | collective-permute-start | bytes 737288 | tf_op jit(solution)/shard_map/ppermute | solution.py:417
  21.7 2.4 %collective-permute-done.3 = bf16[48,1280]{1,0:T(8,128)(2,1)S(1)} collective-permute-done((bf16[48,1280]{1,0:T(8,128)(2,1)S(1)}, bf16[48,1280]{1,0:T(8,128)(2,1)S(1)}, u32[]{:S(2)}, u32[]{:S(2)}) %collective-permute-start.3) | collective-permute-done | bytes 122912 | tf_op jit(solution)/shard_map/ppermute | solution.py:440
  24.1 3.1 %collective-permute-start.5 = (bf16[48,1280]{1,0:T(8,128)(2,1)S(1)}, bf16[48,1280]{1,0:T(8,128)(2,1)S(1)}, u32[]{:S(2)}, u32[]{:S(2)}) collective-permute-start(bf16[48,1280]{1,0:T(8,128)(2,1)S(1)} %get-tuple-element.116), channel_id=1, source_target_pairs={{0,4},{2,6},{4,0},{6,2},{8,12},{10,14},{12,8},{14,10},{1,5},{3,7},... | collective-permute-start | bytes 368648 | tf_op jit(solution)/shard_map/ppermute | solution.py:440
  27.3 3.5 %collective-permute-done.5 = bf16[48,1280]{1,0:T(8,128)(2,1)S(1)} collective-permute-done((bf16[48,1280]{1,0:T(8,128)(2,1)S(1)}, bf16[48,1280]{1,0:T(8,128)(2,1)S(1)}, u32[]{:S(2)}, u32[]{:S(2)}) %collective-permute-start.5) | collective-permute-done | bytes 122912 | tf_op jit(solution)/shard_map/ppermute | solution.py:440
  30.8 2.8 %collective-permute-start.9 = (bf16[2,48,1280]{2,1,0:T(8,128)(2,1)S(1)}, bf16[2,48,1280]{2,1,0:T(8,128)(2,1)S(1)}, u32[]{:S(2)}, u32[]{:S(2)}) collective-permute-start(bf16[2,48,1280]{2,1,0:T(8,128)(2,1)S(1)} %pad_maximum_fusion.9), channel_id=1, source_target_pairs={{0,8},{2,10},{4,12},{6,14},{8,0},{10,2},{12,4},{14,6},{1,9},{3,11}... | collective-permute-start | bytes 737288 | tf_op jit(solution)/shard_map/ppermute | solution.py:440
  35.0 1.6 collective-permute-start.10
  36.5 2.4 %collective-permute-start.11 = (bf16[3,48,1280]{2,1,0:T(8,128)(2,1)S(1)}, bf16[3,48,1280]{2,1,0:T(8,128)(2,1)S(1)}, u32[]{:S(2)}, u32[]{:S(2)}) collective-permute-start(bf16[3,48,1280]{2,1,0:T(8,128)(2,1)S(1)} %pad_maximum_fusion.5.refs_6_.refs_17_), channel_id=1, source_target_pairs={{0,2},{2,0},{4,6},{6,4},{8,10},{10,8},{12,14},{14,12},{1,3},{3,1},... | collective-permute-start | bytes 1105928 | tf_op jit(solution)/shard_map/ppermute | solution.py:414
  38.9 5.3 %collective-permute-done.9 = bf16[2,48,1280]{2,1,0:T(8,128)(2,1)S(1)} collective-permute-done((bf16[2,48,1280]{2,1,0:T(8,128)(2,1)S(1)}, bf16[2,48,1280]{2,1,0:T(8,128)(2,1)S(1)}, u32[]{:S(2)}, u32[]{:S(2)}) %collective-permute-start.9) | collective-permute-done | bytes 245792 | tf_op jit(solution)/shard_map/ppermute | solution.py:440
  44.4 2.1 %collective-permute-done.10.refs_7_.refs_18_ = bf16[3,48,1280]{2,1,0:T(8,128)(2,1)S(1)} collective-permute-done((bf16[3,48,1280]{2,1,0:T(8,128)(2,1)S(1)}, bf16[3,48,1280]{2,1,0:T(8,128)(2,1)S(1)}, u32[]{:S(2)}, u32[]{:S(2)}) %collective-permute-start.10) | collective-permute-done | bytes 368672 | tf_op jit(solution)/shard_map/ppermute | solution.py:411
  46.5 6.9 %collective-permute-done.11.refs_8_.refs_19_ = bf16[3,48,1280]{2,1,0:T(8,128)(2,1)S(1)} collective-permute-done((bf16[3,48,1280]{2,1,0:T(8,128)(2,1)S(1)}, bf16[3,48,1280]{2,1,0:T(8,128)(2,1)S(1)}, u32[]{:S(2)}, u32[]{:S(2)}) %collective-permute-start.11) | collective-permute-done | bytes 368672 | tf_op jit(solution)/shard_map/ppermute | solution.py:414
  53.4 0.7 collective-permute-done.12.refs_9_.refs_20_
  56.4 1.3 collective-permute-done.16.refs_13_.refs_14_.refs_24_
  57.8 1.5 collective-permute-start.21
  59.2 0.8 collective-permute-start.22
  60.1 1.2 collective-permute-start.23
  61.3 8.6 %shard_map.186 = (bf16[416,384]{1,0:T(8,128)(2,1)S(1)}, f32[416,384]{1,0:T(8,128)S(1)}, f32[416,128]{1,0:T(8,128)S(1)}, bf16[416,384]{1,0:T(8,128)(2,1)S(1)}, bf...) custom-call(s32[5]{0:T(128)S(1)} %stack.113.refs_0_.sc, ...), custom_call_target="tpu_custom_call" | custom-call | flops 10000000000 | bytes 8388608 | tf_op jit(solution)/shard_map/pallas_call | solution.py:342
  69.9 6.0 %collective-permute-done.22.refs_9_ = bf16[3,48,1280]{2,1,0:T(8,128)(2,1)S(1)} collective-permute-done((bf16[3,48,1280]{2,1,0:T(8,128)(2,1)S(1)}, bf16[3,48,1280]{2,1,0:T(8,128)(2,1)S(1)}, u32[]{:S(2)}, u32[]{:S(2)}) %collective-permute-start.22) | collective-permute-done | bytes 368672 | tf_op jit(solution)/shard_map/ppermute | solution.py:414
  75.9 1.6 collective-permute-done.23.refs_10_
  78.5 0.7 collective-permute-done.24.refs_15_
  80.8 18.7 %shard_map.187 = (bf16[416,384]{1,0:T(8,128)(2,1)S(1)}, bf16[2,416,256]{2,1,0:T(8,128)(2,1)S(1)}, bf16[416,384]{1,0:T(8,128)(2,1)S(1)}, bf16[416,1536]{1,0:T(8,1...) custom-call(s32[5]{0:T(128)S(1)} %stack.113.refs_0_.sc, ...), custom_call_target="tpu_custom_call" | custom-call | flops 30000001024 | bytes 8388608 | tf_op jit(solution)/shard_map/pallas_call | solution.py:342
  100.0 0.6 collective-permute-start.30
  101.5 2.2 %shard_map.188 = (bf16[2,4,48,640]{3,2,1,0:T(8,128)(2,1)S(1)}, bf16[2,4,48,640]{3,2,1,0:T(8,128)(2,1)S(1)}, bf16[2,4,48,640]{3,2,1,0:T(8,128)(2,1)S(1)}, bf16[2,4,48,640]{3,2,1,0:T(8,128)(2,1)S(1)}) custom-call(s32[5]{0:T(128)S(1)} %stack.113.refs_0_.sc, bf16[416,384]{1,0:T(8,128)(2,1)S(1)} %get-tuple-element.137.refs_1_, ...), custom_call_target="tpu_custom_call" | custom-call | flops 10000000000 | bytes 8388608 | tf_op jit(solution)/shard_map/pallas_call | solution.py:342
  104.2 1.5 collective-permute-start.31
  105.7 0.8 collective-permute-start.32
  106.6 11.8 %shard_map.189 = (bf16[416,384]{1,0:T(8,128)(2,1)S(1)}, bf16[416,384]{1,0:T(8,128)(2,1)S(1)}, bf16[416,384]{1,0:T(8,128)(2,1)S(1)}, bf16[416,1536]{1,0:T(8,128)(...) custom-call(s32[5]{0:T(128)S(1)} %stack.113.refs_0_.sc, ...), custom_call_target="tpu_custom_call" | custom-call | flops 20000000000 | bytes 8388608 | tf_op jit(solution)/shard_map/pallas_call | solution.py:342
  118.4 1.6 collective-permute-start.29
  121.1 0.6 collective-permute-start.34
  121.8 1.7 collective-permute-start.33
  123.6 2.2 %shard_map.190 = (bf16[2,4,48,640]{3,2,1,0:T(8,128)(2,1)S(1)}, bf16[2,4,48,640]{3,2,1,0:T(8,128)(2,1)S(1)}, bf16[2,4,48,640]{3,2,1,0:T(8,128)(2,1)S(1)}, bf16[2,4,48,640]{3,2,1,0:T(8,128)(2,1)S(1)}) custom-call(s32[5]{0:T(128)S(1)} %stack.113.refs_0_.sc, bf16[416,384]{1,0:T(8,128)(2,1)S(1)} %get-tuple-element.155.refs_4_.refs_1_, ...), custom_call_target="tpu_custom_call" | custom-call | flops 10000000000 | bytes 8388608 | tf_op jit(solution)/shard_map/pallas_call | solution.py:342
  126.5 1.7 collective-permute-start.37
  128.2 0.7 collective-permute-done.29
  128.8 5.3 %collective-permute-done.34 = bf16[4,48,640]{2,1,0:T(8,128)(2,1)S(1)} collective-permute-done((bf16[4,48,640]{2,1,0:T(8,128)(2,1)S(1)}, bf16[4,48,640]{2,1,0:T(8,128)(2,1)S(1)}, u32[]{:S(2)}, u32[]{:S(2)}) %collective-permute-start.34) | collective-permute-done | bytes 245792 | tf_op jit(solution)/shard_map/ppermute | solution.py:411
  134.3 0.6 collective-permute-start.45
  135.0 1.4 collective-permute-start.46
  136.3 2.5 %collective-permute-start.47 = (bf16[2,48,640]{2,1,0:T(8,128)(2,1)S(1)}, bf16[2,48,640]{2,1,0:T(8,128)(2,1)S(1)}, u32[]{:S(2)}, u32[]{:S(2)}) collective-permute-start(bf16[2,48,640]{2,1,0:T(8,128)(2,1)S(1)} %get-tuple-element.232), channel_id=1, source_target_pairs={{0,12},{2,14},{4,8},{6,10},{8,4},{10,6},{12,0},{14,2},{1,13},{3,15... | collective-permute-start | bytes 368648 | tf_op jit(solution)/shard_map/ppermute | solution.py:440
  138.8 4.4 %collective-permute-done.36 = bf16[2,4,48,640]{3,2,1,0:T(8,128)(2,1)S(1)} collective-permute-done((bf16[2,4,48,640]{3,2,1,0:T(8,128)(2,1)S(1)}, bf16[2,4,48,640]{3,2,1,0:T(8,128)(2,1)S(1)}, u32[]{:S(2)}, u32[]{:S(2)}) %collective-permute-start.36) | collective-permute-done | bytes 491552 | tf_op jit(solution)/shard_map/ppermute | solution.py:411
  143.4 1.6 collective-permute-start.41
  145.9 0.7 collective-permute-start.38
  147.2 0.7 collective-permute-start.40
  148.4 1.6 collective-permute-done.41
  150.0 5.4 %collective-permute-done.40 = bf16[4,48,640]{2,1,0:T(8,128)(2,1)S(1)} collective-permute-done((bf16[4,48,640]{2,1,0:T(8,128)(2,1)S(1)}, bf16[4,48,640]{2,1,0:T(8,128)(2,1)S(1)}, u32[]{:S(2)}, u32[]{:S(2)}) %collective-permute-start.40) | collective-permute-done | bytes 245792 | tf_op jit(solution)/shard_map/ppermute | solution.py:414
  155.7 0.8 slice-done
  156.9 4.2 %collective-permute-start.39 = (bf16[4,512,384]{2,1,0:T(8,128)(2,1)S(1)}, bf16[4,512,384]{2,1,0:T(8,128)(2,1)S(1)}, u32[]{:S(2)}, u32[]{:S(2)}) collective-permute-start(bf16[4,512,384]{2,1,0:T(8,128)(2,1)S(1)} %pad_maximum_fusion), channel_id=1, source_target_pairs={{0,1},{1,0},{2,3},{3,2},{4,5},{5,4},{6,7},{7,6},{8,9},{9,8},{10,11... | collective-permute-start | bytes 4718600 | tf_op jit(solution)/shard_map/ppermute | solution.py:408
  161.3 2.9 %collective-permute-start.42 = (bf16[2,48,640]{2,1,0:T(8,128)(2,1)S(1)}, bf16[2,48,640]{2,1,0:T(8,128)(2,1)S(1)}, u32[]{:S(2)}, u32[]{:S(2)}) collective-permute-start(bf16[2,48,640]{2,1,0:T(8,128)(2,1)S(1)} %get-tuple-element.237), channel_id=1, source_target_pairs={{0,4},{2,6},{4,0},{6,2},{8,12},{10,14},{12,8},{14,10},{1,5},{3,7},... | collective-permute-start | bytes 368648 | tf_op jit(solution)/shard_map/ppermute | solution.py:440
  164.2 1.3 collective-permute-start.43
  165.6 1.1 collective-permute-start.44
  166.8 2.5 %collective-permute-done.42 = bf16[2,48,640]{2,1,0:T(8,128)(2,1)S(1)} collective-permute-done((bf16[2,48,640]{2,1,0:T(8,128)(2,1)S(1)}, bf16[2,48,640]{2,1,0:T(8,128)(2,1)S(1)}, u32[]{:S(2)}, u32[]{:S(2)}) %collective-permute-start.42) | collective-permute-done | bytes 122912 | tf_op jit(solution)/shard_map/ppermute | solution.py:440
  169.3 7.3 %collective-permute-done.43 = bf16[2,48,640]{2,1,0:T(8,128)(2,1)S(1)} collective-permute-done((bf16[2,48,640]{2,1,0:T(8,128)(2,1)S(1)}, bf16[2,48,640]{2,1,0:T(8,128)(2,1)S(1)}, u32[]{:S(2)}, u32[]{:S(2)}) %collective-permute-start.43) | collective-permute-done | bytes 122912 | tf_op jit(solution)/shard_map/ppermute | solution.py:440
  176.7 0.6 collective-permute-start.48
  177.6 1.2 fusion.13
  178.8 1.0 fusion.11
  179.9 0.7 fusion.36.mine_ref
  180.6 1.1 collective-permute-done.48.other_ref
  181.7 0.6 copy-done.4
  182.3 1.9 %shard_map.191 = (f32[2,48]{1,0:T(2,128)}, f32[4,48]{1,0:T(4,128)}, f32[3,48,192]{2,1,0:T(8,128)}, f32[2,192]{1,0:T(2,128)}, f32[48,192]{1,0:T(8,128)}, /*index=...) custom-call(s32[5]{0:T(128)} %copy-done, f32[48,1280]{1,0:T(8,128)} %fusion.36.mine_ref, bf16[48,1280]{1,0:T(8,128)(2,1)} %copy-done.4), custom_call_target="tpu_custom_call" | custom-call | tf_op jit(solution)/shard_map/pallas_call | solution.py:385
  (146 shorter events, 14.0 us)
Async XLA Ops:
  0.7 2.1 %copy-start.7 = (bf16[1,192,48]{1,2,0:T(8,128)(2,1)S(1)}, bf16[1,192,48]{1,2,0:T(8,128)(2,1)}, u32[]{:S(2)}) copy-start(bf16[1,192,48]{1,2,0:T(8,128)(2,1)} %param.18) | copy-start | bytes 55300
  0.7 2.1 %copy-start.3 = (bf16[1,48,3,192]{3,1,2,0:T(8,128)(2,1)S(1)}, bf16[1,48,3,192]{3,1,2,0:T(8,128)(2,1)}, u32[]{:S(2)}) copy-start(bf16[1,48,3,192]{3,1,2,0:T(8,128)(2,1)} %param.16) | copy-start | bytes 165892
  0.7 2.2 %copy-start.10 = (bf16[1,4,48]{2,1,0:T(4,128)(2,1)S(1)}, bf16[1,4,48]{2,1,0:T(4,128)(2,1)}, u32[]{:S(2)}) copy-start(bf16[1,4,48]{2,1,0:T(4,128)(2,1)} %param.15) | copy-start | bytes 1156
  0.7 2.2 %copy-start.11 = (bf16[1,2,48]{2,1,0:T(2,128)(2,1)S(1)}, bf16[1,2,48]{2,1,0:T(2,128)(2,1)}, u32[]{:S(2)}) copy-start(bf16[1,2,48]{2,1,0:T(2,128)(2,1)} %param.14) | copy-start | bytes 580
  0.7 2.3 %copy-start.8 = (bf16[1,2,192]{2,1,0:T(2,128)(2,1)S(1)}, bf16[1,2,192]{2,1,0:T(2,128)(2,1)}, u32[]{:S(2)}) copy-start(bf16[1,2,192]{2,1,0:T(2,128)(2,1)} %param.17) | copy-start | bytes 2308
  0.7 2.4 %copy-start.9 = (bf16[1,768]{1,0:T(2,128)(2,1)S(1)}, bf16[1,768]{1,0:T(2,128)(2,1)}, u32[]{:S(2)}) copy-start(bf16[1,768]{1,0:T(2,128)(2,1)} %param.20) | copy-start | bytes 4612
  0.7 2.5 %copy-start.5 = (bf16[1,768,48]{1,2,0:T(8,128)(2,1)S(1)}, bf16[1,768,48]{1,2,0:T(8,128)(2,1)}, u32[]{:S(2)}) copy-start(bf16[1,768,48]{1,2,0:T(8,128)(2,1)} %param.21) | copy-start | bytes 221188
  0.7 2.6 %copy-start.6 = (bf16[1,48,768]{2,1,0:T(8,128)(2,1)S(1)}, bf16[1,48,768]{2,1,0:T(8,128)(2,1)}, u32[]{:S(2)}) copy-start(bf16[1,48,768]{2,1,0:T(8,128)(2,1)} %param.19) | copy-start | bytes 221188
  2.1 8.4 %collective-permute-start.1 = (bf16[2,208,384]{2,1,0:T(8,128)(2,1)S(1)}, bf16[2,208,384]{2,1,0:T(8,128)(2,1)S(1)}, u32[]{:S(2)}, u32[]{:S(2)}) collective-permute-start(bf16[2,208,384]{2,1,0:T(8,128)(2,1)S(1)} %pad_maximum_fusion.7), channel_id=1, source_target_pairs={{3,1},{5,3},{7,5},{9,7},{11,9},{13,11},{15,13},{19,17},{21,19},{23... | collective-permute-start | bytes 958472 | tf_op jit(solution)/shard_map/ppermute | solution.py:489
  3.5 30.1 %copy-start.12 = (s32[2]{0:T(128)S(1)}, s32[2]{0:T(128)}, u32[]{:S(2)}) copy-start(s32[2]{0:T(128)} %param.12) | copy-start | bytes 28
  3.5 7.0 %collective-permute-start = (bf16[48,1280]{1,0:T(8,128)(2,1)S(1)}, bf16[48,1280]{1,0:T(8,128)(2,1)S(1)}, u32[]{:S(2)}, u32[]{:S(2)}) collective-permute-start(bf16[48,1280]{1,0:T(8,128)(2,1)S(1)} %broadcast_select_fusion.3), channel_id=1, source_target_pairs={{0,16},{16,0},{1,17},{17,1},{2,18},{18,2},{3,19},{19,3},{4,20},{20... | collective-permute-start | bytes 368648 | tf_op jit(solution)/shard_map/ppermute | solution.py:411
  10.5 8.2 %collective-permute-start.2 = (bf16[48,1280]{1,0:T(8,128)(2,1)S(1)}, bf16[48,1280]{1,0:T(8,128)(2,1)S(1)}, u32[]{:S(2)}, u32[]{:S(2)}) collective-permute-start(bf16[48,1280]{1,0:T(8,128)(2,1)S(1)} %get-tuple-element.239), channel_id=1, source_target_pairs={{0,4},{2,6},{4,0},{6,2},{8,12},{10,14},{12,8},{14,10},{1,5},{3,7},... | collective-permute-start | bytes 368648 | tf_op jit(solution)/shard_map/ppermute | solution.py:440
  11.7 12.4 %collective-permute-start.3 = (bf16[48,1280]{1,0:T(8,128)(2,1)S(1)}, bf16[48,1280]{1,0:T(8,128)(2,1)S(1)}, u32[]{:S(2)}, u32[]{:S(2)}) collective-permute-start(bf16[48,1280]{1,0:T(8,128)(2,1)S(1)} %get-tuple-element.239), channel_id=1, source_target_pairs={{0,8},{2,10},{4,12},{6,14},{8,0},{10,2},{12,4},{14,6},{1,9},{3,11}... | collective-permute-start | bytes 368648 | tf_op jit(solution)/shard_map/ppermute | solution.py:440
  14.3 9.8 %collective-permute-start.4 = (bf16[48,1280]{1,0:T(8,128)(2,1)S(1)}, bf16[48,1280]{1,0:T(8,128)(2,1)S(1)}, u32[]{:S(2)}, u32[]{:S(2)}) collective-permute-start(bf16[48,1280]{1,0:T(8,128)(2,1)S(1)} %get-tuple-element.239), channel_id=1, source_target_pairs={{0,12},{2,14},{4,8},{6,10},{8,4},{10,6},{12,0},{14,2},{1,13},{3,15... | collective-permute-start | bytes 368648 | tf_op jit(solution)/shard_map/ppermute | solution.py:440
  15.0 15.8 %collective-permute-start.6 = (bf16[2,48,1280]{2,1,0:T(8,128)(2,1)S(1)}, bf16[2,48,1280]{2,1,0:T(8,128)(2,1)S(1)}, u32[]{:S(2)}, u32[]{:S(2)}) collective-permute-start(bf16[2,48,1280]{2,1,0:T(8,128)(2,1)S(1)} %pad_maximum_fusion.8.refs_2_.refs_3_.refs_13_), channel_id=1, source_target_pairs={{0,16},{16,0},{1,17},{17,1},{2,18},{18,2},{3,19},{19,3},{4,20},{20... | collective-permute-start | bytes 737288 | tf_op jit(solution)/shard_map/ppermute | solution.py:411
  16.8 14.0 %collective-permute-start.7 = (bf16[2,48,1280]{2,1,0:T(8,128)(2,1)S(1)}, bf16[2,48,1280]{2,1,0:T(8,128)(2,1)S(1)}, u32[]{:S(2)}, u32[]{:S(2)}) collective-permute-start(bf16[2,48,1280]{2,1,0:T(8,128)(2,1)S(1)} %pad_maximum_fusion.8.refs_2_.refs_3_.refs_13_), channel_id=1, source_target_pairs={{0,2},{2,0},{4,6},{6,4},{8,10},{10,8},{12,14},{14,12},{1,3},{3,1},... | collective-permute-start | bytes 737288 | tf_op jit(solution)/shard_map/ppermute | solution.py:414
  18.6 12.1 %collective-permute-start.8 = (bf16[2,48,1280]{2,1,0:T(8,128)(2,1)S(1)}, bf16[2,48,1280]{2,1,0:T(8,128)(2,1)S(1)}, u32[]{:S(2)}, u32[]{:S(2)}) collective-permute-start(bf16[2,48,1280]{2,1,0:T(8,128)(2,1)S(1)} %pad_maximum_fusion.8.refs_2_.refs_3_.refs_13_), channel_id=1, source_target_pairs={{0,18},{2,16},{4,22},{6,20},{8,26},{10,24},{12,30},{14,28},{16,2},... | collective-permute-start | bytes 737288 | tf_op jit(solution)/shard_map/ppermute | solution.py:417
  24.1 6.6 %collective-permute-start.5 = (bf16[48,1280]{1,0:T(8,128)(2,1)S(1)}, bf16[48,1280]{1,0:T(8,128)(2,1)S(1)}, u32[]{:S(2)}, u32[]{:S(2)}) collective-permute-start(bf16[48,1280]{1,0:T(8,128)(2,1)S(1)} %get-tuple-element.116), channel_id=1, source_target_pairs={{0,4},{2,6},{4,0},{6,2},{8,12},{10,14},{12,8},{14,10},{1,5},{3,7},... | collective-permute-start | bytes 368648 | tf_op jit(solution)/shard_map/ppermute | solution.py:440
  30.8 13.5 %collective-permute-start.9 = (bf16[2,48,1280]{2,1,0:T(8,128)(2,1)S(1)}, bf16[2,48,1280]{2,1,0:T(8,128)(2,1)S(1)}, u32[]{:S(2)}, u32[]{:S(2)}) collective-permute-start(bf16[2,48,1280]{2,1,0:T(8,128)(2,1)S(1)} %pad_maximum_fusion.9), channel_id=1, source_target_pairs={{0,8},{2,10},{4,12},{6,14},{8,0},{10,2},{12,4},{14,6},{1,9},{3,11}... | collective-permute-start | bytes 737288 | tf_op jit(solution)/shard_map/ppermute | solution.py:440
  34.9 88.7 %copy-start = (s32[5]{0:T(128)}, s32[5]{0:T(128)S(1)}, u32[]{:S(2)}) copy-start(s32[5]{0:T(128)S(1)} %stack.113.refs_0_.sc) | copy-start | bytes 64
  35.0 11.5 %collective-permute-start.10 = (bf16[3,48,1280]{2,1,0:T(8,128)(2,1)S(1)}, bf16[3,48,1280]{2,1,0:T(8,128)(2,1)S(1)}, u32[]{:S(2)}, u32[]{:S(2)}) collective-permute-start(bf16[3,48,1280]{2,1,0:T(8,128)(2,1)S(1)} %pad_maximum_fusion.5.refs_6_.refs_17_), channel_id=1, source_target_pairs={{0,16},{16,0},{1,17},{17,1},{2,18},{18,2},{3,19},{19,3},{4,20},{20... | collective-permute-start | bytes 1105928 | tf_op jit(solution)/shard_map/ppermute | solution.py:411
  36.5 16.9 %collective-permute-start.11 = (bf16[3,48,1280]{2,1,0:T(8,128)(2,1)S(1)}, bf16[3,48,1280]{2,1,0:T(8,128)(2,1)S(1)}, u32[]{:S(2)}, u32[]{:S(2)}) collective-permute-start(bf16[3,48,1280]{2,1,0:T(8,128)(2,1)S(1)} %pad_maximum_fusion.5.refs_6_.refs_17_), channel_id=1, source_target_pairs={{0,2},{2,0},{4,6},{6,4},{8,10},{10,8},{12,14},{14,12},{1,3},{3,1},... | collective-permute-start | bytes 1105928 | tf_op jit(solution)/shard_map/ppermute | solution.py:414
  38.9 15.2 %collective-permute-start.12 = (bf16[3,48,1280]{2,1,0:T(8,128)(2,1)S(1)}, bf16[3,48,1280]{2,1,0:T(8,128)(2,1)S(1)}, u32[]{:S(2)}, u32[]{:S(2)}) collective-permute-start(bf16[3,48,1280]{2,1,0:T(8,128)(2,1)S(1)} %pad_maximum_fusion.5.refs_6_.refs_17_), channel_id=1, source_target_pairs={{0,18},{2,16},{4,22},{6,20},{8,26},{10,24},{12,30},{14,28},{16,2},... | collective-permute-start | bytes 1105928 | tf_op jit(solution)/shard_map/ppermute | solution.py:417
  38.9 15.7 %collective-permute-start.13 = (bf16[2,48,1280]{2,1,0:T(8,128)(2,1)S(1)}, bf16[2,48,1280]{2,1,0:T(8,128)(2,1)S(1)}, u32[]{:S(2)}, u32[]{:S(2)}) collective-permute-start(bf16[2,48,1280]{2,1,0:T(8,128)(2,1)S(1)} %pad_maximum_fusion.8.refs_2_.refs_3_.refs_13_), channel_id=1, source_target_pairs={{0,1},{1,0},{2,3},{3,2},{4,5},{5,4},{6,7},{7,6},{8,9},{9,8},{10,11... | collective-permute-start | bytes 737288 | tf_op jit(solution)/shard_map/ppermute | solution.py:408
  44.2 10.4 %collective-permute-start.14 = (bf16[2,48,1280]{2,1,0:T(8,128)(2,1)S(1)}, bf16[2,48,1280]{2,1,0:T(8,128)(2,1)S(1)}, u32[]{:S(2)}, u32[]{:S(2)}) collective-permute-start(bf16[2,48,1280]{2,1,0:T(8,128)(2,1)S(1)} %collective-permute-done.6.refs_3_.refs_4_.refs_14_), channel_id=1, source_target_pairs={{0,1},{1,0},{2,3},{3,2},{4,5},{5,4},{6,7},{7,6},{8,9},{9,8},{10,11... | collective-permute-start | bytes 737288 | tf_op jit(solution)/shard_map/ppermute | solution.py:408
  46.5 9.3 %collective-permute-start.15 = (bf16[2,48,1280]{2,1,0:T(8,128)(2,1)S(1)}, bf16[2,48,1280]{2,1,0:T(8,128)(2,1)S(1)}, u32[]{:S(2)}, u32[]{:S(2)}) collective-permute-start(bf16[2,48,1280]{2,1,0:T(8,128)(2,1)S(1)} %collective-permute-done.7.refs_4_.refs_5_.refs_15_), channel_id=1, source_target_pairs={{0,1},{1,0},{2,3},{3,2},{4,5},{5,4},{6,7},{7,6},{8,9},{9,8},{10,11... | collective-permute-start | bytes 737288 | tf_op jit(solution)/shard_map/ppermute | solution.py:408
  54.2 5.1 %collective-permute-start.17 = (bf16[3,48,1280]{2,1,0:T(8,128)(2,1)S(1)}, bf16[3,48,1280]{2,1,0:T(8,128)(2,1)S(1)}, u32[]{:S(2)}, u32[]{:S(2)}) collective-permute-start(bf16[3,48,1280]{2,1,0:T(8,128)(2,1)S(1)} %pad_maximum_fusion.5.refs_6_.refs_17_), channel_id=1, source_target_pairs={{0,1},{1,0},{2,3},{3,2},{4,5},{5,4},{6,7},{7,6},{8,9},{9,8},{10,11... | collective-permute-start | bytes 1105928 | tf_op jit(solution)/shard_map/ppermute | solution.py:408
  54.2 5.9 %collective-permute-start.18 = (bf16[3,48,1280]{2,1,0:T(8,128)(2,1)S(1)}, bf16[3,48,1280]{2,1,0:T(8,128)(2,1)S(1)}, u32[]{:S(2)}, u32[]{:S(2)}) collective-permute-start(bf16[3,48,1280]{2,1,0:T(8,128)(2,1)S(1)} %collective-permute-done.10.refs_7_.refs_18_), channel_id=1, source_target_pairs={{0,1},{1,0},{2,3},{3,2},{4,5},{5,4},{6,7},{7,6},{8,9},{9,8},{10,11... | collective-permute-start | bytes 1105928 | tf_op jit(solution)/shard_map/ppermute | solution.py:408
  54.7 6.6 %collective-permute-start.19 = (bf16[3,48,1280]{2,1,0:T(8,128)(2,1)S(1)}, bf16[3,48,1280]{2,1,0:T(8,128)(2,1)S(1)}, u32[]{:S(2)}, u32[]{:S(2)}) collective-permute-start(bf16[3,48,1280]{2,1,0:T(8,128)(2,1)S(1)} %collective-permute-done.11.refs_8_.refs_19_), channel_id=1, source_target_pairs={{0,1},{1,0},{2,3},{3,2},{4,5},{5,4},{6,7},{7,6},{8,9},{9,8},{10,11... | collective-permute-start | bytes 1105928 | tf_op jit(solution)/shard_map/ppermute | solution.py:408
  54.7 6.6 %collective-permute-start.20 = (bf16[3,48,1280]{2,1,0:T(8,128)(2,1)S(1)}, bf16[3,48,1280]{2,1,0:T(8,128)(2,1)S(1)}, u32[]{:S(2)}, u32[]{:S(2)}) collective-permute-start(bf16[3,48,1280]{2,1,0:T(8,128)(2,1)S(1)} %collective-permute-done.12.refs_9_.refs_20_), channel_id=1, source_target_pairs={{0,1},{1,0},{2,3},{3,2},{4,5},{5,4},{6,7},{7,6},{8,9},{9,8},{10,11... | collective-permute-start | bytes 1105928 | tf_op jit(solution)/shard_map/ppermute | solution.py:408
  55.7 2.0 %collective-permute-start.16 = (bf16[2,48,1280]{2,1,0:T(8,128)(2,1)S(1)}, bf16[2,48,1280]{2,1,0:T(8,128)(2,1)S(1)}, u32[]{:S(2)}, u32[]{:S(2)}) collective-permute-start(bf16[2,48,1280]{2,1,0:T(8,128)(2,1)S(1)} %collective-permute-done.8.refs_5_.refs_6_.refs_16_), channel_id=1, source_target_pairs={{0,1},{1,0},{2,3},{3,2},{4,5},{5,4},{6,7},{7,6},{8,9},{9,8},{10,11... | collective-permute-start | bytes 737288 | tf_op jit(solution)/shard_map/ppermute | solution.py:408
  57.8 12.1 %collective-permute-start.21 = (bf16[3,48,1280]{2,1,0:T(8,128)(2,1)S(1)}, bf16[3,48,1280]{2,1,0:T(8,128)(2,1)S(1)}, u32[]{:S(2)}, u32[]{:S(2)}) collective-permute-start(bf16[3,48,1280]{2,1,0:T(8,128)(2,1)S(1)} %pad_maximum_fusion.6.refs_7_), channel_id=1, source_target_pairs={{0,16},{16,0},{1,17},{17,1},{2,18},{18,2},{3,19},{19,3},{4,20},{20... | collective-permute-start | bytes 1105928 | tf_op jit(solution)/shard_map/ppermute | solution.py:411
  59.2 16.6 %collective-permute-start.22 = (bf16[3,48,1280]{2,1,0:T(8,128)(2,1)S(1)}, bf16[3,48,1280]{2,1,0:T(8,128)(2,1)S(1)}, u32[]{:S(2)}, u32[]{:S(2)}) collective-permute-start(bf16[3,48,1280]{2,1,0:T(8,128)(2,1)S(1)} %pad_maximum_fusion.6.refs_7_), channel_id=1, source_target_pairs={{0,2},{2,0},{4,6},{6,4},{8,10},{10,8},{12,14},{14,12},{1,3},{3,1},... | collective-permute-start | bytes 1105928 | tf_op jit(solution)/shard_map/ppermute | solution.py:414
  60.1 17.4 %collective-permute-start.23 = (bf16[3,48,1280]{2,1,0:T(8,128)(2,1)S(1)}, bf16[3,48,1280]{2,1,0:T(8,128)(2,1)S(1)}, u32[]{:S(2)}, u32[]{:S(2)}) collective-permute-start(bf16[3,48,1280]{2,1,0:T(8,128)(2,1)S(1)} %pad_maximum_fusion.6.refs_7_), channel_id=1, source_target_pairs={{0,18},{2,16},{4,22},{6,20},{8,26},{10,24},{12,30},{14,28},{16,2},... | collective-permute-start | bytes 1105928 | tf_op jit(solution)/shard_map/ppermute | solution.py:417
  77.5 1.7 collective-permute-start.24
  77.5 2.2 %collective-permute-start.25 = (bf16[3,48,1280]{2,1,0:T(8,128)(2,1)S(1)}, bf16[3,48,1280]{2,1,0:T(8,128)(2,1)S(1)}, u32[]{:S(2)}, u32[]{:S(2)}) collective-permute-start(bf16[3,48,1280]{2,1,0:T(8,128)(2,1)S(1)} %collective-permute-done.21.refs_8_), channel_id=1, source_target_pairs={{0,1},{1,0},{2,3},{3,2},{4,5},{5,4},{6,7},{7,6},{8,9},{9,8},{10,11... | collective-permute-start | bytes 1105928 | tf_op jit(solution)/shard_map/ppermute | solution.py:408
  78.0 2.2 %collective-permute-start.26 = (bf16[3,48,1280]{2,1,0:T(8,128)(2,1)S(1)}, bf16[3,48,1280]{2,1,0:T(8,128)(2,1)S(1)}, u32[]{:S(2)}, u32[]{:S(2)}) collective-permute-start(bf16[3,48,1280]{2,1,0:T(8,128)(2,1)S(1)} %collective-permute-done.22.refs_9_), channel_id=1, source_target_pairs={{0,1},{1,0},{2,3},{3,2},{4,5},{5,4},{6,7},{7,6},{8,9},{9,8},{10,11... | collective-permute-start | bytes 1105928 | tf_op jit(solution)/shard_map/ppermute | solution.py:408
  78.0 2.8 %collective-permute-start.27 = (bf16[3,48,1280]{2,1,0:T(8,128)(2,1)S(1)}, bf16[3,48,1280]{2,1,0:T(8,128)(2,1)S(1)}, u32[]{:S(2)}, u32[]{:S(2)}) collective-permute-start(bf16[3,48,1280]{2,1,0:T(8,128)(2,1)S(1)} %collective-permute-done.23.refs_10_), channel_id=1, source_target_pairs={{0,1},{1,0},{2,3},{3,2},{4,5},{5,4},{6,7},{7,6},{8,9},{9,8},{10,11... | collective-permute-start | bytes 1105928 | tf_op jit(solution)/shard_map/ppermute | solution.py:408
  99.5 4.2 %collective-permute-start.28 = (bf16[2,2,2,4,48,640]{5,4,3,2,1,0:T(8,128)(2,1)S(1)}, bf16[2,2,2,4,48,640]{5,4,3,2,1,0:T(8,128)(2,1)S(1)}, u32[]{:S(2)}, u32[]{:S(2)}) collective-permute-start(bf16[2,2,2,4,48,640]{5,4,3,2,1,0:T(8,128)(2,1)S(1)} %get-tuple-element.149), channel_id=1, source_target_pairs={{0,1},{1,0},{2,3},{3,2},{4,5},{5,4},{6,7},{7,6},{8,9},{9,8},{10,11... | collective-permute-start | bytes 5898248 | tf_op jit(solution)/shard_map/ppermute | solution.py:408
  100.0 26.5 %collective-permute-start.30 = (bf16[416,384]{1,0:T(8,128)(2,1)S(1)}, bf16[416,384]{1,0:T(8,128)(2,1)S(1)}, u32[]{:S(2)}, u32[]{:S(2)}) collective-permute-start(bf16[416,384]{1,0:T(8,128)(2,1)S(1)} %get-tuple-element.165), channel_id=1, source_target_pairs={{0,16},{16,0},{1,17},{17,1},{2,18},{18,2},{3,19},{19,3},{4,20},{20... | collective-permute-start | bytes 958472 | tf_op jit(solution)/shard_map/ppermute | solution.py:411
  104.2 16.6 %collective-permute-start.31 = (bf16[2,4,48,640]{3,2,1,0:T(8,128)(2,1)S(1)}, bf16[2,4,48,640]{3,2,1,0:T(8,128)(2,1)S(1)}, u32[]{:S(2)}, u32[]{:S(2)}) collective-permute-start(bf16[2,4,48,640]{3,2,1,0:T(8,128)(2,1)S(1)} %get-tuple-element.225), channel_id=1, source_target_pairs={{0,16},{16,0},{1,17},{17,1},{2,18},{18,2},{3,19},{19,3},{4,20},{20... | collective-permute-start | bytes 1474568 | tf_op jit(solution)/shard_map/ppermute | solution.py:411
  105.7 15.1 %collective-permute-start.32 = (bf16[2,4,48,640]{3,2,1,0:T(8,128)(2,1)S(1)}, bf16[2,4,48,640]{3,2,1,0:T(8,128)(2,1)S(1)}, u32[]{:S(2)}, u32[]{:S(2)}) collective-permute-start(bf16[2,4,48,640]{3,2,1,0:T(8,128)(2,1)S(1)} %get-tuple-element.224), channel_id=1, source_target_pairs={{0,2},{2,0},{4,6},{6,4},{8,10},{10,8},{12,14},{14,12},{1,3},{3,1},... | collective-permute-start | bytes 1474568 | tf_op jit(solution)/shard_map/ppermute | solution.py:414
  118.4 10.5 %collective-permute-start.29 = (bf16[416,384]{1,0:T(8,128)(2,1)S(1)}, bf16[416,384]{1,0:T(8,128)(2,1)S(1)}, u32[]{:S(2)}, u32[]{:S(2)}) collective-permute-start(bf16[416,384]{1,0:T(8,128)(2,1)S(1)} %get-tuple-element.164), channel_id=1, source_target_pairs={{0,16},{16,0},{1,17},{17,1},{2,18},{18,2},{3,19},{19,3},{4,20},{20... | collective-permute-start | bytes 958472 | tf_op jit(solution)/shard_map/ppermute | solution.py:411
  120.4 35.0 %copy-start.1 = (bf16[512,384]{1,0:T(8,128)(2,1)}, bf16[512,384]{1,0:T(8,128)(2,1)S(1)}, u32[]{:S(2)}) copy-start(bf16[512,384]{1,0:T(8,128)(2,1)S(1)} %convolution_convert_fusion.1) | copy-start | bytes 1179652
  120.8 5.0 %collective-permute-start.35 = (bf16[2,2,2,4,48,640]{5,4,3,2,1,0:T(8,128)(2,1)S(1)}, bf16[2,2,2,4,48,640]{5,4,3,2,1,0:T(8,128)(2,1)S(1)}, u32[]{:S(2)}, u32[]{:S(2)}) collective-permute-start(bf16[2,2,2,4,48,640]{5,4,3,2,1,0:T(8,128)(2,1)S(1)} %get-tuple-element.182), channel_id=1, source_target_pairs={{0,1},{1,0},{2,3},{3,2},{4,5},{5,4},{6,7},{7,6},{8,9},{9,8},{10,11... | collective-permute-start | bytes 5898248 | tf_op jit(solution)/shard_map/ppermute | solution.py:408
  121.1 13.1 %collective-permute-start.34 = (bf16[4,48,640]{2,1,0:T(8,128)(2,1)S(1)}, bf16[4,48,640]{2,1,0:T(8,128)(2,1)S(1)}, u32[]{:S(2)}, u32[]{:S(2)}) collective-permute-start(bf16[4,48,640]{2,1,0:T(8,128)(2,1)S(1)} %fusion.23), channel_id=1, source_target_pairs={{0,16},{16,0},{1,17},{17,1},{2,18},{18,2},{3,19},{19,3},{4,20},{20... | collective-permute-start | bytes 737288 | tf_op jit(solution)/shard_map/ppermute | solution.py:411
  121.8 12.3 %collective-permute-start.33 = (bf16[4,48,640]{2,1,0:T(8,128)(2,1)S(1)}, bf16[4,48,640]{2,1,0:T(8,128)(2,1)S(1)}, u32[]{:S(2)}, u32[]{:S(2)}) collective-permute-start(bf16[4,48,640]{2,1,0:T(8,128)(2,1)S(1)} %fusion.22), channel_id=1, source_target_pairs={{0,2},{2,0},{4,6},{6,4},{8,10},{10,8},{12,14},{14,12},{1,3},{3,1},... | collective-permute-start | bytes 737288 | tf_op jit(solution)/shard_map/ppermute | solution.py:414
  126.3 17.0 %collective-permute-start.36 = (bf16[2,4,48,640]{3,2,1,0:T(8,128)(2,1)S(1)}, bf16[2,4,48,640]{3,2,1,0:T(8,128)(2,1)S(1)}, u32[]{:S(2)}, u32[]{:S(2)}) collective-permute-start(bf16[2,4,48,640]{3,2,1,0:T(8,128)(2,1)S(1)} %get-tuple-element.221), channel_id=1, source_target_pairs={{0,16},{16,0},{1,17},{17,1},{2,18},{18,2},{3,19},{19,3},{4,20},{20... | collective-permute-start | bytes 1474568 | tf_op jit(solution)/shard_map/ppermute | solution.py:411
  126.5 16.7 %collective-permute-start.37 = (bf16[2,4,48,640]{3,2,1,0:T(8,128)(2,1)S(1)}, bf16[2,4,48,640]{3,2,1,0:T(8,128)(2,1)S(1)}, u32[]{:S(2)}, u32[]{:S(2)}) collective-permute-start(bf16[2,4,48,640]{3,2,1,0:T(8,128)(2,1)S(1)} %get-tuple-element.220), channel_id=1, source_target_pairs={{0,2},{2,0},{4,6},{6,4},{8,10},{10,8},{12,14},{14,12},{1,3},{3,1},... | collective-permute-start | bytes 1474568 | tf_op jit(solution)/shard_map/ppermute | solution.py:414
  134.3 12.8 %collective-permute-start.45 = (bf16[2,48,640]{2,1,0:T(8,128)(2,1)S(1)}, bf16[2,48,640]{2,1,0:T(8,128)(2,1)S(1)}, u32[]{:S(2)}, u32[]{:S(2)}) collective-permute-start(bf16[2,48,640]{2,1,0:T(8,128)(2,1)S(1)} %get-tuple-element.234), channel_id=1, source_target_pairs={{0,4},{2,6},{4,0},{6,2},{8,12},{10,14},{12,8},{14,10},{1,5},{3,7},... | collective-permute-start | bytes 368648 | tf_op jit(solution)/shard_map/ppermute | solution.py:440
  135.0 13.4 %collective-permute-start.46 = (bf16[2,48,640]{2,1,0:T(8,128)(2,1)S(1)}, bf16[2,48,640]{2,1,0:T(8,128)(2,1)S(1)}, u32[]{:S(2)}, u32[]{:S(2)}) collective-permute-start(bf16[2,48,640]{2,1,0:T(8,128)(2,1)S(1)} %get-tuple-element.233), channel_id=1, source_target_pairs={{0,8},{2,10},{4,12},{6,14},{8,0},{10,2},{12,4},{14,6},{1,9},{3,11}... | collective-permute-start | bytes 368648 | tf_op jit(solution)/shard_map/ppermute | solution.py:440
  136.3 12.1 %collective-permute-start.47 = (bf16[2,48,640]{2,1,0:T(8,128)(2,1)S(1)}, bf16[2,48,640]{2,1,0:T(8,128)(2,1)S(1)}, u32[]{:S(2)}, u32[]{:S(2)}) collective-permute-start(bf16[2,48,640]{2,1,0:T(8,128)(2,1)S(1)} %get-tuple-element.232), channel_id=1, source_target_pairs={{0,12},{2,14},{4,8},{6,10},{8,4},{10,6},{12,0},{14,2},{1,13},{3,15... | collective-permute-start | bytes 368648 | tf_op jit(solution)/shard_map/ppermute | solution.py:440
  143.4 6.6 %collective-permute-start.41 = (bf16[4,48,640]{2,1,0:T(8,128)(2,1)S(1)}, bf16[4,48,640]{2,1,0:T(8,128)(2,1)S(1)}, u32[]{:S(2)}, u32[]{:S(2)}) collective-permute-start(bf16[4,48,640]{2,1,0:T(8,128)(2,1)S(1)} %fusion.25), channel_id=1, source_target_pairs={{0,16},{16,0},{1,17},{17,1},{2,18},{18,2},{3,19},{19,3},{4,20},{20... | collective-permute-start | bytes 737288 | tf_op jit(solution)/shard_map/ppermute | solution.py:411
  145.9 9.6 %collective-permute-start.38 = (bf16[4,208,384]{2,1,0:T(8,128)(2,1)S(1)}, bf16[4,208,384]{2,1,0:T(8,128)(2,1)S(1)}, u32[]{:S(2)}, u32[]{:S(2)}) collective-permute-start(bf16[4,208,384]{2,1,0:T(8,128)(2,1)S(1)} %pad_maximum_fusion.4), channel_id=1, source_target_pairs={{1,3},{3,5},{5,7},{7,9},{9,11},{11,13},{13,15},{17,19},{19,21},{21... | collective-permute-start | bytes 1916936 | tf_op jit(solution)/shard_map/ppermute | solution.py:453
  147.2 8.3 %collective-permute-start.40 = (bf16[4,48,640]{2,1,0:T(8,128)(2,1)S(1)}, bf16[4,48,640]{2,1,0:T(8,128)(2,1)S(1)}, u32[]{:S(2)}, u32[]{:S(2)}) collective-permute-start(bf16[4,48,640]{2,1,0:T(8,128)(2,1)S(1)} %fusion.24), channel_id=1, source_target_pairs={{0,2},{2,0},{4,6},{6,4},{8,10},{10,8},{12,14},{14,12},{1,3},{3,1},... | collective-permute-start | bytes 737288 | tf_op jit(solution)/shard_map/ppermute | solution.py:414
  148.4 7.2 %copy-start.2 = (bf16[512,384]{1,0:T(8,128)(2,1)}, bf16[512,384]{1,0:T(8,128)(2,1)S(1)}, u32[]{:S(2)}) copy-start(bf16[512,384]{1,0:T(8,128)(2,1)S(1)} %convolution_convert_fusion) | copy-start | bytes 1179652
  155.6 0.9 slice-start
  155.6 1.0 slice-start.1
  156.9 19.7 %collective-permute-start.39 = (bf16[4,512,384]{2,1,0:T(8,128)(2,1)S(1)}, bf16[4,512,384]{2,1,0:T(8,128)(2,1)S(1)}, u32[]{:S(2)}, u32[]{:S(2)}) collective-permute-start(bf16[4,512,384]{2,1,0:T(8,128)(2,1)S(1)} %pad_maximum_fusion), channel_id=1, source_target_pairs={{0,1},{1,0},{2,3},{3,2},{4,5},{5,4},{6,7},{7,6},{8,9},{9,8},{10,11... | collective-permute-start | bytes 4718600 | tf_op jit(solution)/shard_map/ppermute | solution.py:408
  161.3 8.0 %collective-permute-start.42 = (bf16[2,48,640]{2,1,0:T(8,128)(2,1)S(1)}, bf16[2,48,640]{2,1,0:T(8,128)(2,1)S(1)}, u32[]{:S(2)}, u32[]{:S(2)}) collective-permute-start(bf16[2,48,640]{2,1,0:T(8,128)(2,1)S(1)} %get-tuple-element.237), channel_id=1, source_target_pairs={{0,4},{2,6},{4,0},{6,2},{8,12},{10,14},{12,8},{14,10},{1,5},{3,7},... | collective-permute-start | bytes 368648 | tf_op jit(solution)/shard_map/ppermute | solution.py:440
  164.2 12.4 %collective-permute-start.43 = (bf16[2,48,640]{2,1,0:T(8,128)(2,1)S(1)}, bf16[2,48,640]{2,1,0:T(8,128)(2,1)S(1)}, u32[]{:S(2)}, u32[]{:S(2)}) collective-permute-start(bf16[2,48,640]{2,1,0:T(8,128)(2,1)S(1)} %get-tuple-element.236), channel_id=1, source_target_pairs={{0,8},{2,10},{4,12},{6,14},{8,0},{10,2},{12,4},{14,6},{1,9},{3,11}... | collective-permute-start | bytes 368648 | tf_op jit(solution)/shard_map/ppermute | solution.py:440
  165.6 11.0 %collective-permute-start.44 = (bf16[2,48,640]{2,1,0:T(8,128)(2,1)S(1)}, bf16[2,48,640]{2,1,0:T(8,128)(2,1)S(1)}, u32[]{:S(2)}, u32[]{:S(2)}) collective-permute-start(bf16[2,48,640]{2,1,0:T(8,128)(2,1)S(1)} %get-tuple-element.235), channel_id=1, source_target_pairs={{0,12},{2,14},{4,8},{6,10},{8,4},{10,6},{12,0},{14,2},{1,13},{3,15... | collective-permute-start | bytes 368648 | tf_op jit(solution)/shard_map/ppermute | solution.py:440
  176.7 4.9 %collective-permute-start.48 = (bf16[48,1280]{1,0:T(8,128)(2,1)S(1)}, bf16[48,1280]{1,0:T(8,128)(2,1)S(1)}, u32[]{:S(2)}, u32[]{:S(2)}) collective-permute-start(bf16[48,1280]{1,0:T(8,128)(2,1)S(1)} %select_convert_fusion), channel_id=1, source_target_pairs={{0,16},{16,0},{1,17},{17,1},{2,18},{18,2},{3,19},{19,3},{4,20},{20... | collective-permute-start | bytes 368648 | tf_op jit(solution)/shard_map/ppermute | solution.py:411
  181.7 0.6 copy-start.4

commit v4 on v1

--- a/solution.py
+++ b/solution.py
@@ -543,9 +543,10 @@
         columns = [jnp.stack([pz_to(start[0], kk) for kk in range(1, m)])]
         start[1] = after(start[1], columns[0])[0]
         near = pz_to(start[1], 1)
-        columns[0], near, *firsts = after(columns[0], near, *firsts)
+        columns[0], *firsts = after(columns[0], *firsts)
         rest = [columns[0], px(columns[0]), py(columns[0]), pd(columns[0])]
-        columns.append(jnp.concatenate([near[None], pz_to(jnp.stack([start[1], near]), 2)]))
+        pair = after(jnp.stack([start[1], near]), *firsts)[0]
+        columns.append(jnp.concatenate([near[None], pz_to(pair, 2)]))
         columns[1], *rest = after(columns[1], *rest)
         twins = [pt(a) for a in firsts]
         sources = [firsts + rest + twins + [pt(a) for a in rest]]

time: 175 us -> 175 us (level)
    ppermute x10, waiting for transfers between devices: 26.6 us -> 24 us  [pz_to(): return lax.ppermute(a, 'dp', [(i, i ^ 2 * kk) for i in range(n_dp)])]
    ppermute x7, waiting for transfers between devices: 12.9 us -> 14.8 us  [py(): return lax.ppermute(a, 'dp', [(i, i ^ 1) for i in range(n_dp)])]
  transfers between devices with their start and end apart: 48 -> 48, of which waited for: 23 -> 25; matrix products, arithmetic and copies ran while one was open for 7% -> 7% of each run, Pallas kernels for 14% -> 14%
where the time goes in v4:
time: 175 us
  waiting for transfers between devices  59 us (34%)
  starting transfers between devices  52.8 us (30%)
  Pallas kernels  45.4 us (26%)
  other arithmetic  6.4 us (4%)
  local copies, waits for them, and re-layouts  4.51 us (3%)
  matrix products  4.5 us (3%)
  between operations  2.09 us (1%)
    pallas_call x5, Pallas kernels, layer_call(): pl.pallas_call(body, out_shape=[jax.ShapeDtypeStruct(*o) for o in outs],...  43.5 us
    ppermute x10, waiting for transfers between devices, pz_to(): return lax.ppermute(a, 'dp', [(i, i ^ 2 * kk) for i in range(n_dp)])  24 us
    ppermute x10, starting transfers between devices, pz_to(): return lax.ppermute(a, 'dp', [(i, i ^ 2 * kk) for i in range(n_dp)])  19.7 us
    ppermute x11, starting transfers between devices, px(): return lax.ppermute(a, 'section', [(0, 1), (1, 0)])  15 us
    ppermute x7, waiting for transfers between devices, py(): return lax.ppermute(a, 'dp', [(i, i ^ 1) for i in range(n_dp)])  14.8 us
    ppermute x11, waiting for transfers between devices, px(): return lax.ppermute(a, 'section', [(0, 1), (1, 0)])  13.5 us
    ppermute x7, starting transfers between devices, py(): return lax.ppermute(a, 'dp', [(i, i ^ 1) for i in range(n_dp)])  9.91 us
    dot_general x10, matrix products, mm(): return lax.dot_general(a, b, (dims, ((), ())), preferred_element_type=F32)  4.5 us
  transfers between devices with their start and end apart: 48, of which 25 were waited for; matrix products, arithmetic and copies ran while one was open for 7% of the time, Pallas kernels for 14%

profile of v4, /device:TPU:0, one launch (start us, length us, event | category | flops | bytes accessed | tf_op | source)
XLA Modules:
  0.0 174.6 jit_solution(17453676727668006095)
XLA Ops:
  0.7 1.3 constant_dynamic-slice_fusion
  2.1 0.7 collective-permute-start.1
  3.5 3.0 %collective-permute-start = (bf16[48,1280]{1,0:T(8,128)(2,1)S(1)}, bf16[48,1280]{1,0:T(8,128)(2,1)S(1)}, u32[]{:S(2)}, u32[]{:S(2)}) collective-permute-start(bf16[48,1280]{1,0:T(8,128)(2,1)S(1)} %broadcast_select_fusion.3), channel_id=1, source_target_pairs={{0,16},{16,0},{1,17},{17,1},{2,18},{18,2},{3,19},{19,3},{4,20},{20... | collective-permute-start | bytes 368648 | tf_op jit(solution)/shard_map/ppermute | solution.py:411
  6.5 3.9 %collective-permute-done = bf16[48,1280]{1,0:T(8,128)(2,1)S(1)} collective-permute-done((bf16[48,1280]{1,0:T(8,128)(2,1)S(1)}, bf16[48,1280]{1,0:T(8,128)(2,1)S(1)}, u32[]{:S(2)}, u32[]{:S(2)}) %collective-permute-start) | collective-permute-done | bytes 122912 | tf_op jit(solution)/shard_map/ppermute | solution.py:411
  10.5 1.2 collective-permute-start.2
  11.7 2.6 %collective-permute-start.3 = (bf16[48,1280]{1,0:T(8,128)(2,1)S(1)}, bf16[48,1280]{1,0:T(8,128)(2,1)S(1)}, u32[]{:S(2)}, u32[]{:S(2)}) collective-permute-start(bf16[48,1280]{1,0:T(8,128)(2,1)S(1)} %get-tuple-element.234), channel_id=1, source_target_pairs={{0,8},{2,10},{4,12},{6,14},{8,0},{10,2},{12,4},{14,6},{1,9},{3,11}... | collective-permute-start | bytes 368648 | tf_op jit(solution)/shard_map/ppermute | solution.py:440
  14.3 0.7 collective-permute-start.4
  15.0 1.8 %collective-permute-start.5 = (bf16[2,48,1280]{2,1,0:T(8,128)(2,1)S(1)}, bf16[2,48,1280]{2,1,0:T(8,128)(2,1)S(1)}, u32[]{:S(2)}, u32[]{:S(2)}) collective-permute-start(bf16[2,48,1280]{2,1,0:T(8,128)(2,1)S(1)} %pad_maximum_fusion.8.refs_2_.refs_3_.refs_13_), channel_id=1, source_target_pairs={{0,16},{16,0},{1,17},{17,1},{2,18},{18,2},{3,19},{19,3},{4,20},{20... | collective-permute-start | bytes 737288 | tf_op jit(solution)/shard_map/ppermute | solution.py:411
  16.8 1.7 collective-permute-start.6
  18.6 3.1 %collective-permute-start.7 = (bf16[2,48,1280]{2,1,0:T(8,128)(2,1)S(1)}, bf16[2,48,1280]{2,1,0:T(8,128)(2,1)S(1)}, u32[]{:S(2)}, u32[]{:S(2)}) collective-permute-start(bf16[2,48,1280]{2,1,0:T(8,128)(2,1)S(1)} %pad_maximum_fusion.8.refs_2_.refs_3_.refs_13_), channel_id=1, source_target_pairs={{0,18},{2,16},{4,22},{6,20},{8,26},{10,24},{12,30},{14,28},{16,2},... | collective-permute-start | bytes 737288 | tf_op jit(solution)/shard_map/ppermute | solution.py:417
  21.7 2.4 %collective-permute-done.3 = bf16[48,1280]{1,0:T(8,128)(2,1)S(1)} collective-permute-done((bf16[48,1280]{1,0:T(8,128)(2,1)S(1)}, bf16[48,1280]{1,0:T(8,128)(2,1)S(1)}, u32[]{:S(2)}, u32[]{:S(2)}) %collective-permute-start.3) | collective-permute-done | bytes 122912 | tf_op jit(solution)/shard_map/ppermute | solution.py:440
  24.1 3.1 %collective-permute-start.8 = (bf16[48,1280]{1,0:T(8,128)(2,1)S(1)}, bf16[48,1280]{1,0:T(8,128)(2,1)S(1)}, u32[]{:S(2)}, u32[]{:S(2)}) collective-permute-start(bf16[48,1280]{1,0:T(8,128)(2,1)S(1)} %get-tuple-element.119), channel_id=1, source_target_pairs={{0,4},{2,6},{4,0},{6,2},{8,12},{10,14},{12,8},{14,10},{1,5},{3,7},... | collective-permute-start | bytes 368648 | tf_op jit(solution)/shard_map/ppermute | solution.py:440
  27.3 1.9 %collective-permute-done.6.refs_4_.refs_5_.refs_15_ = bf16[2,48,1280]{2,1,0:T(8,128)(2,1)S(1)} collective-permute-done((bf16[2,48,1280]{2,1,0:T(8,128)(2,1)S(1)}, bf16[2,48,1280]{2,1,0:T(8,128)(2,1)S(1)}, u32[]{:S(2)}, u32[]{:S(2)}) %collective-permute-start.6) | collective-permute-done | bytes 245792 | tf_op jit(solution)/shard_map/ppermute | solution.py:414
  29.1 0.7 collective-permute-done.7.refs_5_.refs_6_.refs_16_
  29.9 0.9 collective-permute-done.8
  30.7 2.8 %collective-permute-start.9 = (bf16[2,48,1280]{2,1,0:T(8,128)(2,1)S(1)}, bf16[2,48,1280]{2,1,0:T(8,128)(2,1)S(1)}, u32[]{:S(2)}, u32[]{:S(2)}) collective-permute-start(bf16[2,48,1280]{2,1,0:T(8,128)(2,1)S(1)} %pad_maximum_fusion.9), channel_id=1, source_target_pairs={{0,8},{2,10},{4,12},{6,14},{8,0},{10,2},{12,4},{14,6},{1,9},{3,11}... | collective-permute-start | bytes 737288 | tf_op jit(solution)/shard_map/ppermute | solution.py:440
  34.9 1.6 collective-permute-start.10
  36.5 2.4 %collective-permute-start.11 = (bf16[3,48,1280]{2,1,0:T(8,128)(2,1)S(1)}, bf16[3,48,1280]{2,1,0:T(8,128)(2,1)S(1)}, u32[]{:S(2)}, u32[]{:S(2)}) collective-permute-start(bf16[3,48,1280]{2,1,0:T(8,128)(2,1)S(1)} %pad_maximum_fusion.5.refs_6_.refs_17_), channel_id=1, source_target_pairs={{0,2},{2,0},{4,6},{6,4},{8,10},{10,8},{12,14},{14,12},{1,3},{3,1},... | collective-permute-start | bytes 1105928 | tf_op jit(solution)/shard_map/ppermute | solution.py:414
  38.9 5.3 %collective-permute-done.9 = bf16[2,48,1280]{2,1,0:T(8,128)(2,1)S(1)} collective-permute-done((bf16[2,48,1280]{2,1,0:T(8,128)(2,1)S(1)}, bf16[2,48,1280]{2,1,0:T(8,128)(2,1)S(1)}, u32[]{:S(2)}, u32[]{:S(2)}) %collective-permute-start.9) | collective-permute-done | bytes 245792 | tf_op jit(solution)/shard_map/ppermute | solution.py:440
  44.4 2.1 %collective-permute-done.10.refs_7_.refs_18_ = bf16[3,48,1280]{2,1,0:T(8,128)(2,1)S(1)} collective-permute-done((bf16[3,48,1280]{2,1,0:T(8,128)(2,1)S(1)}, bf16[3,48,1280]{2,1,0:T(8,128)(2,1)S(1)}, u32[]{:S(2)}, u32[]{:S(2)}) %collective-permute-start.10) | collective-permute-done | bytes 368672 | tf_op jit(solution)/shard_map/ppermute | solution.py:411
  46.5 6.9 %collective-permute-done.11.refs_8_.refs_19_ = bf16[3,48,1280]{2,1,0:T(8,128)(2,1)S(1)} collective-permute-done((bf16[3,48,1280]{2,1,0:T(8,128)(2,1)S(1)}, bf16[3,48,1280]{2,1,0:T(8,128)(2,1)S(1)}, u32[]{:S(2)}, u32[]{:S(2)}) %collective-permute-start.11) | collective-permute-done | bytes 368672 | tf_op jit(solution)/shard_map/ppermute | solution.py:414
  53.4 0.7 collective-permute-done.12.refs_9_.refs_20_
  56.4 1.3 collective-permute-done.16.refs_13_.refs_14_.refs_24_
  57.8 1.5 collective-permute-start.21
  59.2 0.8 collective-permute-start.22
  60.0 1.2 collective-permute-start.23
  61.3 8.6 %shard_map.186 = (bf16[416,384]{1,0:T(8,128)(2,1)S(1)}, f32[416,384]{1,0:T(8,128)S(1)}, f32[416,128]{1,0:T(8,128)S(1)}, bf16[416,384]{1,0:T(8,128)(2,1)S(1)}, bf...) custom-call(s32[5]{0:T(128)S(1)} %stack.113.refs_0_.sc, ...), custom_call_target="tpu_custom_call" | custom-call | flops 10000000000 | bytes 8388608 | tf_op jit(solution)/shard_map/pallas_call | solution.py:342
  69.9 6.0 %collective-permute-done.22.refs_9_ = bf16[3,48,1280]{2,1,0:T(8,128)(2,1)S(1)} collective-permute-done((bf16[3,48,1280]{2,1,0:T(8,128)(2,1)S(1)}, bf16[3,48,1280]{2,1,0:T(8,128)(2,1)S(1)}, u32[]{:S(2)}, u32[]{:S(2)}) %collective-permute-start.22) | collective-permute-done | bytes 368672 | tf_op jit(solution)/shard_map/ppermute | solution.py:414
  75.8 1.6 collective-permute-done.23.refs_10_
  78.5 0.7 collective-permute-done.24.refs_15_
  80.7 18.7 %shard_map.187 = (bf16[416,384]{1,0:T(8,128)(2,1)S(1)}, bf16[2,416,256]{2,1,0:T(8,128)(2,1)S(1)}, bf16[416,384]{1,0:T(8,128)(2,1)S(1)}, bf16[416,1536]{1,0:T(8,1...) custom-call(s32[5]{0:T(128)S(1)} %stack.113.refs_0_.sc, ...), custom_call_target="tpu_custom_call" | custom-call | flops 30000001024 | bytes 8388608 | tf_op jit(solution)/shard_map/pallas_call | solution.py:342
  100.0 0.6 collective-permute-start.30
  101.5 2.2 %shard_map.188 = (bf16[2,4,48,640]{3,2,1,0:T(8,128)(2,1)S(1)}, bf16[2,4,48,640]{3,2,1,0:T(8,128)(2,1)S(1)}, bf16[2,4,48,640]{3,2,1,0:T(8,128)(2,1)S(1)}, bf16[2,4,48,640]{3,2,1,0:T(8,128)(2,1)S(1)}) custom-call(s32[5]{0:T(128)S(1)} %stack.113.refs_0_.sc, bf16[416,384]{1,0:T(8,128)(2,1)S(1)} %get-tuple-element.136.refs_1_, ...), custom_call_target="tpu_custom_call" | custom-call | flops 10000000000 | bytes 8388608 | tf_op jit(solution)/shard_map/pallas_call | solution.py:342
  104.2 1.5 collective-permute-start.31
  105.7 0.8 collective-permute-start.32
  106.6 11.8 %shard_map.189 = (bf16[416,384]{1,0:T(8,128)(2,1)S(1)}, bf16[416,384]{1,0:T(8,128)(2,1)S(1)}, bf16[416,384]{1,0:T(8,128)(2,1)S(1)}, bf16[416,1536]{1,0:T(8,128)(...) custom-call(s32[5]{0:T(128)S(1)} %stack.113.refs_0_.sc, ...), custom_call_target="tpu_custom_call" | custom-call | flops 20000000000 | bytes 8388608 | tf_op jit(solution)/shard_map/pallas_call | solution.py:342
  118.4 1.5 collective-permute-start.29
  121.1 0.6 collective-permute-start.34
  121.8 1.7 collective-permute-start.33
  123.6 2.2 %shard_map.190 = (bf16[2,4,48,640]{3,2,1,0:T(8,128)(2,1)S(1)}, bf16[2,4,48,640]{3,2,1,0:T(8,128)(2,1)S(1)}, bf16[2,4,48,640]{3,2,1,0:T(8,128)(2,1)S(1)}, bf16[2,4,48,640]{3,2,1,0:T(8,128)(2,1)S(1)}) custom-call(s32[5]{0:T(128)S(1)} %stack.113.refs_0_.sc, bf16[416,384]{1,0:T(8,128)(2,1)S(1)} %get-tuple-element.154.refs_4_.refs_1_, ...), custom_call_target="tpu_custom_call" | custom-call | flops 10000000000 | bytes 8388608 | tf_op jit(solution)/shard_map/pallas_call | solution.py:342
  126.5 1.7 collective-permute-start.38
  128.2 0.7 collective-permute-done.29
  128.9 5.3 %collective-permute-done.34 = bf16[4,48,640]{2,1,0:T(8,128)(2,1)S(1)} collective-permute-done((bf16[4,48,640]{2,1,0:T(8,128)(2,1)S(1)}, bf16[4,48,640]{2,1,0:T(8,128)(2,1)S(1)}, u32[]{:S(2)}, u32[]{:S(2)}) %collective-permute-start.34) | collective-permute-done | bytes 245792 | tf_op jit(solution)/shard_map/ppermute | solution.py:411
  136.1 0.6 collective-permute-start.40
  136.8 0.7 collective-permute-start.36
  137.6 4.7 %collective-permute-done.40 = bf16[2,2,48,640]{3,2,0,1:T(8,128)(2,1)S(1)} collective-permute-done((bf16[2,2,48,640]{3,2,0,1:T(8,128)(2,1)S(1)}, bf16[2,2,48,640]{3,2,0,1:T(8,128)(2,1)S(1)}, u32[]{:S(2)}, u32[]{:S(2)}) %collective-permute-start.40) | collective-permute-done | bytes 245792 | tf_op jit(solution)/shard_map/ppermute | solution.py:440
  142.4 0.8 collective-permute-done.37
  143.4 1.6 collective-permute-start.43
  145.1 0.7 collective-permute-start.42
  145.8 4.3 %collective-permute-start.41 = (bf16[2,48,640]{2,1,0:T(8,128)(2,1)S(1)}, bf16[2,48,640]{2,1,0:T(8,128)(2,1)S(1)}, u32[]{:S(2)}, u32[]{:S(2)}) collective-permute-start(bf16[2,48,640]{2,1,0:T(8,128)(2,1)S(1)} %fusion.31), channel_id=1, source_target_pairs={{0,8},{2,10},{4,12},{6,14},{8,0},{10,2},{12,4},{14,6},{1,9},{3,11}... | collective-permute-start | bytes 368648 | tf_op jit(solution)/shard_map/ppermute | solution.py:440
  150.4 0.8 slice-done
  151.7 2.2 %collective-permute-done.41 = bf16[2,48,640]{2,1,0:T(8,128)(2,1)S(1)} collective-permute-done((bf16[2,48,640]{2,1,0:T(8,128)(2,1)S(1)}, bf16[2,48,640]{2,1,0:T(8,128)(2,1)S(1)}, u32[]{:S(2)}, u32[]{:S(2)}) %collective-permute-start.41) | collective-permute-done | bytes 122912 | tf_op jit(solution)/shard_map/ppermute | solution.py:440
  154.1 1.5 collective-permute-start.44
  155.7 0.8 collective-permute-start.45
  156.5 2.1 %collective-permute-start.46 = (bf16[2,48,640]{2,1,0:T(8,128)(2,1)S(1)}, bf16[2,48,640]{2,1,0:T(8,128)(2,1)S(1)}, u32[]{:S(2)}, u32[]{:S(2)}) collective-permute-start(bf16[2,48,640]{2,1,0:T(8,128)(2,1)S(1)} %get-tuple-element.231), channel_id=1, source_target_pairs={{0,12},{2,14},{4,8},{6,10},{8,4},{10,6},{12,0},{14,2},{1,13},{3,15... | collective-permute-start | bytes 368648 | tf_op jit(solution)/shard_map/ppermute | solution.py:440
  158.6 0.8 collective-permute-done.44
  159.4 7.7 %collective-permute-done.45 = bf16[2,48,640]{2,1,0:T(8,128)(2,1)S(1)} collective-permute-done((bf16[2,48,640]{2,1,0:T(8,128)(2,1)S(1)}, bf16[2,48,640]{2,1,0:T(8,128)(2,1)S(1)}, u32[]{:S(2)}, u32[]{:S(2)}) %collective-permute-start.45) | collective-permute-done | bytes 122912 | tf_op jit(solution)/shard_map/ppermute | solution.py:440
  167.2 1.0 collective-permute-start.47
  168.4 1.2 fusion.12
  169.6 1.0 fusion.10
  170.7 0.7 fusion.26.mine_ref
  171.4 0.7 collective-permute-done.47.other_ref
  172.1 0.6 copy-done.4
  172.8 1.9 %shard_map.191 = (f32[2,48]{1,0:T(2,128)}, f32[4,48]{1,0:T(4,128)}, f32[3,48,192]{2,1,0:T(8,128)}, f32[2,192]{1,0:T(2,128)}, f32[48,192]{1,0:T(8,128)}, /*index=...) custom-call(s32[5]{0:T(128)} %copy-done, f32[48,1280]{1,0:T(8,128)} %fusion.26.mine_ref, bf16[48,1280]{1,0:T(8,128)(2,1)} %copy-done.4), custom_call_target="tpu_custom_call" | custom-call | tf_op jit(solution)/shard_map/pallas_call | solution.py:385
  (149 shorter events, 14.2 us)
Async XLA Ops:
  0.7 2.1 %copy-start.7 = (bf16[1,192,48]{1,2,0:T(8,128)(2,1)S(1)}, bf16[1,192,48]{1,2,0:T(8,128)(2,1)}, u32[]{:S(2)}) copy-start(bf16[1,192,48]{1,2,0:T(8,128)(2,1)} %param.18) | copy-start | bytes 55300
  0.7 2.1 %copy-start.3 = (bf16[1,48,3,192]{3,1,2,0:T(8,128)(2,1)S(1)}, bf16[1,48,3,192]{3,1,2,0:T(8,128)(2,1)}, u32[]{:S(2)}) copy-start(bf16[1,48,3,192]{3,1,2,0:T(8,128)(2,1)} %param.16) | copy-start | bytes 165892
  0.7 2.2 %copy-start.10 = (bf16[1,4,48]{2,1,0:T(4,128)(2,1)S(1)}, bf16[1,4,48]{2,1,0:T(4,128)(2,1)}, u32[]{:S(2)}) copy-start(bf16[1,4,48]{2,1,0:T(4,128)(2,1)} %param.15) | copy-start | bytes 1156
  0.7 2.2 %copy-start.11 = (bf16[1,2,48]{2,1,0:T(2,128)(2,1)S(1)}, bf16[1,2,48]{2,1,0:T(2,128)(2,1)}, u32[]{:S(2)}) copy-start(bf16[1,2,48]{2,1,0:T(2,128)(2,1)} %param.14) | copy-start | bytes 580
  0.7 2.3 %copy-start.8 = (bf16[1,2,192]{2,1,0:T(2,128)(2,1)S(1)}, bf16[1,2,192]{2,1,0:T(2,128)(2,1)}, u32[]{:S(2)}) copy-start(bf16[1,2,192]{2,1,0:T(2,128)(2,1)} %param.17) | copy-start | bytes 2308
  0.7 2.4 %copy-start.9 = (bf16[1,768]{1,0:T(2,128)(2,1)S(1)}, bf16[1,768]{1,0:T(2,128)(2,1)}, u32[]{:S(2)}) copy-start(bf16[1,768]{1,0:T(2,128)(2,1)} %param.20) | copy-start | bytes 4612
  0.7 2.5 %copy-start.5 = (bf16[1,768,48]{1,2,0:T(8,128)(2,1)S(1)}, bf16[1,768,48]{1,2,0:T(8,128)(2,1)}, u32[]{:S(2)}) copy-start(bf16[1,768,48]{1,2,0:T(8,128)(2,1)} %param.21) | copy-start | bytes 221188
  0.7 2.6 %copy-start.6 = (bf16[1,48,768]{2,1,0:T(8,128)(2,1)S(1)}, bf16[1,48,768]{2,1,0:T(8,128)(2,1)}, u32[]{:S(2)}) copy-start(bf16[1,48,768]{2,1,0:T(8,128)(2,1)} %param.19) | copy-start | bytes 221188
  2.1 8.4 %collective-permute-start.1 = (bf16[2,208,384]{2,1,0:T(8,128)(2,1)S(1)}, bf16[2,208,384]{2,1,0:T(8,128)(2,1)S(1)}, u32[]{:S(2)}, u32[]{:S(2)}) collective-permute-start(bf16[2,208,384]{2,1,0:T(8,128)(2,1)S(1)} %pad_maximum_fusion.7), channel_id=1, source_target_pairs={{3,1},{5,3},{7,5},{9,7},{11,9},{13,11},{15,13},{19,17},{21,19},{23... | collective-permute-start | bytes 958472 | tf_op jit(solution)/shard_map/ppermute | solution.py:488
  3.5 30.1 %copy-start.12 = (s32[2]{0:T(128)S(1)}, s32[2]{0:T(128)}, u32[]{:S(2)}) copy-start(s32[2]{0:T(128)} %param.12) | copy-start | bytes 28
  3.5 7.0 %collective-permute-start = (bf16[48,1280]{1,0:T(8,128)(2,1)S(1)}, bf16[48,1280]{1,0:T(8,128)(2,1)S(1)}, u32[]{:S(2)}, u32[]{:S(2)}) collective-permute-start(bf16[48,1280]{1,0:T(8,128)(2,1)S(1)} %broadcast_select_fusion.3), channel_id=1, source_target_pairs={{0,16},{16,0},{1,17},{17,1},{2,18},{18,2},{3,19},{19,3},{4,20},{20... | collective-permute-start | bytes 368648 | tf_op jit(solution)/shard_map/ppermute | solution.py:411
  10.5 8.2 %collective-permute-start.2 = (bf16[48,1280]{1,0:T(8,128)(2,1)S(1)}, bf16[48,1280]{1,0:T(8,128)(2,1)S(1)}, u32[]{:S(2)}, u32[]{:S(2)}) collective-permute-start(bf16[48,1280]{1,0:T(8,128)(2,1)S(1)} %get-tuple-element.234), channel_id=1, source_target_pairs={{0,4},{2,6},{4,0},{6,2},{8,12},{10,14},{12,8},{14,10},{1,5},{3,7},... | collective-permute-start | bytes 368648 | tf_op jit(solution)/shard_map/ppermute | solution.py:440
  11.7 12.4 %collective-permute-start.3 = (bf16[48,1280]{1,0:T(8,128)(2,1)S(1)}, bf16[48,1280]{1,0:T(8,128)(2,1)S(1)}, u32[]{:S(2)}, u32[]{:S(2)}) collective-permute-start(bf16[48,1280]{1,0:T(8,128)(2,1)S(1)} %get-tuple-element.234), channel_id=1, source_target_pairs={{0,8},{2,10},{4,12},{6,14},{8,0},{10,2},{12,4},{14,6},{1,9},{3,11}... | collective-permute-start | bytes 368648 | tf_op jit(solution)/shard_map/ppermute | solution.py:440
  14.3 9.8 %collective-permute-start.4 = (bf16[48,1280]{1,0:T(8,128)(2,1)S(1)}, bf16[48,1280]{1,0:T(8,128)(2,1)S(1)}, u32[]{:S(2)}, u32[]{:S(2)}) collective-permute-start(bf16[48,1280]{1,0:T(8,128)(2,1)S(1)} %get-tuple-element.234), channel_id=1, source_target_pairs={{0,12},{2,14},{4,8},{6,10},{8,4},{10,6},{12,0},{14,2},{1,13},{3,15... | collective-permute-start | bytes 368648 | tf_op jit(solution)/shard_map/ppermute | solution.py:440
  15.0 12.3 %collective-permute-start.5 = (bf16[2,48,1280]{2,1,0:T(8,128)(2,1)S(1)}, bf16[2,48,1280]{2,1,0:T(8,128)(2,1)S(1)}, u32[]{:S(2)}, u32[]{:S(2)}) collective-permute-start(bf16[2,48,1280]{2,1,0:T(8,128)(2,1)S(1)} %pad_maximum_fusion.8.refs_2_.refs_3_.refs_13_), channel_id=1, source_target_pairs={{0,16},{16,0},{1,17},{17,1},{2,18},{18,2},{3,19},{19,3},{4,20},{20... | collective-permute-start | bytes 737288 | tf_op jit(solution)/shard_map/ppermute | solution.py:411
  16.8 12.4 %collective-permute-start.6 = (bf16[2,48,1280]{2,1,0:T(8,128)(2,1)S(1)}, bf16[2,48,1280]{2,1,0:T(8,128)(2,1)S(1)}, u32[]{:S(2)}, u32[]{:S(2)}) collective-permute-start(bf16[2,48,1280]{2,1,0:T(8,128)(2,1)S(1)} %pad_maximum_fusion.8.refs_2_.refs_3_.refs_13_), channel_id=1, source_target_pairs={{0,2},{2,0},{4,6},{6,4},{8,10},{10,8},{12,14},{14,12},{1,3},{3,1},... | collective-permute-start | bytes 737288 | tf_op jit(solution)/shard_map/ppermute | solution.py:414
  18.6 11.2 %collective-permute-start.7 = (bf16[2,48,1280]{2,1,0:T(8,128)(2,1)S(1)}, bf16[2,48,1280]{2,1,0:T(8,128)(2,1)S(1)}, u32[]{:S(2)}, u32[]{:S(2)}) collective-permute-start(bf16[2,48,1280]{2,1,0:T(8,128)(2,1)S(1)} %pad_maximum_fusion.8.refs_2_.refs_3_.refs_13_), channel_id=1, source_target_pairs={{0,18},{2,16},{4,22},{6,20},{8,26},{10,24},{12,30},{14,28},{16,2},... | collective-permute-start | bytes 737288 | tf_op jit(solution)/shard_map/ppermute | solution.py:417
  24.1 6.6 %collective-permute-start.8 = (bf16[48,1280]{1,0:T(8,128)(2,1)S(1)}, bf16[48,1280]{1,0:T(8,128)(2,1)S(1)}, u32[]{:S(2)}, u32[]{:S(2)}) collective-permute-start(bf16[48,1280]{1,0:T(8,128)(2,1)S(1)} %get-tuple-element.119), channel_id=1, source_target_pairs={{0,4},{2,6},{4,0},{6,2},{8,12},{10,14},{12,8},{14,10},{1,5},{3,7},... | collective-permute-start | bytes 368648 | tf_op jit(solution)/shard_map/ppermute | solution.py:440
  30.7 13.5 %collective-permute-start.9 = (bf16[2,48,1280]{2,1,0:T(8,128)(2,1)S(1)}, bf16[2,48,1280]{2,1,0:T(8,128)(2,1)S(1)}, u32[]{:S(2)}, u32[]{:S(2)}) collective-permute-start(bf16[2,48,1280]{2,1,0:T(8,128)(2,1)S(1)} %pad_maximum_fusion.9), channel_id=1, source_target_pairs={{0,8},{2,10},{4,12},{6,14},{8,0},{10,2},{12,4},{14,6},{1,9},{3,11}... | collective-permute-start | bytes 737288 | tf_op jit(solution)/shard_map/ppermute | solution.py:440
  34.9 88.6 %copy-start = (s32[5]{0:T(128)}, s32[5]{0:T(128)S(1)}, u32[]{:S(2)}) copy-start(s32[5]{0:T(128)S(1)} %stack.113.refs_0_.sc) | copy-start | bytes 64
  34.9 11.5 %collective-permute-start.10 = (bf16[3,48,1280]{2,1,0:T(8,128)(2,1)S(1)}, bf16[3,48,1280]{2,1,0:T(8,128)(2,1)S(1)}, u32[]{:S(2)}, u32[]{:S(2)}) collective-permute-start(bf16[3,48,1280]{2,1,0:T(8,128)(2,1)S(1)} %pad_maximum_fusion.5.refs_6_.refs_17_), channel_id=1, source_target_pairs={{0,16},{16,0},{1,17},{17,1},{2,18},{18,2},{3,19},{19,3},{4,20},{20... | collective-permute-start | bytes 1105928 | tf_op jit(solution)/shard_map/ppermute | solution.py:411
  36.5 16.9 %collective-permute-start.11 = (bf16[3,48,1280]{2,1,0:T(8,128)(2,1)S(1)}, bf16[3,48,1280]{2,1,0:T(8,128)(2,1)S(1)}, u32[]{:S(2)}, u32[]{:S(2)}) collective-permute-start(bf16[3,48,1280]{2,1,0:T(8,128)(2,1)S(1)} %pad_maximum_fusion.5.refs_6_.refs_17_), channel_id=1, source_target_pairs={{0,2},{2,0},{4,6},{6,4},{8,10},{10,8},{12,14},{14,12},{1,3},{3,1},... | collective-permute-start | bytes 1105928 | tf_op jit(solution)/shard_map/ppermute | solution.py:414
  38.9 15.2 %collective-permute-start.12 = (bf16[3,48,1280]{2,1,0:T(8,128)(2,1)S(1)}, bf16[3,48,1280]{2,1,0:T(8,128)(2,1)S(1)}, u32[]{:S(2)}, u32[]{:S(2)}) collective-permute-start(bf16[3,48,1280]{2,1,0:T(8,128)(2,1)S(1)} %pad_maximum_fusion.5.refs_6_.refs_17_), channel_id=1, source_target_pairs={{0,18},{2,16},{4,22},{6,20},{8,26},{10,24},{12,30},{14,28},{16,2},... | collective-permute-start | bytes 1105928 | tf_op jit(solution)/shard_map/ppermute | solution.py:417
  38.9 15.7 %collective-permute-start.13 = (bf16[2,48,1280]{2,1,0:T(8,128)(2,1)S(1)}, bf16[2,48,1280]{2,1,0:T(8,128)(2,1)S(1)}, u32[]{:S(2)}, u32[]{:S(2)}) collective-permute-start(bf16[2,48,1280]{2,1,0:T(8,128)(2,1)S(1)} %pad_maximum_fusion.8.refs_2_.refs_3_.refs_13_), channel_id=1, source_target_pairs={{0,1},{1,0},{2,3},{3,2},{4,5},{5,4},{6,7},{7,6},{8,9},{9,8},{10,11... | collective-permute-start | bytes 737288 | tf_op jit(solution)/shard_map/ppermute | solution.py:408
  44.2 10.4 %collective-permute-start.14 = (bf16[2,48,1280]{2,1,0:T(8,128)(2,1)S(1)}, bf16[2,48,1280]{2,1,0:T(8,128)(2,1)S(1)}, u32[]{:S(2)}, u32[]{:S(2)}) collective-permute-start(bf16[2,48,1280]{2,1,0:T(8,128)(2,1)S(1)} %collective-permute-done.5.refs_3_.refs_4_.refs_14_), channel_id=1, source_target_pairs={{0,1},{1,0},{2,3},{3,2},{4,5},{5,4},{6,7},{7,6},{8,9},{9,8},{10,11... | collective-permute-start | bytes 737288 | tf_op jit(solution)/shard_map/ppermute | solution.py:408
  46.5 9.3 %collective-permute-start.15 = (bf16[2,48,1280]{2,1,0:T(8,128)(2,1)S(1)}, bf16[2,48,1280]{2,1,0:T(8,128)(2,1)S(1)}, u32[]{:S(2)}, u32[]{:S(2)}) collective-permute-start(bf16[2,48,1280]{2,1,0:T(8,128)(2,1)S(1)} %collective-permute-done.6.refs_4_.refs_5_.refs_15_), channel_id=1, source_target_pairs={{0,1},{1,0},{2,3},{3,2},{4,5},{5,4},{6,7},{7,6},{8,9},{9,8},{10,11... | collective-permute-start | bytes 737288 | tf_op jit(solution)/shard_map/ppermute | solution.py:408
  54.1 5.1 %collective-permute-start.17 = (bf16[3,48,1280]{2,1,0:T(8,128)(2,1)S(1)}, bf16[3,48,1280]{2,1,0:T(8,128)(2,1)S(1)}, u32[]{:S(2)}, u32[]{:S(2)}) collective-permute-start(bf16[3,48,1280]{2,1,0:T(8,128)(2,1)S(1)} %pad_maximum_fusion.5.refs_6_.refs_17_), channel_id=1, source_target_pairs={{0,1},{1,0},{2,3},{3,2},{4,5},{5,4},{6,7},{7,6},{8,9},{9,8},{10,11... | collective-permute-start | bytes 1105928 | tf_op jit(solution)/shard_map/ppermute | solution.py:408
  54.1 5.9 %collective-permute-start.18 = (bf16[3,48,1280]{2,1,0:T(8,128)(2,1)S(1)}, bf16[3,48,1280]{2,1,0:T(8,128)(2,1)S(1)}, u32[]{:S(2)}, u32[]{:S(2)}) collective-permute-start(bf16[3,48,1280]{2,1,0:T(8,128)(2,1)S(1)} %collective-permute-done.10.refs_7_.refs_18_), channel_id=1, source_target_pairs={{0,1},{1,0},{2,3},{3,2},{4,5},{5,4},{6,7},{7,6},{8,9},{9,8},{10,11... | collective-permute-start | bytes 1105928 | tf_op jit(solution)/shard_map/ppermute | solution.py:408
  54.7 6.6 %collective-permute-start.19 = (bf16[3,48,1280]{2,1,0:T(8,128)(2,1)S(1)}, bf16[3,48,1280]{2,1,0:T(8,128)(2,1)S(1)}, u32[]{:S(2)}, u32[]{:S(2)}) collective-permute-start(bf16[3,48,1280]{2,1,0:T(8,128)(2,1)S(1)} %collective-permute-done.11.refs_8_.refs_19_), channel_id=1, source_target_pairs={{0,1},{1,0},{2,3},{3,2},{4,5},{5,4},{6,7},{7,6},{8,9},{9,8},{10,11... | collective-permute-start | bytes 1105928 | tf_op jit(solution)/shard_map/ppermute | solution.py:408
  54.7 6.6 %collective-permute-start.20 = (bf16[3,48,1280]{2,1,0:T(8,128)(2,1)S(1)}, bf16[3,48,1280]{2,1,0:T(8,128)(2,1)S(1)}, u32[]{:S(2)}, u32[]{:S(2)}) collective-permute-start(bf16[3,48,1280]{2,1,0:T(8,128)(2,1)S(1)} %collective-permute-done.12.refs_9_.refs_20_), channel_id=1, source_target_pairs={{0,1},{1,0},{2,3},{3,2},{4,5},{5,4},{6,7},{7,6},{8,9},{9,8},{10,11... | collective-permute-start | bytes 1105928 | tf_op jit(solution)/shard_map/ppermute | solution.py:408
  55.7 2.0 %collective-permute-start.16 = (bf16[2,48,1280]{2,1,0:T(8,128)(2,1)S(1)}, bf16[2,48,1280]{2,1,0:T(8,128)(2,1)S(1)}, u32[]{:S(2)}, u32[]{:S(2)}) collective-permute-start(bf16[2,48,1280]{2,1,0:T(8,128)(2,1)S(1)} %collective-permute-done.7.refs_5_.refs_6_.refs_16_), channel_id=1, source_target_pairs={{0,1},{1,0},{2,3},{3,2},{4,5},{5,4},{6,7},{7,6},{8,9},{9,8},{10,11... | collective-permute-start | bytes 737288 | tf_op jit(solution)/shard_map/ppermute | solution.py:408
  57.8 12.1 %collective-permute-start.21 = (bf16[3,48,1280]{2,1,0:T(8,128)(2,1)S(1)}, bf16[3,48,1280]{2,1,0:T(8,128)(2,1)S(1)}, u32[]{:S(2)}, u32[]{:S(2)}) collective-permute-start(bf16[3,48,1280]{2,1,0:T(8,128)(2,1)S(1)} %pad_maximum_fusion.6.refs_7_), channel_id=1, source_target_pairs={{0,16},{16,0},{1,17},{17,1},{2,18},{18,2},{3,19},{19,3},{4,20},{20... | collective-permute-start | bytes 1105928 | tf_op jit(solution)/shard_map/ppermute | solution.py:411
  59.2 16.6 %collective-permute-start.22 = (bf16[3,48,1280]{2,1,0:T(8,128)(2,1)S(1)}, bf16[3,48,1280]{2,1,0:T(8,128)(2,1)S(1)}, u32[]{:S(2)}, u32[]{:S(2)}) collective-permute-start(bf16[3,48,1280]{2,1,0:T(8,128)(2,1)S(1)} %pad_maximum_fusion.6.refs_7_), channel_id=1, source_target_pairs={{0,2},{2,0},{4,6},{6,4},{8,10},{10,8},{12,14},{14,12},{1,3},{3,1},... | collective-permute-start | bytes 1105928 | tf_op jit(solution)/shard_map/ppermute | solution.py:414
  60.0 17.4 %collective-permute-start.23 = (bf16[3,48,1280]{2,1,0:T(8,128)(2,1)S(1)}, bf16[3,48,1280]{2,1,0:T(8,128)(2,1)S(1)}, u32[]{:S(2)}, u32[]{:S(2)}) collective-permute-start(bf16[3,48,1280]{2,1,0:T(8,128)(2,1)S(1)} %pad_maximum_fusion.6.refs_7_), channel_id=1, source_target_pairs={{0,18},{2,16},{4,22},{6,20},{8,26},{10,24},{12,30},{14,28},{16,2},... | collective-permute-start | bytes 1105928 | tf_op jit(solution)/shard_map/ppermute | solution.py:417
  77.5 1.7 collective-permute-start.24
  77.5 2.2 %collective-permute-start.25 = (bf16[3,48,1280]{2,1,0:T(8,128)(2,1)S(1)}, bf16[3,48,1280]{2,1,0:T(8,128)(2,1)S(1)}, u32[]{:S(2)}, u32[]{:S(2)}) collective-permute-start(bf16[3,48,1280]{2,1,0:T(8,128)(2,1)S(1)} %collective-permute-done.21.refs_8_), channel_id=1, source_target_pairs={{0,1},{1,0},{2,3},{3,2},{4,5},{5,4},{6,7},{7,6},{8,9},{9,8},{10,11... | collective-permute-start | bytes 1105928 | tf_op jit(solution)/shard_map/ppermute | solution.py:408
  78.0 2.2 %collective-permute-start.26 = (bf16[3,48,1280]{2,1,0:T(8,128)(2,1)S(1)}, bf16[3,48,1280]{2,1,0:T(8,128)(2,1)S(1)}, u32[]{:S(2)}, u32[]{:S(2)}) collective-permute-start(bf16[3,48,1280]{2,1,0:T(8,128)(2,1)S(1)} %collective-permute-done.22.refs_9_), channel_id=1, source_target_pairs={{0,1},{1,0},{2,3},{3,2},{4,5},{5,4},{6,7},{7,6},{8,9},{9,8},{10,11... | collective-permute-start | bytes 1105928 | tf_op jit(solution)/shard_map/ppermute | solution.py:408
  78.0 2.8 %collective-permute-start.27 = (bf16[3,48,1280]{2,1,0:T(8,128)(2,1)S(1)}, bf16[3,48,1280]{2,1,0:T(8,128)(2,1)S(1)}, u32[]{:S(2)}, u32[]{:S(2)}) collective-permute-start(bf16[3,48,1280]{2,1,0:T(8,128)(2,1)S(1)} %collective-permute-done.23.refs_10_), channel_id=1, source_target_pairs={{0,1},{1,0},{2,3},{3,2},{4,5},{5,4},{6,7},{7,6},{8,9},{9,8},{10,11... | collective-permute-start | bytes 1105928 | tf_op jit(solution)/shard_map/ppermute | solution.py:408
  99.5 4.2 %collective-permute-start.28 = (bf16[2,2,2,4,48,640]{5,4,3,2,1,0:T(8,128)(2,1)S(1)}, bf16[2,2,2,4,48,640]{5,4,3,2,1,0:T(8,128)(2,1)S(1)}, u32[]{:S(2)}, u32[]{:S(2)}) collective-permute-start(bf16[2,2,2,4,48,640]{5,4,3,2,1,0:T(8,128)(2,1)S(1)} %get-tuple-element.148), channel_id=1, source_target_pairs={{0,1},{1,0},{2,3},{3,2},{4,5},{5,4},{6,7},{7,6},{8,9},{9,8},{10,11... | collective-permute-start | bytes 5898248 | tf_op jit(solution)/shard_map/ppermute | solution.py:408
  100.0 26.5 %collective-permute-start.30 = (bf16[416,384]{1,0:T(8,128)(2,1)S(1)}, bf16[416,384]{1,0:T(8,128)(2,1)S(1)}, u32[]{:S(2)}, u32[]{:S(2)}) collective-permute-start(bf16[416,384]{1,0:T(8,128)(2,1)S(1)} %get-tuple-element.164), channel_id=1, source_target_pairs={{0,16},{16,0},{1,17},{17,1},{2,18},{18,2},{3,19},{19,3},{4,20},{20... | collective-permute-start | bytes 958472 | tf_op jit(solution)/shard_map/ppermute | solution.py:411
  104.2 16.6 %collective-permute-start.31 = (bf16[2,4,48,640]{3,2,1,0:T(8,128)(2,1)S(1)}, bf16[2,4,48,640]{3,2,1,0:T(8,128)(2,1)S(1)}, u32[]{:S(2)}, u32[]{:S(2)}) collective-permute-start(bf16[2,4,48,640]{3,2,1,0:T(8,128)(2,1)S(1)} %get-tuple-element.223), channel_id=1, source_target_pairs={{0,16},{16,0},{1,17},{17,1},{2,18},{18,2},{3,19},{19,3},{4,20},{20... | collective-permute-start | bytes 1474568 | tf_op jit(solution)/shard_map/ppermute | solution.py:411
  105.7 15.1 %collective-permute-start.32 = (bf16[2,4,48,640]{3,2,1,0:T(8,128)(2,1)S(1)}, bf16[2,4,48,640]{3,2,1,0:T(8,128)(2,1)S(1)}, u32[]{:S(2)}, u32[]{:S(2)}) collective-permute-start(bf16[2,4,48,640]{3,2,1,0:T(8,128)(2,1)S(1)} %get-tuple-element.222), channel_id=1, source_target_pairs={{0,2},{2,0},{4,6},{6,4},{8,10},{10,8},{12,14},{14,12},{1,3},{3,1},... | collective-permute-start | bytes 1474568 | tf_op jit(solution)/shard_map/ppermute | solution.py:414
  118.4 10.5 %collective-permute-start.29 = (bf16[416,384]{1,0:T(8,128)(2,1)S(1)}, bf16[416,384]{1,0:T(8,128)(2,1)S(1)}, u32[]{:S(2)}, u32[]{:S(2)}) collective-permute-start(bf16[416,384]{1,0:T(8,128)(2,1)S(1)} %get-tuple-element.163), channel_id=1, source_target_pairs={{0,16},{16,0},{1,17},{17,1},{2,18},{18,2},{3,19},{19,3},{4,20},{20... | collective-permute-start | bytes 958472 | tf_op jit(solution)/shard_map/ppermute | solution.py:411
  120.4 29.7 %copy-start.1 = (bf16[512,384]{1,0:T(8,128)(2,1)}, bf16[512,384]{1,0:T(8,128)(2,1)S(1)}, u32[]{:S(2)}) copy-start(bf16[512,384]{1,0:T(8,128)(2,1)S(1)} %convolution_convert_fusion.1) | copy-start | bytes 1179652
  120.8 4.9 %collective-permute-start.35 = (bf16[2,2,2,4,48,640]{5,4,3,2,1,0:T(8,128)(2,1)S(1)}, bf16[2,2,2,4,48,640]{5,4,3,2,1,0:T(8,128)(2,1)S(1)}, u32[]{:S(2)}, u32[]{:S(2)}) collective-permute-start(bf16[2,2,2,4,48,640]{5,4,3,2,1,0:T(8,128)(2,1)S(1)} %get-tuple-element.181), channel_id=1, source_target_pairs={{0,1},{1,0},{2,3},{3,2},{4,5},{5,4},{6,7},{7,6},{8,9},{9,8},{10,11... | collective-permute-start | bytes 5898248 | tf_op jit(solution)/shard_map/ppermute | solution.py:408
  121.1 13.1 %collective-permute-start.34 = (bf16[4,48,640]{2,1,0:T(8,128)(2,1)S(1)}, bf16[4,48,640]{2,1,0:T(8,128)(2,1)S(1)}, u32[]{:S(2)}, u32[]{:S(2)}) collective-permute-start(bf16[4,48,640]{2,1,0:T(8,128)(2,1)S(1)} %fusion.18), channel_id=1, source_target_pairs={{0,16},{16,0},{1,17},{17,1},{2,18},{18,2},{3,19},{19,3},{4,20},{20... | collective-permute-start | bytes 737288 | tf_op jit(solution)/shard_map/ppermute | solution.py:411
  121.8 12.3 %collective-permute-start.33 = (bf16[4,48,640]{2,1,0:T(8,128)(2,1)S(1)}, bf16[4,48,640]{2,1,0:T(8,128)(2,1)S(1)}, u32[]{:S(2)}, u32[]{:S(2)}) collective-permute-start(bf16[4,48,640]{2,1,0:T(8,128)(2,1)S(1)} %fusion.17), channel_id=1, source_target_pairs={{0,2},{2,0},{4,6},{6,4},{8,10},{10,8},{12,14},{14,12},{1,3},{3,1},... | collective-permute-start | bytes 737288 | tf_op jit(solution)/shard_map/ppermute | solution.py:414
  126.2 17.0 %collective-permute-start.37 = (bf16[2,4,48,640]{3,2,1,0:T(8,128)(2,1)S(1)}, bf16[2,4,48,640]{3,2,1,0:T(8,128)(2,1)S(1)}, u32[]{:S(2)}, u32[]{:S(2)}) collective-permute-start(bf16[2,4,48,640]{3,2,1,0:T(8,128)(2,1)S(1)} %get-tuple-element.219), channel_id=1, source_target_pairs={{0,16},{16,0},{1,17},{17,1},{2,18},{18,2},{3,19},{19,3},{4,20},{20... | collective-permute-start | bytes 1474568 | tf_op jit(solution)/shard_map/ppermute | solution.py:411
  126.5 16.8 %collective-permute-start.38 = (bf16[2,4,48,640]{3,2,1,0:T(8,128)(2,1)S(1)}, bf16[2,4,48,640]{3,2,1,0:T(8,128)(2,1)S(1)}, u32[]{:S(2)}, u32[]{:S(2)}) collective-permute-start(bf16[2,4,48,640]{3,2,1,0:T(8,128)(2,1)S(1)} %get-tuple-element.218), channel_id=1, source_target_pairs={{0,2},{2,0},{4,6},{6,4},{8,10},{10,8},{12,14},{14,12},{1,3},{3,1},... | collective-permute-start | bytes 1474568 | tf_op jit(solution)/shard_map/ppermute | solution.py:414
  135.9 14.3 %copy-start.2 = (bf16[512,384]{1,0:T(8,128)(2,1)}, bf16[512,384]{1,0:T(8,128)(2,1)S(1)}, u32[]{:S(2)}) copy-start(bf16[512,384]{1,0:T(8,128)(2,1)S(1)} %convolution_convert_fusion) | copy-start | bytes 1179652
  136.1 6.3 %collective-permute-start.40 = (bf16[2,2,48,640]{3,2,0,1:T(8,128)(2,1)S(1)}, bf16[2,2,48,640]{3,2,0,1:T(8,128)(2,1)S(1)}, u32[]{:S(2)}, u32[]{:S(2)}) collective-permute-start(bf16[2,2,48,640]{3,2,0,1:T(8,128)(2,1)S(1)} %slice.238), channel_id=1, source_target_pairs={{0,4},{2,6},{4,0},{6,2},{8,12},{10,14},{12,8},{14,10},{1,5},{3,7},... | collective-permute-start | bytes 737288 | tf_op jit(solution)/shard_map/ppermute | solution.py:440
  136.8 13.3 %collective-permute-start.36 = (bf16[4,208,384]{2,1,0:T(8,128)(2,1)S(1)}, bf16[4,208,384]{2,1,0:T(8,128)(2,1)S(1)}, u32[]{:S(2)}, u32[]{:S(2)}) collective-permute-start(bf16[4,208,384]{2,1,0:T(8,128)(2,1)S(1)} %pad_maximum_fusion.4), channel_id=1, source_target_pairs={{1,3},{3,5},{5,7},{7,9},{9,11},{11,13},{13,15},{17,19},{19,21},{21... | collective-permute-start | bytes 1916936 | tf_op jit(solution)/shard_map/ppermute | solution.py:452
  143.4 10.5 %collective-permute-start.43 = (bf16[4,48,640]{2,1,0:T(8,128)(2,1)S(1)}, bf16[4,48,640]{2,1,0:T(8,128)(2,1)S(1)}, u32[]{:S(2)}, u32[]{:S(2)}) collective-permute-start(bf16[4,48,640]{2,1,0:T(8,128)(2,1)S(1)} %fusion.20), channel_id=1, source_target_pairs={{0,16},{16,0},{1,17},{17,1},{2,18},{18,2},{3,19},{19,3},{4,20},{20... | collective-permute-start | bytes 737288 | tf_op jit(solution)/shard_map/ppermute | solution.py:411
  145.1 8.8 %collective-permute-start.42 = (bf16[4,48,640]{2,1,0:T(8,128)(2,1)S(1)}, bf16[4,48,640]{2,1,0:T(8,128)(2,1)S(1)}, u32[]{:S(2)}, u32[]{:S(2)}) collective-permute-start(bf16[4,48,640]{2,1,0:T(8,128)(2,1)S(1)} %fusion.19), channel_id=1, source_target_pairs={{0,2},{2,0},{4,6},{6,4},{8,10},{10,8},{12,14},{14,12},{1,3},{3,1},... | collective-permute-start | bytes 737288 | tf_op jit(solution)/shard_map/ppermute | solution.py:414
  145.8 8.1 %collective-permute-start.41 = (bf16[2,48,640]{2,1,0:T(8,128)(2,1)S(1)}, bf16[2,48,640]{2,1,0:T(8,128)(2,1)S(1)}, u32[]{:S(2)}, u32[]{:S(2)}) collective-permute-start(bf16[2,48,640]{2,1,0:T(8,128)(2,1)S(1)} %fusion.31), channel_id=1, source_target_pairs={{0,8},{2,10},{4,12},{6,14},{8,0},{10,2},{12,4},{14,6},{1,9},{3,11}... | collective-permute-start | bytes 368648 | tf_op jit(solution)/shard_map/ppermute | solution.py:440
  150.3 0.9 slice-start
  150.3 1.0 slice-start.1
  151.6 15.5 %collective-permute-start.39 = (bf16[4,512,384]{2,1,0:T(8,128)(2,1)S(1)}, bf16[4,512,384]{2,1,0:T(8,128)(2,1)S(1)}, u32[]{:S(2)}, u32[]{:S(2)}) collective-permute-start(bf16[4,512,384]{2,1,0:T(8,128)(2,1)S(1)} %pad_maximum_fusion), channel_id=1, source_target_pairs={{0,1},{1,0},{2,3},{3,2},{4,5},{5,4},{6,7},{7,6},{8,9},{9,8},{10,11... | collective-permute-start | bytes 4718600 | tf_op jit(solution)/shard_map/ppermute | solution.py:408
  154.1 5.2 %collective-permute-start.44 = (bf16[2,48,640]{2,1,0:T(8,128)(2,1)S(1)}, bf16[2,48,640]{2,1,0:T(8,128)(2,1)S(1)}, u32[]{:S(2)}, u32[]{:S(2)}) collective-permute-start(bf16[2,48,640]{2,1,0:T(8,128)(2,1)S(1)} %get-tuple-element.230), channel_id=1, source_target_pairs={{0,4},{2,6},{4,0},{6,2},{8,12},{10,14},{12,8},{14,10},{1,5},{3,7},... | collective-permute-start | bytes 368648 | tf_op jit(solution)/shard_map/ppermute | solution.py:440
  155.7 11.4 %collective-permute-start.45 = (bf16[2,48,640]{2,1,0:T(8,128)(2,1)S(1)}, bf16[2,48,640]{2,1,0:T(8,128)(2,1)S(1)}, u32[]{:S(2)}, u32[]{:S(2)}) collective-permute-start(bf16[2,48,640]{2,1,0:T(8,128)(2,1)S(1)} %get-tuple-element.232), channel_id=1, source_target_pairs={{0,8},{2,10},{4,12},{6,14},{8,0},{10,2},{12,4},{14,6},{1,9},{3,11}... | collective-permute-start | bytes 368648 | tf_op jit(solution)/shard_map/ppermute | solution.py:440
  156.5 10.5 %collective-permute-start.46 = (bf16[2,48,640]{2,1,0:T(8,128)(2,1)S(1)}, bf16[2,48,640]{2,1,0:T(8,128)(2,1)S(1)}, u32[]{:S(2)}, u32[]{:S(2)}) collective-permute-start(bf16[2,48,640]{2,1,0:T(8,128)(2,1)S(1)} %get-tuple-element.231), channel_id=1, source_target_pairs={{0,12},{2,14},{4,8},{6,10},{8,4},{10,6},{12,0},{14,2},{1,13},{3,15... | collective-permute-start | bytes 368648 | tf_op jit(solution)/shard_map/ppermute | solution.py:440
  167.2 4.9 %collective-permute-start.47 = (bf16[48,1280]{1,0:T(8,128)(2,1)S(1)}, bf16[48,1280]{1,0:T(8,128)(2,1)S(1)}, u32[]{:S(2)}, u32[]{:S(2)}) collective-permute-start(bf16[48,1280]{1,0:T(8,128)(2,1)S(1)} %select_convert_fusion), channel_id=1, source_target_pairs={{0,16},{16,0},{1,17},{17,1},{2,18},{18,2},{3,19},{19,3},{4,20},{20... | collective-permute-start | bytes 368648 | tf_op jit(solution)/shard_map/ppermute | solution.py:411
  172.1 0.6 copy-start.4
